TPU v7x, 32 devices: a whole 2x2x4 slice. The times are simulated.
32 devices in a mesh: rows: 8 (over z, x), sub: 4 (over y, core).
Axes of the slice: x: 2, y: 2, z: 4, core: 2. Of those that a mesh axis runs over, the one named last changes fastest.
Arguments:
- queries: float32 [16384, 256], P(('rows', 'sub')), may hold values from -6 to 6
- row_scale: float32 [16384], P(('rows', 'sub')), may hold values from 0.6 to 1.6
- leaf_basis: float32 [16384, 128], P(('rows', 'sub')), may hold values from -6 to 6
- leaf_cores: float32 [8, 128, 128], P('rows'), as said below
- level_basis: float32 [3, 16384, 128], P(None, ('rows', 'sub')), may hold values from -6 to 6
- level_cores: float32 [14, 128, 128], replicated, as said below
Outputs:
- solution: float32 [16384, 256], P(('rows', 'sub'))
Inputs may be any that keep to these rules, and one draw needn't show every extreme that they name: `leaf_cores`: each core is divided by the rows of its block: every entry lies within 3 / (512 * 4) of zero. `level_cores`: each core is divided by the rows of its node: every entry of a level-l core lies within 3 * 2 ** l / 16384 of zero.
All inputs are finite; a program needn't handle non-finite values.
Results may differ from a plain program's by a relative error of at most 0.0001.
Values sent between devices are 32-bit elements; how exact they have to be, the bound alone decides.
No kernel may reach another device: no remote copies, remote signals or barrier semaphores. Data moves between devices by JAX's collectives and lax.ppermute only.
A program may use at most 64 MiB of HBM per device.

v0:
```python
import jax
import jax.numpy as jnp
from jax import lax
from jax.sharding import PartitionSpec as P

LEVELS = 3


precise = lax.Precision.HIGHEST


def partner(array, axis, stride):
    return lax.ppermute(array, axis, [(i, i ^ 1 << stride) for i in range(lax.axis_size(axis))])


def product(left, right):
    return jnp.dot(left, right, precision=precise, preferred_element_type=jnp.float32)


def project(vectors, values):
    return lax.dot_general(
        vectors,
        values,
        (((0,), (0,)), ((), ())),
        precision=precise,
        preferred_element_type=jnp.float32,
    )


def node_total(partial_value, height):
    group_width = lax.axis_size("rows") // 2**height
    summed = lax.psum(partial_value, "sub")
    for bit_index in range(group_width.bit_length() - 1):
        summed = summed + partner(summed, "rows", bit_index)
    return summed


def leaf_apply(values, vectors, core_here, transposed):
    moments = lax.psum(project(vectors, values), "sub")
    inner_core = project(core_here, moments) if transposed else product(core_here, moments)
    return values - product(vectors, inner_core)


def node_core(level_cores, height, node_index):
    return lax.dynamic_index_in_dim(level_cores, 2**height - 2 + node_index, 0, keepdims=False)


def node_of(height):
    return lax.axis_index("rows") // (lax.axis_size("rows") // 2**height)


def level_apply(values, level_basis, level_cores, height, transposed):
    vectors = level_basis[height - 1]
    node_index = node_of(height)
    core_here = node_core(level_cores, height, node_index)
    moments = node_total(project(vectors, values), height)
    inner_core = project(core_here, moments) if transposed else product(core_here, moments)
    return values - product(vectors, inner_core)


def shards(queries, row_scale, leaf_basis, leaf_cores, level_basis, level_cores):
    row_weights = row_scale[:, None]
    leaf_core = leaf_cores[0]
    col_count = queries.shape[1]
    current = row_weights * leaf_apply(queries, leaf_basis, leaf_core, False)
    for height in range(LEVELS, 1, -1):
        current = level_apply(current, level_basis, level_cores, height, False)
    vectors = level_basis[0]
    node_index = node_of(1)
    core_here = node_core(level_cores, 1, node_index)
    joined = jnp.concatenate([project(vectors, current), project(vectors, vectors)], axis=1)
    joined = node_total(joined, 1)
    moments = joined[:, :col_count]
    gram_matrix = joined[:, col_count:]
    inner_core = core_here + core_here.T - project(core_here, product(gram_matrix, core_here))
    current = current - product(vectors, product(inner_core, moments))
    for height in range(2, LEVELS + 1):
        current = level_apply(current, level_basis, level_cores, height, True)
    current = row_weights * current
    return leaf_apply(current, leaf_basis, leaf_core, True)


def solution(mesh):
    in_specs = (
        P(("rows", "sub"), None),
        P(("rows", "sub")),
        P(("rows", "sub"), None),
        P("rows", None, None),
        P(None, ("rows", "sub"), None),
        P(),
    )
    out_specs = P(("rows", "sub"), None)
    return jax.shard_map(shards, mesh=mesh, in_specs=in_specs, out_specs=out_specs, check_vma=False)
```

profile of v0, /device:TPU:0, one launch (start us, length us, event | category | flops | bytes accessed | tf_op | source)
XLA Modules:
  0.0 287.0 jit_solution(7679352918736281961)
XLA Ops:
  6.5 0.0 copy-start
  6.5 2.5 fusion.58
  9.0 0.0 all-reduce.8.cloned.1.call-update
  9.1 0.0 copy-start.4
  9.1 0.0 all-reduce.10.cloned.1.call-start
  9.1 0.2 copy.12
  9.3 0.0 copy-start.2
  9.3 0.0 copy-start.6
  9.4 34.8 %all-reduce.8.cloned.1.call-done = f32[128,256]{1,0:T(8,128)} async-done(((f32[128,256]{1,0:T(8,128)}), f32[128,256]{1,0:T(8,128)}) %all-reduce.8.cloned.1.call-update) | async-done | bytes 131088 | tf_op jit(solution)/shard_map/psum | solution.py:39
  44.2 0.0 copy-done.4
  44.2 1.3 fusion.48
  45.5 0.0 copy-start.1
  45.5 0.6 fusion.1
  46.1 0.5 copy-done.1
  46.6 1.2 convolution_bitcast_fusion.12
  47.9 0.0 all-reduce.10.cloned.1.call-update
  47.9 0.0 all-reduce.12.cloned.1.call-start
  48.0 31.9 %all-reduce.10.cloned.1.call-done = f32[128,256]{0,1:T(8,128)} async-done(((f32[128,256]{0,1:T(8,128)}), f32[128,256]{0,1:T(8,128)}) %all-reduce.10.cloned.1.call-update) | async-done | bytes 131088 | tf_op jit(solution)/shard_map/psum | solution.py:32
  79.9 1.2 fusion.44
  81.0 0.6 fusion.2
  81.7 1.2 convolution_bitcast_fusion.11
  82.9 0.0 all-reduce.12.cloned.1.call-update
  82.9 0.0 all-reduce.14.cloned.1.call-start
  83.0 31.8 %all-reduce.12.cloned.1.call-done = f32[128,256]{0,1:T(8,128)} async-done(((f32[128,256]{0,1:T(8,128)}), f32[128,256]{0,1:T(8,128)}) %all-reduce.12.cloned.1.call-update) | async-done | bytes 131088 | tf_op jit(solution)/shard_map/psum | solution.py:32
  114.9 1.5 collective-permute-start
  116.3 0.6 fusion.10
  116.9 3.1 %collective-permute-done = f32[128,256]{0,1:T(8,128)S(1)} collective-permute-done((f32[128,256]{0,1:T(8,128)}, f32[128,256]{0,1:T(8,128)S(1)}, u32[]{:S(2)}, u32[]{:S(2)}) %collective-permute-start) | collective-permute-done | bytes 131104 | tf_op jit(solution)/shard_map/ppermute | solution.py:13
  120.0 0.3 fusion.36
  120.3 0.6 fusion.3
  121.0 0.6 convolution_bitcast_fusion.10
  121.5 0.7 pad_maximum_fusion
  122.2 0.0 all-reduce.14.cloned.1.call-update
  122.3 0.0 all-reduce.16.cloned.1.call-start
  122.3 32.1 %all-reduce.14.cloned.1.call-done = f32[128,384]{0,1:T(8,128)} async-done(((f32[128,384]{0,1:T(8,128)}), f32[128,384]{0,1:T(8,128)}) %all-reduce.14.cloned.1.call-update) | async-done | bytes 196624 | tf_op jit(solution)/shard_map/psum | solution.py:32
  154.4 1.5 collective-permute-start.1
  155.9 4.4 %collective-permute-done.1 = f32[128,384]{0,1:T(8,128)S(1)} collective-permute-done((f32[128,384]{0,1:T(8,128)}, f32[128,384]{0,1:T(8,128)S(1)}, u32[]{:S(2)}, u32[]{:S(2)}) %collective-permute-start.1) | collective-permute-done | bytes 196640 | tf_op jit(solution)/shard_map/ppermute | solution.py:13
  160.3 1.0 add.63
  161.3 1.5 collective-permute-start.2
  162.8 0.1 copy.13
  162.9 4.1 %collective-permute-done.2 = f32[128,384]{0,1:T(8,128)S(1)} collective-permute-done((f32[128,384]{0,1:T(8,128)S(1)}, f32[128,384]{0,1:T(8,128)S(1)}, u32[]{:S(2)}, u32[]{:S(2)}) %collective-permute-start.2) | collective-permute-done | bytes 196640 | tf_op jit(solution)/shard_map/ppermute | solution.py:13
  167.0 0.3 fusion.38
  167.3 0.3 convolution_subtract_fusion
  167.6 0.3 fusion.32
  167.9 0.6 fusion.4
  168.5 1.2 convolution_bitcast_fusion.9
  169.8 0.0 all-reduce.16.cloned.1.call-update
  169.8 0.0 all-reduce.18.cloned.1.call-start
  169.9 32.3 %all-reduce.16.cloned.1.call-done = f32[128,256]{0,1:T(8,128)} async-done(((f32[128,256]{0,1:T(8,128)}), f32[128,256]{0,1:T(8,128)}) %all-reduce.16.cloned.1.call-update) | async-done | bytes 131088 | tf_op jit(solution)/shard_map/psum | solution.py:32
  202.1 1.5 collective-permute-start.3
  203.6 3.7 %collective-permute-done.3 = f32[128,256]{0,1:T(8,128)S(1)} collective-permute-done((f32[128,256]{0,1:T(8,128)}, f32[128,256]{0,1:T(8,128)S(1)}, u32[]{:S(2)}, u32[]{:S(2)}) %collective-permute-start.3) | collective-permute-done | bytes 131104 | tf_op jit(solution)/shard_map/ppermute | solution.py:13
  207.3 1.2 fusion.34
  208.5 0.6 fusion.5
  209.2 1.2 convolution_bitcast_fusion.8
  210.4 0.0 all-reduce.18.cloned.1.call-update
  210.4 0.2 all-reduce.20.cloned.1.call-start
  210.7 31.7 %all-reduce.18.cloned.1.call-done = f32[128,256]{0,1:T(8,128)} async-done(((f32[128,256]{0,1:T(8,128)}), f32[128,256]{0,1:T(8,128)}) %all-reduce.18.cloned.1.call-update) | async-done | bytes 131088 | tf_op jit(solution)/shard_map/psum | solution.py:32
  242.4 1.2 fusion.42
  243.6 0.6 fusion.7
  244.2 1.2 convolution_bitcast_fusion.7
  245.5 0.0 all-reduce.20.cloned.1.call-update
  245.5 31.9 %all-reduce.20.cloned.1.call-done = f32[128,256]{0,1:T(8,128)} async-done(((f32[128,256]{0,1:T(8,128)}), f32[128,256]{0,1:T(8,128)}) %all-reduce.20.cloned.1.call-update) | async-done | bytes 131088 | tf_op jit(solution)/shard_map/psum | solution.py:39
  277.4 1.2 fusion.46
  278.6 0.6 fusion.8
  279.2 1.0 copy.14
  (10 shorter events, 0.0 us)
Async XLA Ops:
  6.5 73.3 %copy-start = (f32[14,128,128]{2,1,0:T(8,128)S(1)}, f32[14,128,128]{2,1,0:T(8,128)}, u32[]{:S(2)}) copy-start(f32[14,128,128]{2,1,0:T(8,128)} %param.11) | copy-start | bytes 2752516
  6.5 2.6 copy-start.3
  6.5 37.7 %all-reduce.8.cloned.1.call-start = ((), (), s32[]{:S(2)}) async-start(), calls=%async_computation | async-start | bytes 262144 | tf_op jit(solution)/shard_map/psum | solution.py:39
  9.1 35.1 %copy-start.4 = (f32[1,128,128]{2,1,0:T(8,128)S(1)}, f32[1,128,128]{2,1,0:T(8,128)}, u32[]{:S(2)}) copy-start(f32[1,128,128]{2,1,0:T(8,128)} %param.9) | copy-start | bytes 196612
  9.1 70.8 %all-reduce.10.cloned.1.call-start = ((), (), s32[]{:S(2)}) async-start(), calls=%async_computation.1 | async-start | bytes 262144 | tf_op jit(solution)/shard_map/psum | solution.py:32
  9.3 36.2 %copy-start.2 = (f32[512,128]{1,0:T(8,128)S(1)}, f32[512,128]{1,0:T(8,128)}, u32[]{:S(2)}) copy-start(f32[512,128]{1,0:T(8,128)} %param.8) | copy-start | bytes 786436
  9.3 36.2 %copy-start.6 = (f32[512]{0:T(512)S(1)}, f32[512]{0:T(512)}, u32[]{:S(2)}) copy-start(f32[512]{0:T(512)} %param.7) | copy-start | bytes 6148
  45.5 1.1 copy-start.1
  47.9 66.9 %all-reduce.12.cloned.1.call-start = ((), (), s32[]{:S(2)}) async-start(), calls=%async_computation.2 | async-start | bytes 262144 | tf_op jit(solution)/shard_map/psum | solution.py:32
  82.9 71.5 %all-reduce.14.cloned.1.call-start = ((), (), s32[]{:S(2)}) async-start(), calls=%async_computation.3 | async-start | bytes 393216 | tf_op jit(solution)/shard_map/psum | solution.py:32
  114.8 5.2 %copy-start.5 = (f32[128,256]{0,1:T(8,128)S(1)}, f32[128,256]{0,1:T(8,128)}, u32[]{:S(2)}) copy-start(f32[128,256]{0,1:T(8,128)} %all-reduce.12.cloned.1.call-done) | copy-start | bytes 393220
  114.9 5.2 %collective-permute-start = (f32[128,256]{0,1:T(8,128)}, f32[128,256]{0,1:T(8,128)S(1)}, u32[]{:S(2)}, u32[]{:S(2)}) collective-permute-start(f32[128,256]{0,1:T(8,128)} %all-reduce.12.cloned.1.call-done), channel_id=1, source_target_pairs={{0,4},{4,0},{8,12},{12,8},{16,20},{20,16},{24,28},{28,24},{1,5},{5... | collective-permute-start | bytes 393224 | tf_op jit(solution)/shard_map/ppermute | solution.py:13
  122.3 79.9 %all-reduce.16.cloned.1.call-start = ((), (), s32[]{:S(2)}) async-start(), calls=%async_computation.4 | async-start | bytes 262144 | tf_op jit(solution)/shard_map/psum | solution.py:32
  154.4 5.9 %collective-permute-start.1 = (f32[128,384]{0,1:T(8,128)}, f32[128,384]{0,1:T(8,128)S(1)}, u32[]{:S(2)}, u32[]{:S(2)}) collective-permute-start(f32[128,384]{0,1:T(8,128)} %all-reduce.14.cloned.1.call-done), channel_id=1, source_target_pairs={{0,4},{4,0},{8,12},{12,8},{16,20},{20,16},{24,28},{28,24},{1,5},{5... | collective-permute-start | bytes 589832 | tf_op jit(solution)/shard_map/ppermute | solution.py:13
  161.3 5.7 %collective-permute-start.2 = (f32[128,384]{0,1:T(8,128)S(1)}, f32[128,384]{0,1:T(8,128)S(1)}, u32[]{:S(2)}, u32[]{:S(2)}) collective-permute-start(f32[128,384]{0,1:T(8,128)S(1)} %add.63), channel_id=1, source_target_pairs={{0,8},{4,12},{8,0},{12,4},{16,24},{20,28},{24,16},{28,20},{1,9},{5... | collective-permute-start | bytes 589832 | tf_op jit(solution)/shard_map/ppermute | solution.py:13
  169.8 72.6 %all-reduce.18.cloned.1.call-start = ((), (), s32[]{:S(2)}) async-start(), calls=%async_computation.5 | async-start | bytes 262144 | tf_op jit(solution)/shard_map/psum | solution.py:32
  202.1 5.2 %collective-permute-start.3 = (f32[128,256]{0,1:T(8,128)}, f32[128,256]{0,1:T(8,128)S(1)}, u32[]{:S(2)}, u32[]{:S(2)}) collective-permute-start(f32[128,256]{0,1:T(8,128)} %all-reduce.16.cloned.1.call-done), channel_id=1, source_target_pairs={{0,4},{4,0},{8,12},{12,8},{16,20},{20,16},{24,28},{28,24},{1,5},{5... | collective-permute-start | bytes 393224 | tf_op jit(solution)/shard_map/ppermute | solution.py:13
  210.4 67.0 %all-reduce.20.cloned.1.call-start = ((), (), s32[]{:S(2)}) async-start(), calls=%async_computation.6 | async-start | bytes 262144 | tf_op jit(solution)/shard_map/psum | solution.py:39
Sparse Core Ops, SparseCore 0:
  9.6 34.4 all-reduce.7
  48.0 31.7 all-reduce.9
  83.1 31.7 all-reduce.11
  122.4 32.0 all-reduce.13
  169.9 32.1 all-reduce.15
  210.6 31.7 all-reduce.17
  245.6 31.7 all-reduce.19
where the time goes:
time: 287 us
  waiting for transfers between devices  242 us (84%)
  matrix products  21.4 us (7%)
  between operations  13.7 us (5%)
  starting transfers between devices  6.39 us (2%)
    psum x5, waiting for transfers between devices, node_total(): summed = lax.psum(partial_value, 'sub')  160 us
    psum x2, waiting for transfers between devices, leaf_apply(): moments = lax.psum(project(vectors, values), 'sub')  66.8 us
    ppermute x4, waiting for transfers between devices, partner(): lax.ppermute(array, axis, [(i, i ^ 1 << stride) for i in range(lax.axis_s...  15.3 us
    dot_general x12, matrix products, project(): lax.dot_general(vectors, values, (((0,), (0,)), ((), ())), precision=prec...  13.8 us
    dot_general x12, matrix products, product(): jnp.dot(left, right, precision=precise, preferred_element_type=jnp.float32)  7.61 us
    ppermute x4, starting transfers between devices, partner(): lax.ppermute(array, axis, [(i, i ^ 1 << stride) for i in range(lax.axis_s...  5.95 us
  transfers between devices with their start and end apart: 11, of which 11 were waited for; matrix products, arithmetic and copies ran while one was open for 0% of the time, Pallas kernels for 0%

commit v1 on v0

v1 whole, which is shorter than its diff:
```python
import functools

import jax
import jax.numpy as jnp
from jax import lax
from jax.experimental import pallas as pl
from jax.experimental.pallas import tpu as pltpu
from jax.sharding import PartitionSpec as P


FLOAT = jnp.float32


def halves(value):
    high = value.astype(jnp.bfloat16)
    return high, (value - high.astype(FLOAT)).astype(jnp.bfloat16)


def dot(left, right, left_dim=1):
    mult = functools.partial(
        lax.dot_general,
        dimension_numbers=(((left_dim,), (0,)), ((), ())),
        preferred_element_type=FLOAT,
    )
    left_high, left_low = halves(left)
    right_high, right_low = halves(right)
    return mult(left_high, right_high) + (mult(left_high, right_low) + mult(left_low, right_high))


def column_scale(scale_ref, width):
    lanes = scale_ref.shape[1]
    blocks = [
        jnp.broadcast_to(scale_ref[i : i + 1, :], (lanes, lanes)).T for i in range(scale_ref.shape[0])
    ]
    block = jnp.concatenate(blocks, axis=0)
    return block if width == lanes else jnp.concatenate([block] * (width // lanes), axis=1)


def core_side():
    return lax.rem(lax.axis_index("sub"), 2)


def store_halves(value, axis, keep_ref, send_ref, offset):
    size = value.shape[axis] // 2
    first = lax.slice_in_dim(value, 0, size, axis=axis)
    second = lax.slice_in_dim(value, size, 2 * size, axis=axis)
    where = pl.ds(offset, first.shape[0])
    side = core_side()

    @pl.when(side == 0)
    def _():
        keep_ref[where, :] = first
        send_ref[where, :] = second

    @pl.when(side == 1)
    def _():
        keep_ref[where, :] = second
        send_ref[where, :] = first


def join(own, other, axis):
    first = core_side() == 0
    return jnp.concatenate([jnp.where(first, own, other), jnp.where(first, other, own)], axis=axis)


def call(body, out_shapes, *operands, name, flops):
    space = pl.BlockSpec(memory_space=pltpu.VMEM)
    size = sum(4 * a.size for a in operands)
    outs = [jax.ShapeDtypeStruct(shape, FLOAT) for shape in out_shapes]
    return pl.pallas_call(
        body,
        out_shape=outs,
        in_specs=[space] * len(operands),
        out_specs=[space] * len(outs),
        name=name,
        cost_estimate=pl.CostEstimate(flops=flops, bytes_accessed=size, transcendentals=0),
    )(*operands)


def swap(array, axis, bit):
    return lax.ppermute(array, axis, [(i, i ^ 1 << bit) for i in range(lax.axis_size(axis))])


def partial_sums(array, axis, bits):
    bits = list(bits)
    if not bits:
        return [array]
    for bit in bits[:-1]:
        array = array + swap(array, axis, bit)
    return [array, swap(array, axis, bits[-1])]


def add_all(parts):
    return functools.reduce(lambda a, b: a + b, parts)


def shards(queries, row_scale, leaf_basis, leaf_cores, level_basis, level_cores):
    levels = level_basis.shape[0]
    count = levels + 1
    top = levels
    rows_here, rank = leaf_basis.shape
    columns = queries.shape[1]
    wide = columns // 2
    groups, sub = lax.axis_size("rows"), lax.axis_size("sub")
    heights = [None] + [levels + 1 - e for e in range(1, count)]
    widths = [1] + [groups // 2 ** heights[e] for e in range(1, count)]
    head = sum(w == 1 for w in widths)
    bits = [range(0)] + [
        range(widths[e - 1].bit_length() - 1, widths[e].bit_length() - 1) for e in range(1, count)
    ]
    blocks = [list(range(e + 1 if e < head else e, count)) for e in range(count)]
    leaf_bits = range(1, sub.bit_length() - 1)
    small = 2 * 3 * rank**3

    scale = row_scale.reshape(-1, rank)
    index = lax.axis_index("rows")
    cores = [leaf_cores[0]] + [
        lax.dynamic_index_in_dim(level_cores, 2 ** heights[e] - 2 + index // widths[e], 0, keepdims=False)
        for e in range(1, count)
    ]

    half_rows = [len(b) * rank // 2 for b in blocks]
    starts = [sum(half_rows[:e]) for e in range(count + 1)]

    def gram_body(scale_ref, leaf_ref, level_ref, keep_ref, send_ref):
        vectors = [column_scale(scale_ref, rank) * leaf_ref[...]]
        vectors += [level_ref[levels - e] for e in range(1, count)]
        for e in range(count):
            left = jnp.concatenate([vectors[f] for f in blocks[e]], axis=1)
            store_halves(dot(left, vectors[e], 0), 0, keep_ref, send_ref, starts[e])

    gram_shape = (starts[count], rank)
    gram_keep, gram_send = call(
        gram_body,
        [gram_shape] * 2,
        scale,
        leaf_basis,
        level_basis,
        name="gram",
        flops=small * sum(map(len, blocks)) * rows_here // rank,
    )
    gram_chip = gram_keep + swap(gram_send, "sub", 0)
    gram_leaf = add_all(partial_sums(gram_chip, "sub", leaf_bits))

    def moment_body(scale_ref, queries_ref, leaf_ref, level_ref, keep_ref, send_ref):
        values = queries_ref[...]
        store_halves(dot(leaf_ref[...], values, 0), 1, keep_ref, send_ref, 0)
        values = column_scale(scale_ref, columns) * values
        for e in range(1, count):
            store_halves(dot(level_ref[levels - e], values, 0), 1, keep_ref, send_ref, e * rank)

    moment_keep, moment_send = call(
        moment_body,
        [(count * rank, wide)] * 2,
        scale,
        queries,
        leaf_basis,
        level_basis,
        name="moment",
        flops=small * count * 2 * rows_here // rank,
    )
    moment_chip = moment_keep + swap(moment_send, "sub", 0)
    moment_parts = partial_sums(moment_chip, "sub", leaf_bits)

    def late_body(scale_ref, queries_ref, leaf_ref, level_ref, keep_ref, send_ref):
        spread = column_scale(scale_ref, rank)
        vectors = spread * leaf_ref[...]
        store_halves(dot(spread * vectors, queries_ref[...], 0), 1, keep_ref, send_ref, 0)
        for e in range(head):
            basis = vectors if e == 0 else level_ref[levels - e]
            store_halves(dot(basis, basis, 0), 0, keep_ref, send_ref, rank + e * rank // 2)

    late_keep, late_send = call(
        late_body,
        [(rank + head * rank // 2, rank)] * 2,
        scale,
        queries,
        leaf_basis,
        level_basis,
        name="late",
        flops=small * (2 + head) * rows_here // rank,
    )
    late_chip = late_keep + swap(late_send, "sub", 0)
    late_leaf = add_all(partial_sums(late_chip, "sub", leaf_bits))
    late_other = swap(late_leaf[rank:], "sub", 0)

    def product_body(group, own_ref, other_ref, *refs):
        core_refs, out_refs = refs[: len(group)], refs[len(group) :]
        base = starts[group[0]]
        for place, e in enumerate(group):
            where = pl.ds(starts[e] - base, half_rows[e])
            out_refs[place][...] = dot(join(own_ref[where, :], other_ref[where, :], 0), core_refs[place][...])

    def products(group, own):
        return call(
            functools.partial(product_body, group),
            [(2 * half_rows[e], rank) for e in group],
            own,
            swap(own, "sub", 0),
            *[cores[e] for e in group],
            name=f"product{group[0]}",
            flops=small * sum(len(blocks[e]) for e in group),
        )

    factors = products(list(range(head)), gram_leaf[: starts[head]])
    remaining = gram_leaf[starts[head] :]
    for e in range(head, count):
        remaining = add_all(partial_sums(remaining, "rows", bits[e]))
        factors += products([e], remaining[: half_rows[e]])
        remaining = remaining[half_rows[e] :]

    def head_body(*refs):
        part_refs, factor_refs = refs[: len(moment_parts)], refs[len(moment_parts) : -2]
        own_ref, rest_ref = refs[-2:]
        rest = add_all([part[...] for part in part_refs])
        for e in range(head):
            own, rest = rest[:rank], rest[rank:]
            own_ref[e * rank : (e + 1) * rank, :] = own
            rest = rest - dot(factor_refs[e][...], own)
        rest_ref[...] = rest

    head_moments, rest = call(
        head_body,
        [(head * rank, wide), ((count - head) * rank, wide)],
        *moment_parts,
        *factors[:head],
        name="head",
        flops=small * sum(map(len, blocks[:head])),
    )

    def step_body(size, *refs):
        part_refs, factor_ref, own_ref, rest_ref = refs[:size], refs[size], refs[-2], refs[-1]
        total = add_all([part[...] for part in part_refs])
        own_ref[...] = total[:rank]
        rest_ref[...] = total[rank:] - dot(factor_ref[rank:, :], total[:rank])

    moments = []
    for e in range(head, top):
        parts = partial_sums(rest, "rows", bits[e])
        own, rest = call(
            functools.partial(step_body, len(parts)),
            [(rank, wide), ((top - e) * rank, wide)],
            *parts,
            factors[e],
            name=f"step{e}",
            flops=small * (top - e),
        )
        moments.append([own, swap(own, "sub", 0)])
    parts = partial_sums(rest, "rows", bits[top])
    moments.append(parts + [swap(part, "sub", 0) for part in parts])

    def own_body(moment_ref, late_ref, other_ref, *refs):
        core_refs, factor_refs, out_ref = refs[:head], refs[head:-1], refs[-1]
        coefficients = [None] * head
        for e in reversed(range(head)):
            core = core_refs[e][...]
            where = slice(e * rank // 2, (e + 1) * rank // 2)
            gram = join(late_ref[rank:, :][where], other_ref[where, :], 0)
            moment = moment_ref[e * rank : (e + 1) * rank, :]
            first = dot(core, moment)
            target = (late_ref[:rank, :] if e == 0 else moment) - dot(gram, first)
            value = dot(core, target, 0)
            if e:
                value = value + first
            else:
                out_ref[head * rank :, :] = first
            for f in range(e + 1, head):
                block = factor_refs[e][(f - e - 1) * rank : (f - e) * rank, :]
                value = value - dot(block, coefficients[f], 0)
            coefficients[e] = value
            out_ref[e * rank : (e + 1) * rank, :] = value

    (own,) = call(
        own_body,
        [((head + 1) * rank, wide)],
        head_moments,
        late_leaf,
        late_other,
        *cores[:head],
        *factors[:head],
        name="own",
        flops=small * 6,
    )
    other = swap(own, "sub", 0)

    def start_body(scale_ref, queries_ref, leaf_ref, level_ref, own_ref, other_ref, out_ref):
        spread = column_scale(scale_ref, rank)
        whole = join(own_ref[...], other_ref[...], 1)
        left = [spread * (spread * leaf_ref[...])] + [spread * level_ref[levels - e] for e in range(1, head)]
        right = [whole[head * rank :]] + [whole[e * rank : (e + 1) * rank] for e in range(1, head)]
        left.append(leaf_ref[...])
        right.append(whole[:rank])
        total = dot(jnp.concatenate(left, axis=1), jnp.concatenate(right, axis=0))
        square = spread * spread
        square = jnp.concatenate([square] * (columns // rank), axis=1)
        out_ref[...] = square * queries_ref[...] - total

    (base,) = call(
        start_body,
        [(rows_here, columns)],
        scale,
        queries,
        leaf_basis,
        level_basis,
        own,
        other,
        name="start",
        flops=small * 2 * (head + 1) * rows_here // rank,
    )

    def response_body(scale_ref, leaf_ref, level_ref, *refs):
        core_refs, factor_refs, out_ref = refs[:levels], refs[levels:-1], refs[-1]
        spread = column_scale(scale_ref, rank)
        for e in range(head, count):
            core = core_refs[e - 1][...]
            gains = {e: core + core.T - dot(core, factor_refs[e][:rank, :], 0)}
            for f in reversed(range(e)):
                at = (0 if f < head else 1) * rank
                block = factor_refs[f][at : at + (e - f) * rank, :]
                stack = jnp.concatenate([gains[g] for g in range(f + 1, e + 1)], axis=0)
                gains[f] = -dot(block, stack, 0)
            left = [spread * level_ref[levels - f] for f in range(1, e + 1)] + [leaf_ref[...]]
            right = [gains[f] for f in range(1, e + 1)] + [gains[0]]
            out_ref[:, (e - head) * rank : (e - head + 1) * rank] = dot(
                jnp.concatenate(left, axis=1), jnp.concatenate(right, axis=0)
            )

    (response,) = call(
        response_body,
        [(rows_here, (count - head) * rank)],
        scale,
        leaf_basis,
        level_basis,
        *cores[1:],
        *factors,
        name="response",
        flops=small * (count - head) * count * rows_here // rank,
    )

    flat = [part for parts in moments for part in parts]
    sizes = [len(parts) // 2 for parts in moments]

    def last_body(base_ref, response_ref, *refs):
        part_refs, out_ref = refs[:-1], refs[-1]
        stack, at = [], 0
        for size in sizes:
            own = add_all([part[...] for part in part_refs[at : at + size]])
            other = add_all([part[...] for part in part_refs[at + size : at + 2 * size]])
            stack.append(join(own, other, 1))
            at += 2 * size
        out_ref[...] = base_ref[...] - dot(response_ref[...], jnp.concatenate(stack, axis=0))

    (out,) = call(
        last_body,
        [(rows_here, columns)],
        base,
        response,
        *flat,
        name="last",
        flops=small * 2 * (count - head) * rows_here // rank,
    )
    return out


def solution(mesh):
    in_specs = (
        P(("rows", "sub"), None),
        P(("rows", "sub")),
        P(("rows", "sub"), None),
        P("rows", None, None),
        P(None, ("rows", "sub"), None),
        P(),
    )
    out_specs = P(("rows", "sub"), None)
    return jax.shard_map(shards, mesh=mesh, in_specs=in_specs, out_specs=out_specs, check_vma=False)
```

time: 287 us -> 61.9 us (0.22)
  waiting for transfers between devices: 242 us -> 6.95 us
  Pallas kernels: 0 us -> 33.2 us
  matrix products: 21.4 us -> 0 us
  between operations: 13.7 us -> 0.2 us
  starting transfers between devices: 6.39 us -> 13 us
  local copies, waits for them, and re-layouts: 1.85 us -> 7.9 us
    psum x7 -> x0, waiting for transfers between devices: 227 us -> none  [the longest x5 160 us: node_total(): summed = lax.psum(partial_value, 'sub')]
    pallas_call x0 -> x12, Pallas kernels: none -> 33.2 us  [call(): pl.pallas_call(body, out_shape=outs, in_specs=[space] * len(operands), ou...]
    dot_general x24 -> x0, matrix products: 21.4 us -> none  [the longest x12 13.8 us: project(): lax.dot_general(vectors, values, (((0,), (0,)), ((), ())), precision=prec...]
    ppermute x4 -> x18, waiting for transfers between devices: 15.3 us -> 6.95 us  [swap(): lax.ppermute(array, axis, [(i, i ^ 1 << bit) for i in range(lax.axis_size...]
    ppermute x4 -> x18, starting transfers between devices: 5.95 us -> 13 us  [swap(): lax.ppermute(array, axis, [(i, i ^ 1 << bit) for i in range(lax.axis_size...]
    unnamed x15 -> x42, local copies, waits for them, and re-layouts: 0.76 us -> 6.29 us
  transfers between devices with their start and end apart: 11 -> 18, of which waited for: 11 -> 2; matrix products, arithmetic and copies ran while one was open for 0% -> 3% of each run, Pallas kernels for 0% -> 43%
where the time goes in v1:
time: 61.9 us; the launch traced here: 61.3 us
  Pallas kernels  33.2 us (54%)
  starting transfers between devices  13 us (21%)
  local copies, waits for them, and re-layouts  7.9 us (13%)
  waiting for transfers between devices  6.95 us (11%)
    pallas_call x12, Pallas kernels, call(): pl.pallas_call(body, out_shape=outs, in_specs=[space] * len(operands), ou...  33.2 us
    ppermute x18, starting transfers between devices, swap(): lax.ppermute(array, axis, [(i, i ^ 1 << bit) for i in range(lax.axis_size...  13 us
    ppermute x18, waiting for transfers between devices, swap(): lax.ppermute(array, axis, [(i, i ^ 1 << bit) for i in range(lax.axis_size...  6.95 us
    unnamed x42, local copies, waits for them, and re-layouts  6.29 us
    squeeze x1, local copies, waits for them, and re-layouts, shards(): lax.dynamic_index_in_dim(level_cores, 2 ** heights[e] - 2 + index // widt...  1.57 us
  transfers between devices with their start and end apart: 18, of which 2 were waited for; matrix products, arithmetic and copies ran while one was open for 3% of the time, Pallas kernels for 43%

profile of v1, /device:TPU:0, one launch (start us, length us, event | category | flops | bytes accessed | tf_op | source)
XLA Modules:
  0.0 61.3 jit_solution(17553733633194328718)
XLA Ops:
  0.0 4.2 %gram.1 = (f32[512,128]{1,0:T(8,128)}, f32[512,128]{1,0:T(8,128)}) custom-call(f32[4,128]{1,0:T(4,128)} %bitcast.10, f32[512,128]{1,0:T(8,128)} %leaf_ref.9, f32[3,512,128]{2,1,0:T(8,128)} %level_ref.9), custom_call_target="tpu_custom_call" | custom-call | flops 402653184 | bytes 1050624 | tf_op jit(solution)/shard_map/gram/pallas_call | solution.py:70
  4.2 0.5 collective-permute-start.2
  4.7 3.8 %moment.1 = (f32[512,128]{1,0:T(8,128)}, f32[512,128]{1,0:T(8,128)}) custom-call(f32[4,128]{1,0:T(4,128)} %bitcast.11, f32[512,256]{1,0:T(8,128)} %queries_ref.5, f32[512,128]{1,0:T(8,128)} %leaf_ref.9, f32[3,512,128]{2,1,0:T(8,128)} %level_ref.9), custom_call_target="tpu_custom_call" | custom-call | flops 402653184 | bytes 1574912 | tf_op jit(solution)/shard_map/moment/pallas_call | solution.py:70
  8.5 0.1 collective-permute-start
  8.6 0.0 collective-permute-done.2
  8.6 3.0 %collective-permute-start.3 = (f32[512,128]{1,0:T(8,128)S(1)}, f32[512,128]{1,0:T(8,128)S(1)}, u32[]{:S(2)}, u32[]{:S(2)}) collective-permute-start(f32[512,128]{1,0:T(8,128)S(1)} %add.42), channel_id=1, source_target_pairs={{0,2},{1,3},{2,0},{3,1},{4,6},{5,7},{6,4},{7,5},{8,10},{9,11},{10,... | collective-permute-start | bytes 786440 | tf_op jit(solution)/shard_map/ppermute | solution.py:81
  11.6 0.0 collective-permute-done
  11.6 0.0 copy-done.3
  11.7 0.0 copy-start
  11.7 1.3 %collective-permute-start.1 = (f32[512,128]{1,0:T(8,128)S(1)}, f32[512,128]{1,0:T(8,128)S(1)}, u32[]{:S(2)}, u32[]{:S(2)}) collective-permute-start(f32[512,128]{1,0:T(8,128)S(1)} %add.41.refs_0_), channel_id=1, source_target_pairs={{0,2},{1,3},{2,0},{3,1},{4,6},{5,7},{6,4},{7,5},{8,10},{9,11},{10,... | collective-permute-start | bytes 786440 | tf_op jit(solution)/shard_map/ppermute | solution.py:81
  13.0 5.8 %collective-permute-done.3 = f32[512,128]{1,0:T(8,128)S(1)} collective-permute-done((f32[512,128]{1,0:T(8,128)S(1)}, f32[512,128]{1,0:T(8,128)S(1)}, u32[]{:S(2)}, u32[]{:S(2)}) %collective-permute-start.3) | collective-permute-done | bytes 262176 | tf_op jit(solution)/shard_map/ppermute | solution.py:81
  18.8 0.1 collective-permute-start.4
  18.9 3.2 %late.1 = (f32[256,128]{1,0:T(8,128)}, f32[256,128]{1,0:T(8,128)}) custom-call(f32[4,128]{1,0:T(4,128)} %bitcast.12, f32[512,256]{1,0:T(8,128)} %queries_ref.5, f32[512,128]{1,0:T(8,128)} %leaf_ref.9, f32[3,512,128]{2,1,0:T(8,128)} %level_ref.9), custom_call_target="tpu_custom_call" | custom-call | flops 201326592 | bytes 1574912 | tf_op jit(solution)/shard_map/late/pallas_call | solution.py:70
  22.2 0.0 copy-done.2
  22.2 0.5 collective-permute-start.5
  22.7 2.1 %collective-permute-start.9 = (f32[192,128]{1,0:T(8,128)S(1)}, f32[192,128]{1,0:T(8,128)S(1)}, u32[]{:S(2)}, u32[]{:S(2)}) collective-permute-start(f32[192,128]{1,0:T(8,128)S(1)} %slice.22), channel_id=1, source_target_pairs={{0,4},{4,0},{8,12},{12,8},{16,20},{20,16},{24,28},{28,24},{1,5},{5... | collective-permute-start | bytes 294920 | tf_op jit(solution)/shard_map/ppermute | solution.py:81
  24.7 1.6 %dynamic-slice_bitcast_fusion = (f32[128,128]{1,0:T(8,128)}, f32[128,128]{1,0:T(8,128)}, f32[128,128]{1,0:T(8,128)}) fusion(f32[14,128,128]{2,1,0:T(8,128)} %param.11, s32[]{:T(128)S(6)} %select_n.23, s32[]{:T(128)S(6)} %select_n.19, s32[]{:T(128)S(6)} %select_n.21), kind=kLoop, calls=%fused_computation | loop fusion | bytes 393228 | tf_op jit(solution)/shard_map/jit(dynamic_index_in_dim)/squeeze | solution.py:118
  26.3 0.0 collective-permute-done.5
  26.3 1.6 %collective-permute-start.6 = (f32[256,128]{1,0:T(8,128)S(1)}, f32[256,128]{1,0:T(8,128)S(1)}, u32[]{:S(2)}, u32[]{:S(2)}) collective-permute-start(f32[256,128]{1,0:T(8,128)S(1)} %add.45), channel_id=1, source_target_pairs={{0,2},{1,3},{2,0},{3,1},{4,6},{5,7},{6,4},{7,5},{8,10},{9,11},{10,... | collective-permute-start | bytes 393224 | tf_op jit(solution)/shard_map/ppermute | solution.py:81
  27.9 0.0 collective-permute-done.4.other_ref
  27.9 0.7 %copy-done.8 = f32[320,128]{1,0:T(8,128)} copy-done((f32[320,128]{1,0:T(8,128)}, f32[320,128]{1,0:T(8,128)S(1)}, u32[]{:S(2)}) %copy-start.8) | copy-done | bytes 163864
  28.6 2.1 %product0.1 = (f32[384,128]{1,0:T(8,128)}, f32[256,128]{1,0:T(8,128)}) custom-call(f32[320,128]{1,0:T(8,128)} %copy-done.2, f32[320,128]{1,0:T(8,128)} %copy-done.8, f32[128,128]{1,0:T(8,128)} %bitcast.8, f32[128,128]{1,0:T(8,128)} %get-tuple-element.30.refs_1_.refs_0_), custom_call_target="tpu_custom_call" | custom-call | flops 62914560 | bytes 458752 | tf_op jit(solution)/shard_map/product0/pallas_call | solution.py:70
  30.6 0.0 collective-permute-done.1.refs_1_
  30.6 0.7 %copy-done.6 = f32[512,128]{1,0:T(8,128)} copy-done((f32[512,128]{1,0:T(8,128)}, f32[512,128]{1,0:T(8,128)S(1)}, u32[]{:S(2)}) %copy-start.6) | copy-done | bytes 262168
  31.3 2.2 %head.1 = (f32[256,128]{1,0:T(8,128)}, f32[256,128]{1,0:T(8,128)}) custom-call(f32[512,128]{1,0:T(8,128)} %copy-done, f32[512,128]{1,0:T(8,128)} %copy-done.6, f32[384,128]{1,0:T(8,128)} %get-tuple-element.21.refs_2_.refs_3_, f32[256,128]{1,0:T(8,128)} %get-tuple-element.22.refs_3_.refs_4_), custom_call_target="tpu_custom_call" | custom-call | flops 62914560 | bytes 851968 | tf_op jit(solution)/shard_map/head/pallas_call | solution.py:70
  33.6 0.5 collective-permute-start.13
  34.1 0.0 collective-permute-done.9
  34.1 0.0 copy-start.5
  34.2 0.1 collective-permute-start.10
  34.2 0.0 collective-permute-done.6
  34.3 0.5 copy-done.5
  34.8 0.1 collective-permute-start.7
  34.9 1.6 %collective-permute-start.11 = (f32[64,128]{1,0:T(8,128)S(1)}, f32[64,128]{1,0:T(8,128)S(1)}, u32[]{:S(2)}, u32[]{:S(2)}) collective-permute-start(f32[64,128]{1,0:T(8,128)S(1)} %slice.24), channel_id=1, source_target_pairs={{0,8},{4,12},{8,0},{12,4},{16,24},{20,28},{24,16},{28,20},{1,9},{5... | collective-permute-start | bytes 98312 | tf_op jit(solution)/shard_map/ppermute | solution.py:81
  36.5 0.0 collective-permute-done.10.other_ref
  36.5 0.6 %copy-done.18 = f32[128,128]{1,0:T(8,128)} copy-done((f32[128,128]{1,0:T(8,128)}, f32[128,128]{1,0:T(8,128)S(1)}, u32[]{:S(2)}) %copy-start.18) | copy-done | bytes 65560
  37.1 1.8 %product2.1.refs_5_.refs_2_ = f32[256,128]{1,0:T(8,128)} custom-call(f32[128,128]{1,0:T(8,128)} %copy-done.5, f32[128,128]{1,0:T(8,128)} %copy-done.18, f32[128,128]{1,0:T(8,128)} %get-tuple-element.31.refs_0_.refs_1_), custom_call_target="tpu_custom_call" | custom-call | flops 25165824 | bytes 196608 | tf_op jit(solution)/shard_map/product2/pallas_call | solution.py:70
  38.9 0.0 collective-permute-done.7.other_ref
  38.9 0.6 %copy-done.19 = f32[128,128]{1,0:T(8,128)} copy-done((f32[128,128]{1,0:T(8,128)}, f32[128,128]{1,0:T(8,128)S(1)}, u32[]{:S(2)}) %copy-start.19) | copy-done | bytes 65560
  39.5 2.6 %own.1.own_ref = f32[384,128]{1,0:T(8,128)} custom-call(f32[256,128]{1,0:T(8,128)} %get-tuple-element.23.moment_ref, f32[256,128]{1,0:T(8,128)} %copy-done.1, f32[128,128]{1,0:T(8,128)} %copy-done.19, f32[128,128]{1,0:T(8,128)} %bitcast.9, f32[128,128]{1,0:T(8,128)} %get-tuple-element.30.refs_1_.refs_0_, f32[384,128]{1,0:T(8,128)} %get-tuple-element.21.refs_2_.refs_3_, ...), custom_call_target="tpu_custom_call" | custom-call | flops 75497472 | bytes 786432 | tf_op jit(solution)/shard_map/own/pallas_call | solution.py:70
  42.2 0.1 collective-permute-start.8
  42.3 0.0 collective-permute-done.13.refs_1_
  42.3 0.6 %copy-done.10 = f32[256,128]{1,0:T(8,128)} copy-done((f32[256,128]{1,0:T(8,128)}, f32[256,128]{1,0:T(8,128)S(1)}, u32[]{:S(2)}) %copy-start.10) | copy-done | bytes 131096
  42.9 1.8 %step2.1 = (f32[128,128]{1,0:T(8,128)}, f32[128,128]{1,0:T(8,128)}) custom-call(f32[256,128]{1,0:T(8,128)} %get-tuple-element.26.refs_0_, f32[256,128]{1,0:T(8,128)} %copy-done.10, f32[256,128]{1,0:T(8,128)} %product2.1.refs_5_.refs_2_), custom_call_target="tpu_custom_call" | custom-call | flops 12582912 | bytes 393216 | tf_op jit(solution)/shard_map/step2/pallas_call | solution.py:70
  44.8 0.6 collective-permute-start.15
  45.3 0.0 collective-permute-done.11
  45.3 0.1 collective-permute-start.12
  45.5 1.1 %collective-permute-done.12.other_ref = f32[64,128]{1,0:T(8,128)S(1)} collective-permute-done((f32[64,128]{1,0:T(8,128)S(1)}, f32[64,128]{1,0:T(8,128)S(1)}, u32[]{:S(2)}, u32[]{:S(2)}) %collective-permute-start.12) | collective-permute-done | bytes 32800 | tf_op jit(solution)/shard_map/ppermute | solution.py:81
  46.6 0.6 copy-done.20
  47.2 1.7 %product3.1.refs_6_ = f32[128,128]{1,0:T(8,128)} custom-call(f32[64,128]{1,0:T(8,128)} %copy-done.11, f32[64,128]{1,0:T(8,128)} %copy-done.20, f32[128,128]{1,0:T(8,128)} %get-tuple-element.29.refs_0_.refs_2_), custom_call_target="tpu_custom_call" | custom-call | flops 12582912 | bytes 131072 | tf_op jit(solution)/shard_map/product3/pallas_call | solution.py:70
  48.9 0.2 collective-permute-start.16
  49.1 0.3 collective-permute-start.14
  49.4 0.0 collective-permute-done.15.refs_3_
  49.4 0.2 collective-permute-start.17
  49.6 4.4 %response.1.response_ref = f32[512,256]{1,0:T(8,128)} custom-call(f32[4,128]{1,0:T(4,128)} %bitcast.13, f32[512,128]{1,0:T(8,128)} %leaf_ref.9, f32[3,512,128]{2,1,0:T(8,128)} %level_ref.9, f32[128,128]{1,0:T(8,128)} %get-tuple-element.30.refs_1_.refs_0_, f32[128,128]{1,0:T(8,128)} %get-tuple-element.31.refs_0_.refs_1_, ...), custom_call_target="tpu_custom_call" | custom-call | flops 402653184 | bytes 1771520 | tf_op jit(solution)/shard_map/response/pallas_call | solution.py:70
  54.1 0.0 collective-permute-done.8.other_ref
  54.1 0.7 %copy-done.7 = f32[384,128]{1,0:T(8,128)} copy-done((f32[384,128]{1,0:T(8,128)}, f32[384,128]{1,0:T(8,128)S(1)}, u32[]{:S(2)}) %copy-start.7) | copy-done | bytes 196632
  54.7 2.9 %start.1.base_ref = f32[512,256]{1,0:T(8,128)} custom-call(f32[4,128]{1,0:T(4,128)} %bitcast.14, f32[512,256]{1,0:T(8,128)} %queries_ref.5, f32[512,128]{1,0:T(8,128)} %leaf_ref.9, f32[3,512,128]{2,1,0:T(8,128)} %level_ref.9, f32[384,128]{1,0:T(8,128)} %own.1.own_ref, f32[384,128]{1,0:T(8,128)} %copy-done.7), custom_call_target="tpu_custom_call" | custom-call | flops 301989888 | bytes 1968128 | tf_op jit(solution)/shard_map/start/pallas_call | solution.py:70
  57.6 0.0 collective-permute-done.14.refs_1_
  57.6 0.0 collective-permute-done.16.refs_4_
  57.7 0.0 collective-permute-done.17.refs_5_
  57.7 0.6 copy-done.16
  58.3 0.0 copy-done.15
  58.3 0.6 %copy-done.17 = f32[128,128]{1,0:T(8,128)} copy-done((f32[128,128]{1,0:T(8,128)}, f32[128,128]{1,0:T(8,128)S(1)}, u32[]{:S(2)}) %copy-start.17) | copy-done | bytes 65560
  58.9 2.4 %last.1 = f32[512,256]{1,0:T(8,128)} custom-call(f32[512,256]{1,0:T(8,128)} %start.1.base_ref, f32[512,256]{1,0:T(8,128)} %response.1.response_ref, f32[128,128]{1,0:T(8,128)} %get-tuple-element.27.refs_0_, f32[128,128]{1,0:T(8,128)} %copy-done.16, f32[128,128]{1,0:T(8,128)} %get-tuple-element.28.refs_2_, f32[128,128]{1,0:T(8,128)} %copy-done.14, ...), custom_call_target="tpu_custom_call" | custom-call | flops 201326592 | bytes 1441792 | tf_op jit(solution)/shard_map/last/pallas_call | solution.py:70
  (39 shorter events, 0.2 us)
Async XLA Ops:
  4.2 4.4 %copy-start.4 = (f32[512,128]{1,0:T(8,128)S(1)}, f32[512,128]{1,0:T(8,128)}, u32[]{:S(2)}) copy-start(f32[512,128]{1,0:T(8,128)} %get-tuple-element.19) | copy-start | bytes 786436
  4.2 4.4 %collective-permute-start.2 = (f32[512,128]{1,0:T(8,128)}, f32[512,128]{1,0:T(8,128)S(1)}, u32[]{:S(2)}, u32[]{:S(2)}) collective-permute-start(f32[512,128]{1,0:T(8,128)} %get-tuple-element.20), channel_id=1, source_target_pairs={{0,1},{1,0},{2,3},{3,2},{4,5},{5,4},{6,7},{7,6},{8,9},{9,8},{10,11... | collective-permute-start | bytes 786440 | tf_op jit(solution)/shard_map/ppermute | solution.py:81
  8.5 3.1 %collective-permute-start = (f32[512,128]{1,0:T(8,128)}, f32[512,128]{1,0:T(8,128)S(1)}, u32[]{:S(2)}, u32[]{:S(2)}) collective-permute-start(f32[512,128]{1,0:T(8,128)} %get-tuple-element.18), channel_id=1, source_target_pairs={{0,1},{1,0},{2,3},{3,2},{4,5},{5,4},{6,7},{7,6},{8,9},{9,8},{10,11... | collective-permute-start | bytes 786440 | tf_op jit(solution)/shard_map/ppermute | solution.py:81
  8.6 3.0 %copy-start.3 = (f32[512,128]{1,0:T(8,128)S(1)}, f32[512,128]{1,0:T(8,128)}, u32[]{:S(2)}) copy-start(f32[512,128]{1,0:T(8,128)} %get-tuple-element.17) | copy-start | bytes 786436
  8.6 10.2 %collective-permute-start.3 = (f32[512,128]{1,0:T(8,128)S(1)}, f32[512,128]{1,0:T(8,128)S(1)}, u32[]{:S(2)}, u32[]{:S(2)}) collective-permute-start(f32[512,128]{1,0:T(8,128)S(1)} %add.42), channel_id=1, source_target_pairs={{0,2},{1,3},{2,0},{3,1},{4,6},{5,7},{6,4},{7,5},{8,10},{9,11},{10,... | collective-permute-start | bytes 786440 | tf_op jit(solution)/shard_map/ppermute | solution.py:81
  11.7 7.2 %copy-start = (f32[512,128]{1,0:T(8,128)}, f32[512,128]{1,0:T(8,128)S(1)}, u32[]{:S(2)}) copy-start(f32[512,128]{1,0:T(8,128)S(1)} %add.41.refs_0_) | copy-start | bytes 786436
  11.7 19.0 %collective-permute-start.1 = (f32[512,128]{1,0:T(8,128)S(1)}, f32[512,128]{1,0:T(8,128)S(1)}, u32[]{:S(2)}, u32[]{:S(2)}) collective-permute-start(f32[512,128]{1,0:T(8,128)S(1)} %add.41.refs_0_), channel_id=1, source_target_pairs={{0,2},{1,3},{2,0},{3,1},{4,6},{5,7},{6,4},{7,5},{8,10},{9,11},{10,... | collective-permute-start | bytes 786440 | tf_op jit(solution)/shard_map/ppermute | solution.py:81
  18.8 3.3 %copy-start.2 = (f32[320,128]{1,0:T(8,128)}, f32[320,128]{1,0:T(8,128)S(1)}, u32[]{:S(2)}) copy-start(f32[320,128]{1,0:T(8,128)S(1)} %slice.20.own_ref) | copy-start | bytes 491524
  18.8 9.1 %collective-permute-start.4 = (f32[320,128]{1,0:T(8,128)S(1)}, f32[320,128]{1,0:T(8,128)S(1)}, u32[]{:S(2)}, u32[]{:S(2)}) collective-permute-start(f32[320,128]{1,0:T(8,128)S(1)} %slice.20.own_ref), channel_id=1, source_target_pairs={{0,1},{1,0},{2,3},{3,2},{4,5},{5,4},{6,7},{7,6},{8,9},{9,8},{10,11... | collective-permute-start | bytes 491528 | tf_op jit(solution)/shard_map/ppermute | solution.py:81
  22.2 4.2 %collective-permute-start.5 = (f32[256,128]{1,0:T(8,128)}, f32[256,128]{1,0:T(8,128)S(1)}, u32[]{:S(2)}, u32[]{:S(2)}) collective-permute-start(f32[256,128]{1,0:T(8,128)} %get-tuple-element.25), channel_id=1, source_target_pairs={{0,1},{1,0},{2,3},{3,2},{4,5},{5,4},{6,7},{7,6},{8,9},{9,8},{10,11... | collective-permute-start | bytes 393224 | tf_op jit(solution)/shard_map/ppermute | solution.py:81
  22.7 3.6 %copy-start.9 = (f32[256,128]{1,0:T(8,128)S(1)}, f32[256,128]{1,0:T(8,128)}, u32[]{:S(2)}) copy-start(f32[256,128]{1,0:T(8,128)} %get-tuple-element.24) | copy-start | bytes 393220
  22.7 11.4 %collective-permute-start.9 = (f32[192,128]{1,0:T(8,128)S(1)}, f32[192,128]{1,0:T(8,128)S(1)}, u32[]{:S(2)}, u32[]{:S(2)}) collective-permute-start(f32[192,128]{1,0:T(8,128)S(1)} %slice.22), channel_id=1, source_target_pairs={{0,4},{4,0},{8,12},{12,8},{16,20},{20,16},{24,28},{28,24},{1,5},{5... | collective-permute-start | bytes 294920 | tf_op jit(solution)/shard_map/ppermute | solution.py:81
  26.3 7.9 %collective-permute-start.6 = (f32[256,128]{1,0:T(8,128)S(1)}, f32[256,128]{1,0:T(8,128)S(1)}, u32[]{:S(2)}, u32[]{:S(2)}) collective-permute-start(f32[256,128]{1,0:T(8,128)S(1)} %add.45), channel_id=1, source_target_pairs={{0,2},{1,3},{2,0},{3,1},{4,6},{5,7},{6,4},{7,5},{8,10},{9,11},{10,... | collective-permute-start | bytes 393224 | tf_op jit(solution)/shard_map/ppermute | solution.py:81
  27.9 0.7 %copy-start.8 = (f32[320,128]{1,0:T(8,128)}, f32[320,128]{1,0:T(8,128)S(1)}, u32[]{:S(2)}) copy-start(f32[320,128]{1,0:T(8,128)S(1)} %collective-permute-done.4.other_ref) | copy-start | bytes 491524
  30.6 0.7 %copy-start.6 = (f32[512,128]{1,0:T(8,128)}, f32[512,128]{1,0:T(8,128)S(1)}, u32[]{:S(2)}) copy-start(f32[512,128]{1,0:T(8,128)S(1)} %collective-permute-done.1.refs_1_) | copy-start | bytes 786436
  33.6 8.7 %collective-permute-start.13 = (f32[256,128]{1,0:T(8,128)}, f32[256,128]{1,0:T(8,128)S(1)}, u32[]{:S(2)}, u32[]{:S(2)}) collective-permute-start(f32[256,128]{1,0:T(8,128)} %get-tuple-element.26.refs_0_), channel_id=1, source_target_pairs={{0,4},{4,0},{8,12},{12,8},{16,20},{20,16},{24,28},{28,24},{1,5},{5... | collective-permute-start | bytes 393224 | tf_op jit(solution)/shard_map/ppermute | solution.py:81
  34.1 0.6 %copy-start.5 = (f32[128,128]{1,0:T(8,128)}, f32[128,128]{1,0:T(8,128)S(1)}, u32[]{:S(2)}) copy-start(f32[128,128]{1,0:T(8,128)S(1)} %slice.23.own_ref) | copy-start | bytes 196612
  34.2 2.4 %collective-permute-start.10 = (f32[128,128]{1,0:T(8,128)S(1)}, f32[128,128]{1,0:T(8,128)S(1)}, u32[]{:S(2)}, u32[]{:S(2)}) collective-permute-start(f32[128,128]{1,0:T(8,128)S(1)} %slice.23.own_ref), channel_id=1, source_target_pairs={{0,1},{1,0},{2,3},{3,2},{4,5},{5,4},{6,7},{7,6},{8,9},{9,8},{10,11... | collective-permute-start | bytes 196616 | tf_op jit(solution)/shard_map/ppermute | solution.py:81
  34.8 4.1 %copy-start.1 = (f32[256,128]{1,0:T(8,128)}, f32[256,128]{1,0:T(8,128)S(1)}, u32[]{:S(2)}) copy-start(f32[256,128]{1,0:T(8,128)S(1)} %add.46.late_ref) | copy-start | bytes 393220
  34.8 4.1 %collective-permute-start.7 = (f32[128,128]{1,0:T(8,128)S(1)}, f32[128,128]{1,0:T(8,128)S(1)}, u32[]{:S(2)}, u32[]{:S(2)}) collective-permute-start(f32[128,128]{1,0:T(8,128)S(1)} %slice.21), channel_id=1, source_target_pairs={{0,1},{1,0},{2,3},{3,2},{4,5},{5,4},{6,7},{7,6},{8,9},{9,8},{10,11... | collective-permute-start | bytes 196616 | tf_op jit(solution)/shard_map/ppermute | solution.py:81
  34.9 10.4 %collective-permute-start.11 = (f32[64,128]{1,0:T(8,128)S(1)}, f32[64,128]{1,0:T(8,128)S(1)}, u32[]{:S(2)}, u32[]{:S(2)}) collective-permute-start(f32[64,128]{1,0:T(8,128)S(1)} %slice.24), channel_id=1, source_target_pairs={{0,8},{4,12},{8,0},{12,4},{16,24},{20,28},{24,16},{28,20},{1,9},{5... | collective-permute-start | bytes 98312 | tf_op jit(solution)/shard_map/ppermute | solution.py:81
  36.5 0.6 %copy-start.18 = (f32[128,128]{1,0:T(8,128)}, f32[128,128]{1,0:T(8,128)S(1)}, u32[]{:S(2)}) copy-start(f32[128,128]{1,0:T(8,128)S(1)} %collective-permute-done.10.other_ref) | copy-start | bytes 196612
  38.9 0.6 %copy-start.19 = (f32[128,128]{1,0:T(8,128)}, f32[128,128]{1,0:T(8,128)S(1)}, u32[]{:S(2)}) copy-start(f32[128,128]{1,0:T(8,128)S(1)} %collective-permute-done.7.other_ref) | copy-start | bytes 196612
  42.2 11.9 %collective-permute-start.8 = (f32[384,128]{1,0:T(8,128)}, f32[384,128]{1,0:T(8,128)S(1)}, u32[]{:S(2)}, u32[]{:S(2)}) collective-permute-start(f32[384,128]{1,0:T(8,128)} %own.1.own_ref), channel_id=1, source_target_pairs={{0,1},{1,0},{2,3},{3,2},{4,5},{5,4},{6,7},{7,6},{8,9},{9,8},{10,11... | collective-permute-start | bytes 589832 | tf_op jit(solution)/shard_map/ppermute | solution.py:81
  42.3 0.6 %copy-start.10 = (f32[256,128]{1,0:T(8,128)}, f32[256,128]{1,0:T(8,128)S(1)}, u32[]{:S(2)}) copy-start(f32[256,128]{1,0:T(8,128)S(1)} %collective-permute-done.13.refs_1_) | copy-start | bytes 393220
  44.8 4.7 %collective-permute-start.15 = (f32[128,128]{1,0:T(8,128)}, f32[128,128]{1,0:T(8,128)S(1)}, u32[]{:S(2)}, u32[]{:S(2)}) collective-permute-start(f32[128,128]{1,0:T(8,128)} %get-tuple-element.28.refs_2_), channel_id=1, source_target_pairs={{0,8},{4,12},{8,0},{12,4},{16,24},{20,28},{24,16},{28,20},{1,9},{5... | collective-permute-start | bytes 196616 | tf_op jit(solution)/shard_map/ppermute | solution.py:81
  45.3 1.3 %copy-start.11 = (f32[64,128]{1,0:T(8,128)}, f32[64,128]{1,0:T(8,128)S(1)}, u32[]{:S(2)}) copy-start(f32[64,128]{1,0:T(8,128)S(1)} %slice_add_fusion.own_ref) | copy-start | bytes 98308
  45.3 1.3 %collective-permute-start.12 = (f32[64,128]{1,0:T(8,128)S(1)}, f32[64,128]{1,0:T(8,128)S(1)}, u32[]{:S(2)}, u32[]{:S(2)}) collective-permute-start(f32[64,128]{1,0:T(8,128)S(1)} %slice_add_fusion.own_ref), channel_id=1, source_target_pairs={{0,1},{1,0},{2,3},{3,2},{4,5},{5,4},{6,7},{7,6},{8,9},{9,8},{10,11... | collective-permute-start | bytes 98312 | tf_op jit(solution)/shard_map/ppermute | solution.py:81
  46.6 0.6 copy-start.20
  47.2 1.7 %copy-start.13 = (f32[128,128]{1,0:T(8,128)S(1)}, f32[128,128]{1,0:T(8,128)}, u32[]{:S(2)}) copy-start(f32[128,128]{1,0:T(8,128)} %get-tuple-element.28.refs_2_) | copy-start | bytes 196612
  47.2 1.9 %copy-start.12 = (f32[128,128]{1,0:T(8,128)S(1)}, f32[128,128]{1,0:T(8,128)}, u32[]{:S(2)}) copy-start(f32[128,128]{1,0:T(8,128)} %get-tuple-element.27.refs_0_) | copy-start | bytes 196612
  48.9 8.7 %collective-permute-start.16 = (f32[128,128]{1,0:T(8,128)S(1)}, f32[128,128]{1,0:T(8,128)S(1)}, u32[]{:S(2)}, u32[]{:S(2)}) collective-permute-start(f32[128,128]{1,0:T(8,128)S(1)} %copy-done.13), channel_id=1, source_target_pairs={{0,1},{1,0},{2,3},{3,2},{4,5},{5,4},{6,7},{7,6},{8,9},{9,8},{10,11... | collective-permute-start | bytes 196616 | tf_op jit(solution)/shard_map/ppermute | solution.py:81
  49.1 8.5 %collective-permute-start.14 = (f32[128,128]{1,0:T(8,128)S(1)}, f32[128,128]{1,0:T(8,128)S(1)}, u32[]{:S(2)}, u32[]{:S(2)}) collective-permute-start(f32[128,128]{1,0:T(8,128)S(1)} %copy-done.12), channel_id=1, source_target_pairs={{0,1},{1,0},{2,3},{3,2},{4,5},{5,4},{6,7},{7,6},{8,9},{9,8},{10,11... | collective-permute-start | bytes 196616 | tf_op jit(solution)/shard_map/ppermute | solution.py:81
  49.4 4.6 %copy-start.14 = (f32[128,128]{1,0:T(8,128)}, f32[128,128]{1,0:T(8,128)S(1)}, u32[]{:S(2)}) copy-start(f32[128,128]{1,0:T(8,128)S(1)} %collective-permute-done.15.refs_3_) | copy-start | bytes 196612
  49.4 8.2 %collective-permute-start.17 = (f32[128,128]{1,0:T(8,128)S(1)}, f32[128,128]{1,0:T(8,128)S(1)}, u32[]{:S(2)}, u32[]{:S(2)}) collective-permute-start(f32[128,128]{1,0:T(8,128)S(1)} %collective-permute-done.15.refs_3_), channel_id=1, source_target_pairs={{0,1},{1,0},{2,3},{3,2},{4,5},{5,4},{6,7},{7,6},{8,9},{9,8},{10,11... | collective-permute-start | bytes 196616 | tf_op jit(solution)/shard_map/ppermute | solution.py:81
  54.1 0.7 %copy-start.7 = (f32[384,128]{1,0:T(8,128)}, f32[384,128]{1,0:T(8,128)S(1)}, u32[]{:S(2)}) copy-start(f32[384,128]{1,0:T(8,128)S(1)} %collective-permute-done.8.other_ref) | copy-start | bytes 589828
  57.6 0.6 %copy-start.16 = (f32[128,128]{1,0:T(8,128)}, f32[128,128]{1,0:T(8,128)S(1)}, u32[]{:S(2)}) copy-start(f32[128,128]{1,0:T(8,128)S(1)} %collective-permute-done.14.refs_1_) | copy-start | bytes 196612
  57.6 0.6 %copy-start.15 = (f32[128,128]{1,0:T(8,128)}, f32[128,128]{1,0:T(8,128)S(1)}, u32[]{:S(2)}) copy-start(f32[128,128]{1,0:T(8,128)S(1)} %collective-permute-done.16.refs_4_) | copy-start | bytes 196612
  58.3 0.6 %copy-start.17 = (f32[128,128]{1,0:T(8,128)}, f32[128,128]{1,0:T(8,128)S(1)}, u32[]{:S(2)}) copy-start(f32[128,128]{1,0:T(8,128)S(1)} %collective-permute-done.17.refs_5_) | copy-start | bytes 196612

commit v2 on v1

--- a/solution.py
+++ b/solution.py
@@ -9,6 +9,7 @@
 
 
 FLOAT = jnp.float32
+VMEM_LIMIT = 16 << 20
 
 
 def halves(value):
@@ -73,6 +74,7 @@
         in_specs=[space] * len(operands),
         out_specs=[space] * len(outs),
         name=name,
+        compiler_params=pltpu.CompilerParams(vmem_limit_bytes=VMEM_LIMIT),
         cost_estimate=pl.CostEstimate(flops=flops, bytes_accessed=size, transcendentals=0),
     )(*operands)
 

time: 61.9 us -> 39.5 us (0.64)
  Pallas kernels: 33.2 us -> 10.9 us
  local copies, waits for them, and re-layouts: 7.9 us -> 3.74 us
  waiting for transfers between devices: 6.95 us -> 10.7 us
    pallas_call x12, Pallas kernels: 33.2 us -> 10.9 us  [call(): pl.pallas_call(body, out_shape=outs, in_specs=[space] * len(operands), ou...]
    ppermute x18, waiting for transfers between devices: 6.95 us -> 10.7 us  [swap(): lax.ppermute(array, axis, [(i, i ^ 1 << bit) for i in range(lax.axis_size...]
    unnamed x42 -> x16, local copies, waits for them, and re-layouts: 6.29 us -> 2.79 us
    squeeze x1, local copies, waits for them, and re-layouts: 1.57 us -> 0.92 us  [shards(): lax.dynamic_index_in_dim(level_cores, 2 ** heights[e] - 2 + index // widt...]
  transfers between devices with their start and end apart: 18 -> 18, of which waited for: 2 -> 4; matrix products, arithmetic and copies ran while one was open for 3% -> 3% of each run, Pallas kernels for 43% -> 19%
where the time goes in v2:
time: 39.5 us; the launch traced here: 39.2 us
  starting transfers between devices  13.5 us (34%)
  Pallas kernels  10.9 us (28%)
  waiting for transfers between devices  10.7 us (27%)
  local copies, waits for them, and re-layouts  3.74 us (9%)
    ppermute x18, starting transfers between devices, swap(): lax.ppermute(array, axis, [(i, i ^ 1 << bit) for i in range(lax.axis_size...  13.5 us
    pallas_call x12, Pallas kernels, call(): pl.pallas_call(body, out_shape=outs, in_specs=[space] * len(operands), ou...  10.9 us
    ppermute x18, waiting for transfers between devices, swap(): lax.ppermute(array, axis, [(i, i ^ 1 << bit) for i in range(lax.axis_size...  10.7 us
    unnamed x16, local copies, waits for them, and re-layouts  2.79 us
    squeeze x1, local copies, waits for them, and re-layouts, shards(): lax.dynamic_index_in_dim(level_cores, 2 ** heights[e] - 2 + index // widt...  0.92 us
  transfers between devices with their start and end apart: 18, of which 4 were waited for; matrix products, arithmetic and copies ran while one was open for 3% of the time, Pallas kernels for 19%

profile of v2, /device:TPU:0, one launch (start us, length us, event | category | flops | bytes accessed | tf_op | source)
XLA Modules:
  0.0 39.2 jit_solution(7116225446000514086)
XLA Ops:
  0.0 0.0 copy-start
  0.0 1.1 %copy-done = f32[3,512,128]{2,1,0:T(8,128)S(1)} copy-done((f32[3,512,128]{2,1,0:T(8,128)S(1)}, f32[3,512,128]{2,1,0:T(8,128)}, u32[]{:S(2)}) %copy-start) | copy-done | bytes 786456
  1.1 0.0 copy-start.3
  1.1 0.9 %copy-done.3 = f32[512,128]{1,0:T(8,128)S(1)} copy-done((f32[512,128]{1,0:T(8,128)S(1)}, f32[512,128]{1,0:T(8,128)}, u32[]{:S(2)}) %copy-start.3) | copy-done | bytes 262168
  2.1 0.0 copy-start.6
  2.1 0.7 %copy-done.6 = f32[512]{0:T(512)S(1)} copy-done((f32[512]{0:T(512)S(1)}, f32[512]{0:T(512)}, u32[]{:S(2)}) %copy-start.6) | copy-done | bytes 2072
  2.8 0.0 copy-start.1
  2.8 0.0 copy-start.2
  2.8 2.1 %gram.1 = (f32[512,128]{1,0:T(8,128)S(1)}, f32[512,128]{1,0:T(8,128)S(1)}) custom-call(f32[4,128]{1,0:T(4,128)S(1)} %bitcast.10, f32[512,128]{1,0:T(8,128)S(1)} %copy-done.3, f32[3,512,128]{2,1,0:T(8,128)S(1)} %copy-done), custom_call_target="tpu_custom_call" | custom-call | flops 402653184 | bytes 1050624 | tf_op jit(solution)/shard_map/gram/pallas_call | solution.py:71
  4.9 0.6 %collective-permute-start.2 = (f32[512,128]{1,0:T(8,128)S(1)}, f32[512,128]{1,0:T(8,128)S(1)}, u32[]{:S(2)}, u32[]{:S(2)}) collective-permute-start(f32[512,128]{1,0:T(8,128)S(1)} %get-tuple-element.20), channel_id=1, source_target_pairs={{0,1},{1,0},{2,3},{3,2},{4,5},{5,4},{6,7},{7,6},{8,9},{9,8},{10,11... | collective-permute-start | bytes 786440 | tf_op jit(solution)/shard_map/ppermute | solution.py:83
  5.5 0.0 copy-done.1
  5.5 0.0 copy-done.2
  5.5 1.6 %moment.1 = (f32[512,128]{1,0:T(8,128)S(1)}, f32[512,128]{1,0:T(8,128)S(1)}) custom-call(f32[4,128]{1,0:T(4,128)S(1)} %bitcast.11, f32[512,256]{1,0:T(8,128)S(1)} %copy-done.2, f32[512,128]{1,0:T(8,128)S(1)} %copy-done.3, f32[3,512,128]{2,1,0:T(8,128)S(1)} %copy-done.1), custom_call_target="tpu_custom_call" | custom-call | flops 402653184 | bytes 1574912 | tf_op jit(solution)/shard_map/moment/pallas_call | solution.py:71
  7.1 0.1 collective-permute-start
  7.2 0.0 collective-permute-done.2
  7.3 3.0 %collective-permute-start.3 = (f32[512,128]{1,0:T(8,128)S(1)}, f32[512,128]{1,0:T(8,128)S(1)}, u32[]{:S(2)}, u32[]{:S(2)}) collective-permute-start(f32[512,128]{1,0:T(8,128)S(1)} %add.42), channel_id=1, source_target_pairs={{0,2},{1,3},{2,0},{3,1},{4,6},{5,7},{6,4},{7,5},{8,10},{9,11},{10,... | collective-permute-start | bytes 786440 | tf_op jit(solution)/shard_map/ppermute | solution.py:83
  10.3 0.0 collective-permute-done
  10.3 1.1 %collective-permute-start.1 = (f32[512,128]{1,0:T(8,128)S(1)}, f32[512,128]{1,0:T(8,128)S(1)}, u32[]{:S(2)}, u32[]{:S(2)}) collective-permute-start(f32[512,128]{1,0:T(8,128)S(1)} %add.41.refs_0_), channel_id=1, source_target_pairs={{0,2},{1,3},{2,0},{3,1},{4,6},{5,7},{6,4},{7,5},{8,10},{9,11},{10,... | collective-permute-start | bytes 786440 | tf_op jit(solution)/shard_map/ppermute | solution.py:83
  11.5 6.0 %collective-permute-done.3 = f32[512,128]{1,0:T(8,128)S(1)} collective-permute-done((f32[512,128]{1,0:T(8,128)S(1)}, f32[512,128]{1,0:T(8,128)S(1)}, u32[]{:S(2)}, u32[]{:S(2)}) %collective-permute-start.3) | collective-permute-done | bytes 262176 | tf_op jit(solution)/shard_map/ppermute | solution.py:83
  17.5 0.1 collective-permute-start.4
  17.6 1.1 %late.1 = (f32[256,128]{1,0:T(8,128)S(1)}, f32[256,128]{1,0:T(8,128)S(1)}) custom-call(f32[4,128]{1,0:T(4,128)S(1)} %bitcast.12, f32[512,256]{1,0:T(8,128)S(1)} %copy-done.2, f32[512,128]{1,0:T(8,128)S(1)} %copy-done.3, f32[3,512,128]{2,1,0:T(8,128)S(1)} %copy-done.1), custom_call_target="tpu_custom_call" | custom-call | flops 201326592 | bytes 1574912 | tf_op jit(solution)/shard_map/late/pallas_call | solution.py:71
  18.7 0.6 %collective-permute-start.5 = (f32[256,128]{1,0:T(8,128)S(1)}, f32[256,128]{1,0:T(8,128)S(1)}, u32[]{:S(2)}, u32[]{:S(2)}) collective-permute-start(f32[256,128]{1,0:T(8,128)S(1)} %get-tuple-element.25), channel_id=1, source_target_pairs={{0,1},{1,0},{2,3},{3,2},{4,5},{5,4},{6,7},{7,6},{8,9},{9,8},{10,11... | collective-permute-start | bytes 393224 | tf_op jit(solution)/shard_map/ppermute | solution.py:83
  19.3 2.1 %collective-permute-start.9 = (f32[192,128]{1,0:T(8,128)S(1)}, f32[192,128]{1,0:T(8,128)S(1)}, u32[]{:S(2)}, u32[]{:S(2)}) collective-permute-start(f32[192,128]{1,0:T(8,128)S(1)} %slice.22), channel_id=1, source_target_pairs={{0,4},{4,0},{8,12},{12,8},{16,20},{20,16},{24,28},{28,24},{1,5},{5... | collective-permute-start | bytes 294920 | tf_op jit(solution)/shard_map/ppermute | solution.py:83
  21.4 0.9 %dynamic-slice_bitcast_fusion = (f32[128,128]{1,0:T(8,128)S(1)}, f32[128,128]{1,0:T(8,128)S(1)}, f32[128,128]{1,0:T(8,128)S(1)}) fusion(f32[14,128,128]{2,1,0:T(8,128)} %param.11, s32[]{:T(128)S(6)} %select_n.23, s32[]{:T(128)S(6)} %select_n.19, s32[]{:T(128)S(6)} %select_n.21), kind=kLoop, calls=%fused_computation | loop fusion | bytes 393228 | tf_op jit(solution)/shard_map/jit(dynamic_index_in_dim)/squeeze | solution.py:120
  22.3 0.0 collective-permute-done.5
  22.3 0.0 copy-start.5
  22.3 1.6 %collective-permute-start.6 = (f32[256,128]{1,0:T(8,128)S(1)}, f32[256,128]{1,0:T(8,128)S(1)}, u32[]{:S(2)}, u32[]{:S(2)}) collective-permute-start(f32[256,128]{1,0:T(8,128)S(1)} %add.45), channel_id=1, source_target_pairs={{0,2},{1,3},{2,0},{3,1},{4,6},{5,7},{6,4},{7,5},{8,10},{9,11},{10,... | collective-permute-start | bytes 393224 | tf_op jit(solution)/shard_map/ppermute | solution.py:83
  23.9 0.0 collective-permute-done.4.other_ref
  23.9 0.0 copy-done.5
  23.9 0.3 product0.1
  24.2 0.0 collective-permute-done.1.refs_1_
  24.2 0.4 %head.1 = (f32[256,128]{1,0:T(8,128)S(1)}, f32[256,128]{1,0:T(8,128)S(1)}) custom-call(f32[512,128]{1,0:T(8,128)S(1)} %add.41.refs_0_, f32[512,128]{1,0:T(8,128)S(1)} %collective-permute-done.1.refs_1_, f32[384,128]{1,0:T(8,128)S(1)} %get-tuple-element.21.refs_2_.refs_3_, f32[256,128]{1,0:T(8,128)S(1)} %get-tuple-element.22.refs_3_.refs_4_), custom_call_target="tpu_custom_call" | custom-call | flops 62914560 | bytes 851968 | tf_op jit(solution)/shard_map/head/pallas_call | solution.py:71
  24.7 0.6 %collective-permute-start.13 = (f32[256,128]{1,0:T(8,128)S(1)}, f32[256,128]{1,0:T(8,128)S(1)}, u32[]{:S(2)}, u32[]{:S(2)}) collective-permute-start(f32[256,128]{1,0:T(8,128)S(1)} %get-tuple-element.26.refs_0_), channel_id=1, source_target_pairs={{0,4},{4,0},{8,12},{12,8},{16,20},{20,16},{24,28},{28,24},{1,5},{5... | collective-permute-start | bytes 393224 | tf_op jit(solution)/shard_map/ppermute | solution.py:83
  25.3 0.0 collective-permute-done.9
  25.3 0.1 collective-permute-start.10
  25.4 2.2 %collective-permute-done.6 = f32[256,128]{1,0:T(8,128)S(1)} collective-permute-done((f32[256,128]{1,0:T(8,128)S(1)}, f32[256,128]{1,0:T(8,128)S(1)}, u32[]{:S(2)}, u32[]{:S(2)}) %collective-permute-start.6) | collective-permute-done | bytes 131104 | tf_op jit(solution)/shard_map/ppermute | solution.py:83
  27.6 0.1 collective-permute-start.7
  27.7 1.6 %collective-permute-start.11 = (f32[64,128]{1,0:T(8,128)S(1)}, f32[64,128]{1,0:T(8,128)S(1)}, u32[]{:S(2)}, u32[]{:S(2)}) collective-permute-start(f32[64,128]{1,0:T(8,128)S(1)} %slice.24), channel_id=1, source_target_pairs={{0,8},{4,12},{8,0},{12,4},{16,24},{20,28},{24,16},{28,20},{1,9},{5... | collective-permute-start | bytes 98312 | tf_op jit(solution)/shard_map/ppermute | solution.py:83
  29.4 0.0 collective-permute-done.10.other_ref
  29.4 0.2 product2.1.refs_5_.refs_2_
  29.6 0.0 collective-permute-done.7.other_ref
  29.6 0.7 %own.1.own_ref = f32[384,128]{1,0:T(8,128)S(1)} custom-call(f32[256,128]{1,0:T(8,128)S(1)} %get-tuple-element.23.moment_ref, f32[256,128]{1,0:T(8,128)S(1)} %add.46.late_ref, f32[128,128]{1,0:T(8,128)S(1)} %collective-permute-done.7.other_ref, f32[128,128]{1,0:T(8,128)S(1)} %bitcast.9, f32[128,128]{1,0:T(8,128)S(1)} %get-tuple-element.30.refs_1_.refs_0_, ...), custom_call_target="tpu_custom_call" | custom-call | flops 75497472 | bytes 786432 | tf_op jit(solution)/shard_map/own/pallas_call | solution.py:71
  30.3 0.0 copy-start.4
  30.3 0.2 collective-permute-start.8
  30.5 0.0 collective-permute-done.13.refs_1_
  30.6 0.2 step2.1
  30.7 1.0 %collective-permute-start.15 = (f32[128,128]{1,0:T(8,128)S(1)}, f32[128,128]{1,0:T(8,128)S(1)}, u32[]{:S(2)}, u32[]{:S(2)}) collective-permute-start(f32[128,128]{1,0:T(8,128)S(1)} %get-tuple-element.28.refs_2_), channel_id=1, source_target_pairs={{0,8},{4,12},{8,0},{12,4},{16,24},{20,28},{24,16},{28,20},{1,9},{5... | collective-permute-start | bytes 196616 | tf_op jit(solution)/shard_map/ppermute | solution.py:83
  31.8 0.0 collective-permute-done.11
  31.8 0.1 collective-permute-start.12
  31.9 1.1 %collective-permute-done.12.other_ref = f32[64,128]{1,0:T(8,128)S(1)} collective-permute-done((f32[64,128]{1,0:T(8,128)S(1)}, f32[64,128]{1,0:T(8,128)S(1)}, u32[]{:S(2)}, u32[]{:S(2)}) %collective-permute-start.12) | collective-permute-done | bytes 32800 | tf_op jit(solution)/shard_map/ppermute | solution.py:83
  33.0 0.2 product3.1.refs_6_
  33.2 0.2 collective-permute-start.16
  33.4 0.3 collective-permute-start.14
  33.8 1.4 %collective-permute-done.15.refs_3_ = f32[128,128]{1,0:T(8,128)S(1)} collective-permute-done((f32[128,128]{1,0:T(8,128)S(1)}, f32[128,128]{1,0:T(8,128)S(1)}, u32[]{:S(2)}, u32[]{:S(2)}) %collective-permute-start.15) | collective-permute-done | bytes 65568 | tf_op jit(solution)/shard_map/ppermute | solution.py:83
  35.2 0.0 collective-permute-start.17
  35.2 0.0 copy-done.4
  35.2 0.0 copy-done.7
  35.2 2.2 %response.1.response_ref = f32[512,256]{1,0:T(8,128)S(1)} custom-call(f32[4,128]{1,0:T(4,128)S(1)} %bitcast.13, f32[512,128]{1,0:T(8,128)S(1)} %copy-done.4, f32[3,512,128]{2,1,0:T(8,128)S(1)} %copy-done.1, f32[128,128]{1,0:T(8,128)S(1)} %get-tuple-element.30.refs_1_.refs_0_, f32[128,128]{1,0:T(8,128)S(1)} %get-tuple-element.31.refs_0_.refs_1_, ...), custom_call_target="tpu_custom_call" | custom-call | flops 402653184 | bytes 1771520 | tf_op jit(solution)/shard_map/response/pallas_call | solution.py:71
  37.4 0.0 collective-permute-done.8.other_ref
  37.4 0.6 %start.1.base_ref = f32[512,256]{1,0:T(8,128)S(1)} custom-call(f32[4,128]{1,0:T(4,128)S(1)} %bitcast.14, f32[512,256]{1,0:T(8,128)S(1)} %copy-done.2, f32[512,128]{1,0:T(8,128)S(1)} %copy-done.4, f32[3,512,128]{2,1,0:T(8,128)S(1)} %copy-done.1, f32[384,128]{1,0:T(8,128)S(1)} %own.1.own_ref, f32[384,128]{1,0:T(8,128)S(1)} %collective-permute-done.8.other_ref), custom_call_target="tpu_custom_call" | custom-call | flops 301989888 | bytes 1968128 | tf_op jit(solution)/shard_map/start/pallas_call | solution.py:71
  38.0 0.0 collective-permute-done.14.refs_1_
  38.0 0.0 collective-permute-done.16.refs_4_
  38.0 0.0 collective-permute-done.17.refs_5_
  38.0 1.2 %last.1 = f32[512,256]{1,0:T(8,128)} custom-call(f32[512,256]{1,0:T(8,128)S(1)} %start.1.base_ref, f32[512,256]{1,0:T(8,128)S(1)} %response.1.response_ref, f32[128,128]{1,0:T(8,128)S(1)} %get-tuple-element.27.refs_0_, f32[128,128]{1,0:T(8,128)S(1)} %collective-permute-done.14.refs_1_, f32[128,128]{1,0:T(8,128)S(1)} %get-tuple-element.28.refs_2_, ...), custom_call_target="tpu_custom_call" | custom-call | flops 201326592 | bytes 1441792 | tf_op jit(solution)/shard_map/last/pallas_call | solution.py:71
  (13 shorter events, 0.2 us)
Async XLA Ops:
  0.0 1.1 %copy-start = (f32[3,512,128]{2,1,0:T(8,128)S(1)}, f32[3,512,128]{2,1,0:T(8,128)}, u32[]{:S(2)}) copy-start(f32[3,512,128]{2,1,0:T(8,128)} %level_ref.9) | copy-start | bytes 2359300
  1.1 0.9 %copy-start.3 = (f32[512,128]{1,0:T(8,128)S(1)}, f32[512,128]{1,0:T(8,128)}, u32[]{:S(2)}) copy-start(f32[512,128]{1,0:T(8,128)} %leaf_ref.9) | copy-start | bytes 786436
  2.1 0.7 %copy-start.6 = (f32[512]{0:T(512)S(1)}, f32[512]{0:T(512)}, u32[]{:S(2)}) copy-start(f32[512]{0:T(512)} %param.7) | copy-start | bytes 6148
  2.8 2.7 %copy-start.1 = (f32[3,512,128]{2,1,0:T(8,128)S(1)}, f32[3,512,128]{2,1,0:T(8,128)}, u32[]{:S(2)}) copy-start(f32[3,512,128]{2,1,0:T(8,128)} %level_ref.9) | copy-start | bytes 2359300
  2.8 2.7 %copy-start.2 = (f32[512,256]{1,0:T(8,128)S(1)}, f32[512,256]{1,0:T(8,128)}, u32[]{:S(2)}) copy-start(f32[512,256]{1,0:T(8,128)} %queries_ref.5) | copy-start | bytes 1572868
  4.9 2.3 %collective-permute-start.2 = (f32[512,128]{1,0:T(8,128)S(1)}, f32[512,128]{1,0:T(8,128)S(1)}, u32[]{:S(2)}, u32[]{:S(2)}) collective-permute-start(f32[512,128]{1,0:T(8,128)S(1)} %get-tuple-element.20), channel_id=1, source_target_pairs={{0,1},{1,0},{2,3},{3,2},{4,5},{5,4},{6,7},{7,6},{8,9},{9,8},{10,11... | collective-permute-start | bytes 786440 | tf_op jit(solution)/shard_map/ppermute | solution.py:83
  7.1 3.2 %collective-permute-start = (f32[512,128]{1,0:T(8,128)S(1)}, f32[512,128]{1,0:T(8,128)S(1)}, u32[]{:S(2)}, u32[]{:S(2)}) collective-permute-start(f32[512,128]{1,0:T(8,128)S(1)} %get-tuple-element.18), channel_id=1, source_target_pairs={{0,1},{1,0},{2,3},{3,2},{4,5},{5,4},{6,7},{7,6},{8,9},{9,8},{10,11... | collective-permute-start | bytes 786440 | tf_op jit(solution)/shard_map/ppermute | solution.py:83
  7.3 10.2 %collective-permute-start.3 = (f32[512,128]{1,0:T(8,128)S(1)}, f32[512,128]{1,0:T(8,128)S(1)}, u32[]{:S(2)}, u32[]{:S(2)}) collective-permute-start(f32[512,128]{1,0:T(8,128)S(1)} %add.42), channel_id=1, source_target_pairs={{0,2},{1,3},{2,0},{3,1},{4,6},{5,7},{6,4},{7,5},{8,10},{9,11},{10,... | collective-permute-start | bytes 786440 | tf_op jit(solution)/shard_map/ppermute | solution.py:83
  10.3 13.9 %collective-permute-start.1 = (f32[512,128]{1,0:T(8,128)S(1)}, f32[512,128]{1,0:T(8,128)S(1)}, u32[]{:S(2)}, u32[]{:S(2)}) collective-permute-start(f32[512,128]{1,0:T(8,128)S(1)} %add.41.refs_0_), channel_id=1, source_target_pairs={{0,2},{1,3},{2,0},{3,1},{4,6},{5,7},{6,4},{7,5},{8,10},{9,11},{10,... | collective-permute-start | bytes 786440 | tf_op jit(solution)/shard_map/ppermute | solution.py:83
  17.5 6.4 %collective-permute-start.4 = (f32[320,128]{1,0:T(8,128)S(1)}, f32[320,128]{1,0:T(8,128)S(1)}, u32[]{:S(2)}, u32[]{:S(2)}) collective-permute-start(f32[320,128]{1,0:T(8,128)S(1)} %slice.20.own_ref), channel_id=1, source_target_pairs={{0,1},{1,0},{2,3},{3,2},{4,5},{5,4},{6,7},{7,6},{8,9},{9,8},{10,11... | collective-permute-start | bytes 491528 | tf_op jit(solution)/shard_map/ppermute | solution.py:83
  18.7 3.5 %collective-permute-start.5 = (f32[256,128]{1,0:T(8,128)S(1)}, f32[256,128]{1,0:T(8,128)S(1)}, u32[]{:S(2)}, u32[]{:S(2)}) collective-permute-start(f32[256,128]{1,0:T(8,128)S(1)} %get-tuple-element.25), channel_id=1, source_target_pairs={{0,1},{1,0},{2,3},{3,2},{4,5},{5,4},{6,7},{7,6},{8,9},{9,8},{10,11... | collective-permute-start | bytes 393224 | tf_op jit(solution)/shard_map/ppermute | solution.py:83
  19.3 6.0 %collective-permute-start.9 = (f32[192,128]{1,0:T(8,128)S(1)}, f32[192,128]{1,0:T(8,128)S(1)}, u32[]{:S(2)}, u32[]{:S(2)}) collective-permute-start(f32[192,128]{1,0:T(8,128)S(1)} %slice.22), channel_id=1, source_target_pairs={{0,4},{4,0},{8,12},{12,8},{16,20},{20,16},{24,28},{28,24},{1,5},{5... | collective-permute-start | bytes 294920 | tf_op jit(solution)/shard_map/ppermute | solution.py:83
  22.3 1.6 %copy-start.5 = (f32[1,128,128]{2,1,0:T(8,128)S(1)}, f32[1,128,128]{2,1,0:T(8,128)}, u32[]{:S(2)}) copy-start(f32[1,128,128]{2,1,0:T(8,128)} %param.9) | copy-start | bytes 196612
  22.3 5.2 %collective-permute-start.6 = (f32[256,128]{1,0:T(8,128)S(1)}, f32[256,128]{1,0:T(8,128)S(1)}, u32[]{:S(2)}, u32[]{:S(2)}) collective-permute-start(f32[256,128]{1,0:T(8,128)S(1)} %add.45), channel_id=1, source_target_pairs={{0,2},{1,3},{2,0},{3,1},{4,6},{5,7},{6,4},{7,5},{8,10},{9,11},{10,... | collective-permute-start | bytes 393224 | tf_op jit(solution)/shard_map/ppermute | solution.py:83
  24.7 5.9 %collective-permute-start.13 = (f32[256,128]{1,0:T(8,128)S(1)}, f32[256,128]{1,0:T(8,128)S(1)}, u32[]{:S(2)}, u32[]{:S(2)}) collective-permute-start(f32[256,128]{1,0:T(8,128)S(1)} %get-tuple-element.26.refs_0_), channel_id=1, source_target_pairs={{0,4},{4,0},{8,12},{12,8},{16,20},{20,16},{24,28},{28,24},{1,5},{5... | collective-permute-start | bytes 393224 | tf_op jit(solution)/shard_map/ppermute | solution.py:83
  25.3 4.0 %collective-permute-start.10 = (f32[128,128]{1,0:T(8,128)S(1)}, f32[128,128]{1,0:T(8,128)S(1)}, u32[]{:S(2)}, u32[]{:S(2)}) collective-permute-start(f32[128,128]{1,0:T(8,128)S(1)} %slice.23.own_ref), channel_id=1, source_target_pairs={{0,1},{1,0},{2,3},{3,2},{4,5},{5,4},{6,7},{7,6},{8,9},{9,8},{10,11... | collective-permute-start | bytes 196616 | tf_op jit(solution)/shard_map/ppermute | solution.py:83
  27.6 1.9 %collective-permute-start.7 = (f32[128,128]{1,0:T(8,128)S(1)}, f32[128,128]{1,0:T(8,128)S(1)}, u32[]{:S(2)}, u32[]{:S(2)}) collective-permute-start(f32[128,128]{1,0:T(8,128)S(1)} %slice.21), channel_id=1, source_target_pairs={{0,1},{1,0},{2,3},{3,2},{4,5},{5,4},{6,7},{7,6},{8,9},{9,8},{10,11... | collective-permute-start | bytes 196616 | tf_op jit(solution)/shard_map/ppermute | solution.py:83
  27.7 4.0 %collective-permute-start.11 = (f32[64,128]{1,0:T(8,128)S(1)}, f32[64,128]{1,0:T(8,128)S(1)}, u32[]{:S(2)}, u32[]{:S(2)}) collective-permute-start(f32[64,128]{1,0:T(8,128)S(1)} %slice.24), channel_id=1, source_target_pairs={{0,8},{4,12},{8,0},{12,4},{16,24},{20,28},{24,16},{28,20},{1,9},{5... | collective-permute-start | bytes 98312 | tf_op jit(solution)/shard_map/ppermute | solution.py:83
  30.3 4.8 %copy-start.4 = (f32[512,128]{1,0:T(8,128)S(1)}, f32[512,128]{1,0:T(8,128)}, u32[]{:S(2)}) copy-start(f32[512,128]{1,0:T(8,128)} %leaf_ref.9) | copy-start | bytes 786436
  30.3 7.0 %collective-permute-start.8 = (f32[384,128]{1,0:T(8,128)S(1)}, f32[384,128]{1,0:T(8,128)S(1)}, u32[]{:S(2)}, u32[]{:S(2)}) collective-permute-start(f32[384,128]{1,0:T(8,128)S(1)} %own.1.own_ref), channel_id=1, source_target_pairs={{0,1},{1,0},{2,3},{3,2},{4,5},{5,4},{6,7},{7,6},{8,9},{9,8},{10,11... | collective-permute-start | bytes 589832 | tf_op jit(solution)/shard_map/ppermute | solution.py:83
  30.7 4.4 %collective-permute-start.15 = (f32[128,128]{1,0:T(8,128)S(1)}, f32[128,128]{1,0:T(8,128)S(1)}, u32[]{:S(2)}, u32[]{:S(2)}) collective-permute-start(f32[128,128]{1,0:T(8,128)S(1)} %get-tuple-element.28.refs_2_), channel_id=1, source_target_pairs={{0,8},{4,12},{8,0},{12,4},{16,24},{20,28},{24,16},{28,20},{1,9},{5... | collective-permute-start | bytes 196616 | tf_op jit(solution)/shard_map/ppermute | solution.py:83
  31.8 1.3 %collective-permute-start.12 = (f32[64,128]{1,0:T(8,128)S(1)}, f32[64,128]{1,0:T(8,128)S(1)}, u32[]{:S(2)}, u32[]{:S(2)}) collective-permute-start(f32[64,128]{1,0:T(8,128)S(1)} %slice_add_fusion.own_ref), channel_id=1, source_target_pairs={{0,1},{1,0},{2,3},{3,2},{4,5},{5,4},{6,7},{7,6},{8,9},{9,8},{10,11... | collective-permute-start | bytes 98312 | tf_op jit(solution)/shard_map/ppermute | solution.py:83
  33.0 2.1 %copy-start.7 = (f32[512]{0:T(512)S(1)}, f32[512]{0:T(512)}, u32[]{:S(2)}) copy-start(f32[512]{0:T(512)} %param.7) | copy-start | bytes 6148
  33.2 4.8 %collective-permute-start.16 = (f32[128,128]{1,0:T(8,128)S(1)}, f32[128,128]{1,0:T(8,128)S(1)}, u32[]{:S(2)}, u32[]{:S(2)}) collective-permute-start(f32[128,128]{1,0:T(8,128)S(1)} %get-tuple-element.28.refs_2_), channel_id=1, source_target_pairs={{0,1},{1,0},{2,3},{3,2},{4,5},{5,4},{6,7},{7,6},{8,9},{9,8},{10,11... | collective-permute-start | bytes 196616 | tf_op jit(solution)/shard_map/ppermute | solution.py:83
  33.4 4.6 %collective-permute-start.14 = (f32[128,128]{1,0:T(8,128)S(1)}, f32[128,128]{1,0:T(8,128)S(1)}, u32[]{:S(2)}, u32[]{:S(2)}) collective-permute-start(f32[128,128]{1,0:T(8,128)S(1)} %get-tuple-element.27.refs_0_), channel_id=1, source_target_pairs={{0,1},{1,0},{2,3},{3,2},{4,5},{5,4},{6,7},{7,6},{8,9},{9,8},{10,11... | collective-permute-start | bytes 196616 | tf_op jit(solution)/shard_map/ppermute | solution.py:83
  35.2 2.9 %collective-permute-start.17 = (f32[128,128]{1,0:T(8,128)S(1)}, f32[128,128]{1,0:T(8,128)S(1)}, u32[]{:S(2)}, u32[]{:S(2)}) collective-permute-start(f32[128,128]{1,0:T(8,128)S(1)} %collective-permute-done.15.refs_3_), channel_id=1, source_target_pairs={{0,1},{1,0},{2,3},{3,2},{4,5},{5,4},{6,7},{7,6},{8,9},{9,8},{10,11... | collective-permute-start | bytes 196616 | tf_op jit(solution)/shard_map/ppermute | solution.py:83

commit v3 on v2

v3 whole, which is shorter than its diff:
```python
import functools

import jax
import jax.numpy as jnp
from jax import lax
from jax.experimental import pallas as pl
from jax.experimental.pallas import tpu as pltpu
from jax.sharding import PartitionSpec as P


FLOAT = jnp.float32
VMEM_LIMIT = 16 << 20


def halves(value):
    high = value.astype(jnp.bfloat16)
    return high, (value - high.astype(FLOAT)).astype(jnp.bfloat16)


def dot_parts(left, right, right_dim=0):
    mult = functools.partial(
        lax.dot_general,
        dimension_numbers=(((1,), (right_dim,)), ((), ())),
        preferred_element_type=FLOAT,
    )
    return mult(left[0], right[0]) + (mult(left[0], right[1]) + mult(left[1], right[0]))


def dot(left, right, right_dim=0):
    return dot_parts(halves(left), halves(right), right_dim)


def lanes(values):
    return values[0] if len(values) == 1 else jnp.concatenate(values, axis=1)


def column_scale(scale):
    size = scale.shape[1]
    return jnp.concatenate(
        [jnp.broadcast_to(scale[i : i + 1, :], (size, size)).T for i in range(scale.shape[0])], axis=0
    )


def core_side():
    return lax.rem(lax.axis_index("sub"), 2)


def own_block():
    place, value = lax.axis_index("sub"), 0
    for _ in range(lax.axis_size("sub").bit_length() - 1):
        value = value * 2 + lax.rem(place, 2)
        place = place // 2
    return value


def at(index, size):
    return pl.ds(pl.multiple_of(index * size, 8), size)


def call(body, out_shapes, *operands, name, flops, spaces=None, scratch=()):
    spaces = spaces or [pltpu.VMEM] * len(operands)
    size = sum(4 * a.size for a in operands)
    outs = [jax.ShapeDtypeStruct(shape, FLOAT) for shape in out_shapes]
    return pl.pallas_call(
        body,
        out_shape=outs,
        in_specs=[pl.BlockSpec(memory_space=space) for space in spaces],
        out_specs=[pl.BlockSpec(memory_space=pltpu.VMEM)] * len(outs),
        scratch_shapes=list(scratch),
        name=name,
        compiler_params=pltpu.CompilerParams(vmem_limit_bytes=VMEM_LIMIT),
        cost_estimate=pl.CostEstimate(flops=flops, bytes_accessed=size, transcendentals=0),
    )(*operands)


def swap(array, axis, bit):
    return lax.ppermute(array, axis, [(i, i ^ 1 << bit) for i in range(lax.axis_size(axis))])


def partial_sums(array, axis, bits):
    bits = list(bits)
    if not bits:
        return [array]
    for bit in bits[:-1]:
        array = array + swap(array, axis, bit)
    return [array, swap(array, axis, bits[-1])]


def add_all(parts):
    return functools.reduce(lambda a, b: a + b, parts)


def shards(queries, row_scale, leaf_basis, leaf_cores, level_basis, level_cores):
    levels = level_basis.shape[0]
    count = levels + 1
    top = levels
    rows_here, rank = leaf_basis.shape
    columns = queries.shape[1]
    groups, sub = lax.axis_size("rows"), lax.axis_size("sub")
    heights = [None] + [levels + 1 - e for e in range(1, count)]
    widths = [1] + [groups // 2 ** heights[e] for e in range(1, count)]
    head = sum(w == 1 for w in widths)
    bits = [range(0)] + [
        range(widths[e - 1].bit_length() - 1, widths[e].bit_length() - 1) for e in range(1, count)
    ]
    blocks = [list(range(e + 1 if e < head else e, count)) for e in range(count)]
    sub_bits = sub.bit_length() - 1
    leaf_bits = range(1, sub_bits)
    mine = columns // sub
    half = rank // 2
    small = 2 * 3 * rank**3

    scale = row_scale.reshape(-1, rank)
    index = lax.axis_index("rows")
    cores = [leaf_cores[0]] + [
        lax.dynamic_index_in_dim(level_cores, 2 ** heights[e] - 2 + index // widths[e], 0, keepdims=False)
        for e in range(1, count)
    ]
    starts = [sum(len(b) for b in blocks[:e]) * rank for e in range(count + 1)]

    def gram_body(scale_hbm, leaf_hbm, level_hbm, out_ref, scale_ref, leaf_ref, level_ref, sems):
        copies = [
            pltpu.make_async_copy(scale_hbm, scale_ref, sems.at[0]),
            pltpu.make_async_copy(leaf_hbm, leaf_ref, sems.at[1]),
        ]
        copies += [
            pltpu.make_async_copy(level_hbm.at[e], level_ref.at[e], sems.at[2 + e]) for e in range(levels)
        ]
        for copy in copies:
            copy.start()
        for copy in copies:
            copy.wait()
        vectors = [column_scale(scale_ref[...]) * leaf_ref[...]]
        vectors += [level_ref[levels - e] for e in range(1, count)]
        parts = [halves(v) for v in vectors]
        side = core_side()
        for e in range(count):
            right = [lanes([parts[f][i] for f in blocks[e]]) for i in range(2)]
            value = dot_parts(halves(vectors[e].T), right)
            for h in range(2):
                out_ref[at(h ^ side, half), starts[e] : starts[e + 1]] = value[h * half : (h + 1) * half]

    (gram,) = call(
        gram_body,
        [(rank, starts[count])],
        scale,
        leaf_basis,
        level_basis,
        name="gram",
        flops=small * sum(map(len, blocks)) * rows_here // rank,
        spaces=[pltpu.HBM] * 3,
        scratch=[
            pltpu.VMEM(scale.shape, FLOAT),
            pltpu.VMEM(leaf_basis.shape, FLOAT),
            pltpu.VMEM(level_basis.shape, FLOAT),
            pltpu.SemaphoreType.DMA((2 + levels,)),
        ],
    )
    gram_chip = gram[:half] + swap(gram[half:], "sub", 0)
    gram_leaf = add_all(partial_sums(gram_chip, "sub", leaf_bits))

    def moment_body(scale_ref, queries_ref, leaf_ref, level_ref, out_ref):
        spread = column_scale(scale_ref[...])
        right = lanes([leaf_ref[...]] + [spread * level_ref[levels - e] for e in range(1, count)])
        value = dot(queries_ref[...].T, right)
        own = own_block()
        for i in range(sub):
            out_ref[at(i ^ own, mine), :] = value[i * mine : (i + 1) * mine]

    (value,) = call(
        moment_body,
        [(columns, count * rank)],
        scale,
        queries,
        leaf_basis,
        level_basis,
        name="moment",
        flops=small * count * 2 * rows_here // rank,
    )
    size = columns
    for bit in range(sub_bits):
        size //= 2
        moment_parts = [value[:size], swap(value[size:], "sub", bit)]
        value = add_all(moment_parts)

    late_rows = columns // 2 + head * half

    def late_body(scale_ref, queries_ref, leaf_ref, level_ref, out_ref):
        spread = column_scale(scale_ref[...])
        vectors = spread * leaf_ref[...]
        side = core_side()
        value = dot(queries_ref[...].T, spread * vectors)
        for h in range(2):
            base = (h ^ side) * late_rows
            part = value[h * columns // 2 : (h + 1) * columns // 2]
            out_ref[pl.ds(pl.multiple_of(base, 8), columns // 2), :] = part
        for e in range(head):
            basis = vectors if e == 0 else level_ref[levels - e]
            value = dot(basis.T, basis)
            for h in range(2):
                base = (h ^ side) * late_rows + columns // 2 + e * half
                out_ref[pl.ds(pl.multiple_of(base, 8), half), :] = value[h * half : (h + 1) * half]

    (late,) = call(
        late_body,
        [(2 * late_rows, rank)],
        scale,
        queries,
        leaf_basis,
        level_basis,
        name="late",
        flops=small * (2 + head) * rows_here // rank,
    )
    late_keep, late_got = late[:late_rows], swap(late[late_rows:], "sub", 0)

    def product_body(group, own_ref, other_ref, *refs):
        core_refs, out_refs, stack_ref = refs[: len(group)], refs[len(group) : -1], refs[-1]
        side = core_side()
        stack_ref[at(side, half), :] = own_ref[...]
        stack_ref[at(1 - side, half), :] = other_ref[...]
        base = starts[group[0]]
        for place, e in enumerate(group):
            out_refs[place][...] = dot(
                core_refs[place][...].T, stack_ref[:, starts[e] - base : starts[e + 1] - base]
            )

    def products(group, own):
        return call(
            functools.partial(product_body, group),
            [(rank, starts[e + 1] - starts[e]) for e in group],
            own,
            swap(own, "sub", 0),
            *[cores[e] for e in group],
            name=f"product{group[0]}",
            flops=small * sum(len(blocks[e]) for e in group),
            scratch=[pltpu.VMEM((rank, own.shape[1]), FLOAT)],
        )

    factors = products(list(range(head)), gram_leaf[:, : starts[head]])
    remaining = gram_leaf[:, starts[head] :]
    for e in range(head, count):
        remaining = add_all(partial_sums(remaining, "rows", bits[e]))
        size = starts[e + 1] - starts[e]
        factors += products([e], remaining[:, :size])
        remaining = remaining[:, size:]

    def head_body(*refs):
        part_refs, factor_refs = refs[: len(moment_parts)], refs[len(moment_parts) : -5]
        keep_ref, got_ref, own_ref, rest_ref, late_ref = refs[-5:]
        rest = add_all([part[...] for part in part_refs])
        for e in range(head):
            own, rest = rest[:, :rank], rest[:, rank:]
            own_ref[:, e * rank : (e + 1) * rank] = own
            rest = rest - dot(own, factor_refs[e][...])
        rest_ref[...] = rest
        late_ref[...] = keep_ref[...] + got_ref[...]

    head_moments, rest, late_chip = call(
        head_body,
        [(mine, head * rank), (mine, (count - head) * rank), (late_rows, rank)],
        *moment_parts,
        *factors[:head],
        late_keep,
        late_got,
        name="head",
        flops=small * sum(map(len, blocks[:head])),
    )

    def step_body(number, *refs):
        part_refs, factor_ref, own_ref, rest_ref = refs[:number], refs[number], refs[-2], refs[-1]
        total = add_all([part[...] for part in part_refs])
        own_ref[...] = total[:, :rank]
        rest_ref[...] = total[:, rank:] - dot(total[:, :rank], factor_ref[:, rank:])

    def gather(own):
        for bit in reversed(range(1, sub_bits)):
            own = jnp.concatenate([own, swap(own, "sub", bit)], axis=0)
        return [own, swap(own, "sub", 0)]

    def scatter(parts, stack_ref, where):
        own, slot = own_block(), 0
        for part in parts:
            for i in range(part.shape[0] // mine):
                stack_ref[at(slot ^ own, mine), where] = part[i * mine : (i + 1) * mine, :]
                slot += 1

    late_leaf = add_all(partial_sums(late_chip, "sub", leaf_bits))
    late_other = swap(late_leaf, "sub", 0)
    head_parts = gather(head_moments)

    coarse_parts = []
    for e in range(head, top):
        parts = partial_sums(rest, "rows", bits[e])
        own, rest = call(
            functools.partial(step_body, len(parts)),
            [(mine, rank), (mine, (top - e) * rank)],
            *parts,
            factors[e],
            name=f"step{e}",
            flops=small * (top - e),
        )
        coarse_parts.append(gather(own))
    coarse_parts.append(gather(add_all(partial_sums(rest, "rows", bits[top]))))

    def response(e, spread, leaf_ref, level_ref, core_refs, factor_refs, diagonal):
        core = core_refs[e][...]
        if e == 0:
            right = [core, -dot(diagonal, core)]
            left = [spread * (spread * leaf_ref[...]), leaf_ref[...]]
        else:
            gains = {e: core + core.T - dot(diagonal, core)}
            for f in reversed(range(e)):
                start = (0 if f < head else 1) * rank
                stack = jnp.concatenate([gains[g] for g in range(f + 1, e + 1)], axis=0)
                gains[f] = -dot(factor_refs[f][:, start : start + (e - f) * rank], stack)
            left = [spread * level_ref[levels - f] for f in range(1, e + 1)] + [leaf_ref[...]]
            right = [gains[f] for f in range(1, e + 1)] + [gains[0]]
        return dot(lanes(left), jnp.concatenate(right, axis=0))

    def coarse_body(scale_ref, leaf_ref, level_ref, *refs):
        core_refs, factor_refs, out_ref = refs[:count], refs[count:-1], refs[-1]
        spread = column_scale(scale_ref[...])
        for e in range(head, count):
            out_ref[:, (e - head) * rank : (e - head + 1) * rank] = response(
                e, spread, leaf_ref, level_ref, core_refs, factor_refs, factor_refs[e][:, :rank]
            )

    (coarse,) = call(
        coarse_body,
        [(rows_here, (count - head) * rank)],
        scale,
        leaf_basis,
        level_basis,
        *cores,
        *factors,
        name="coarse",
        flops=small * (count - head) * count * rows_here // rank,
    )

    def base_body(scale_ref, queries_ref, leaf_ref, level_ref, own_ref, other_ref, *refs):
        core_refs, factor_refs = refs[:head], refs[head : 2 * head]
        part_refs, out_ref, stack_ref, gram_ref = refs[2 * head : -3], refs[-3], refs[-2], refs[-1]
        spread = column_scale(scale_ref[...])
        scatter(part_refs, stack_ref, pl.ds(0, head * rank))
        side = core_side()
        for late_ref, place in ((own_ref, side), (other_ref, 1 - side)):
            stack_ref[at(place, columns // 2), head * rank :] = late_ref[: columns // 2]
            for e in range(head):
                start = columns // 2 + e * half
                gram_ref[at(place, half), e * rank : (e + 1) * rank] = late_ref[start : start + half]
        left = []
        for e in range(head):
            diagonal = dot(core_refs[e][...].T, gram_ref[:, e * rank : (e + 1) * rank])
            left.append(response(e, spread, leaf_ref, level_ref, core_refs, factor_refs, diagonal))
        left.append(dot(leaf_ref[...], core_refs[0][...].T))
        square = spread * spread
        out_ref[...] = lanes([square] * (columns // rank)) * queries_ref[...] - dot(
            lanes(left), stack_ref[...], 1
        )

    (base,) = call(
        base_body,
        [(rows_here, columns)],
        scale,
        queries,
        leaf_basis,
        level_basis,
        late_leaf,
        late_other,
        *cores[:head],
        *factors[:head],
        *head_parts,
        name="base",
        flops=small * 2 * (head + 1) * rows_here // rank,
        scratch=[pltpu.VMEM((columns, (head + 1) * rank), FLOAT), pltpu.VMEM((rank, head * rank), FLOAT)],
    )

    def last_body(base_ref, coarse_ref, *refs):
        part_refs, out_ref, stack_ref = refs[:-2], refs[-2], refs[-1]
        at_part = 0
        for e, parts in enumerate(coarse_parts):
            scatter(part_refs[at_part : at_part + len(parts)], stack_ref, pl.ds(e * rank, rank))
            at_part += len(parts)
        out_ref[...] = base_ref[...] - dot(coarse_ref[...], stack_ref[...], 1)

    (out,) = call(
        last_body,
        [(rows_here, columns)],
        base,
        coarse,
        *[part for parts in coarse_parts for part in parts],
        name="last",
        flops=small * 2 * (count - head) * rows_here // rank,
        scratch=[pltpu.VMEM((columns, (count - head) * rank), FLOAT)],
    )
    return out


def solution(mesh):
    in_specs = (
        P(("rows", "sub"), None),
        P(("rows", "sub")),
        P(("rows", "sub"), None),
        P("rows", None, None),
        P(None, ("rows", "sub"), None),
        P(),
    )
    out_specs = P(("rows", "sub"), None)
    return jax.shard_map(shards, mesh=mesh, in_specs=in_specs, out_specs=out_specs, check_vma=False)
```

time: 39.5 us -> 49 us (1.24)
  waiting for transfers between devices: 10.7 us -> 17.1 us
  starting transfers between devices: 13.5 us -> 17.4 us
  Pallas kernels: 10.9 us -> 9.29 us
  local copies, waits for them, and re-layouts: 3.74 us -> 4.39 us
    ppermute x18 -> x20, waiting for transfers between devices: 10.7 us -> 17.1 us  [swap(): lax.ppermute(array, axis, [(i, i ^ 1 << bit) for i in range(lax.axis_size...]
    ppermute x18 -> x20, starting transfers between devices: 13.5 us -> 17.4 us  [swap(): lax.ppermute(array, axis, [(i, i ^ 1 << bit) for i in range(lax.axis_size...]
    pallas_call x12 -> x11, Pallas kernels: 10.9 us -> 9.29 us  [call(): pl.pallas_call(body, out_shape=outs, in_specs=[pl.BlockSpec(memory_space=...]
    unnamed x16 -> x18, local copies, waits for them, and re-layouts: 2.79 us -> 3.35 us
  transfers between devices with their start and end apart: 18 -> 20, of which waited for: 4 -> 7; matrix products, arithmetic and copies ran while one was open for 3% -> 2% of each run, Pallas kernels for 19% -> 15%
where the time goes in v3:
time: 49 us; the launch traced here: 48.6 us
  starting transfers between devices  17.4 us (36%)
  waiting for transfers between devices  17.1 us (35%)
  Pallas kernels  9.29 us (19%)
  local copies, waits for them, and re-layouts  4.39 us (9%)
    ppermute x20, starting transfers between devices, swap(): lax.ppermute(array, axis, [(i, i ^ 1 << bit) for i in range(lax.axis_size...  17.4 us
    ppermute x20, waiting for transfers between devices, swap(): lax.ppermute(array, axis, [(i, i ^ 1 << bit) for i in range(lax.axis_size...  17.1 us
    pallas_call x11, Pallas kernels, call(): pl.pallas_call(body, out_shape=outs, in_specs=[pl.BlockSpec(memory_space=...  9.29 us
    unnamed x18, local copies, waits for them, and re-layouts  3.35 us
  transfers between devices with their start and end apart: 20, of which 7 were waited for; matrix products, arithmetic and copies ran while one was open for 2% of the time, Pallas kernels for 15%

profile of v3, /device:TPU:0, one launch (start us, length us, event | category | flops | bytes accessed | tf_op | source)
XLA Modules:
  0.0 48.6 jit_solution(11688109842730686533)
XLA Ops:
  0.0 1.1 %copy-done = f32[3,512,128]{2,1,0:T(8,128)S(1)} copy-done((f32[3,512,128]{2,1,0:T(8,128)S(1)}, f32[3,512,128]{2,1,0:T(8,128)}, u32[]{:S(2)}) %copy-start) | copy-done | bytes 786456
  1.1 0.9 %copy-done.2 = f32[512,128]{1,0:T(8,128)S(1)} copy-done((f32[512,128]{1,0:T(8,128)S(1)}, f32[512,128]{1,0:T(8,128)}, u32[]{:S(2)}) %copy-start.2) | copy-done | bytes 262168
  2.1 0.7 %copy-done.6 = f32[512]{0:T(512)S(1)} copy-done((f32[512]{0:T(512)S(1)}, f32[512]{0:T(512)}, u32[]{:S(2)}) %copy-start.6) | copy-done | bytes 2072
  2.8 0.9 %gram.1 = f32[128,1024]{1,0:T(8,128)S(1)} custom-call(f32[4,128]{1,0:T(4,128)S(1)} %bitcast.11, f32[512,128]{1,0:T(8,128)S(1)} %copy-done.2, f32[3,512,128]{2,1,0:T(8,128)S(1)} %copy-done), custom_call_target="tpu_custom_call" | custom-call | flops 402653184 | bytes 1050624 | tf_op jit(solution)/shard_map/gram/pallas_call | solution.py:64
  3.7 0.0 copy-start.1
  3.8 0.0 copy-start.3
  3.8 0.6 %collective-permute-start.2 = (f32[64,1024]{1,0:T(8,128)S(1)}, f32[64,1024]{1,0:T(8,128)S(1)}, u32[]{:S(2)}, u32[]{:S(2)}) collective-permute-start(f32[64,1024]{1,0:T(8,128)S(1)} %slice.53), channel_id=1, source_target_pairs={{0,1},{1,0},{2,3},{3,2},{4,5},{5,4},{6,7},{7,6},{8,9},{9,8},{10,11... | collective-permute-start | bytes 786440 | tf_op jit(solution)/shard_map/ppermute | solution.py:77
  4.3 1.2 %collective-permute-done.2 = f32[64,1024]{1,0:T(8,128)S(1)} collective-permute-done((f32[64,1024]{1,0:T(8,128)S(1)}, f32[64,1024]{1,0:T(8,128)S(1)}, u32[]{:S(2)}, u32[]{:S(2)}) %collective-permute-start.2) | collective-permute-done | bytes 262176 | tf_op jit(solution)/shard_map/ppermute | solution.py:77
  5.5 2.9 %collective-permute-start.3 = (f32[64,1024]{1,0:T(8,128)S(1)}, f32[64,1024]{1,0:T(8,128)S(1)}, u32[]{:S(2)}, u32[]{:S(2)}) collective-permute-start(f32[64,1024]{1,0:T(8,128)S(1)} %slice_add_fusion), channel_id=1, source_target_pairs={{0,2},{1,3},{2,0},{3,1},{4,6},{5,7},{6,4},{7,5},{8,10},{9,11},{10,... | collective-permute-start | bytes 786440 | tf_op jit(solution)/shard_map/ppermute | solution.py:77
  8.5 0.0 copy-done.4
  8.5 0.0 copy-done.1
  8.5 0.0 copy-done.3
  8.5 0.7 %moment.1 = f32[256,512]{1,0:T(8,128)S(1)} custom-call(f32[4,128]{1,0:T(4,128)S(1)} %bitcast.12, f32[512,256]{1,0:T(8,128)S(1)} %copy-done.4, f32[512,128]{1,0:T(8,128)S(1)} %copy-done.3, f32[3,512,128]{2,1,0:T(8,128)S(1)} %copy-done.1), custom_call_target="tpu_custom_call" | custom-call | flops 402653184 | bytes 1574912 | tf_op jit(solution)/shard_map/moment/pallas_call | solution.py:64
  9.3 0.1 collective-permute-start
  9.3 0.7 %late.1 = f32[512,128]{1,0:T(8,128)S(1)} custom-call(f32[4,128]{1,0:T(4,128)S(1)} %bitcast.13, f32[512,256]{1,0:T(8,128)S(1)} %copy-done.4, f32[512,128]{1,0:T(8,128)S(1)} %copy-done.3, f32[3,512,128]{2,1,0:T(8,128)S(1)} %copy-done.1), custom_call_target="tpu_custom_call" | custom-call | flops 201326592 | bytes 1574912 | tf_op jit(solution)/shard_map/late/pallas_call | solution.py:64
  10.1 0.6 %collective-permute-start.5 = (f32[256,128]{1,0:T(8,128)S(1)}, f32[256,128]{1,0:T(8,128)S(1)}, u32[]{:S(2)}, u32[]{:S(2)}) collective-permute-start(f32[256,128]{1,0:T(8,128)S(1)} %get-tuple-element.22), channel_id=1, source_target_pairs={{0,1},{1,0},{2,3},{3,2},{4,5},{5,4},{6,7},{7,6},{8,9},{9,8},{10,11... | collective-permute-start | bytes 393224 | tf_op jit(solution)/shard_map/ppermute | solution.py:77
  10.7 4.4 %collective-permute-done.3 = f32[64,1024]{1,0:T(8,128)S(1)} collective-permute-done((f32[64,1024]{1,0:T(8,128)S(1)}, f32[64,1024]{1,0:T(8,128)S(1)}, u32[]{:S(2)}, u32[]{:S(2)}) %collective-permute-start.3) | collective-permute-done | bytes 262176 | tf_op jit(solution)/shard_map/ppermute | solution.py:77
  15.1 1.8 %collective-permute-start.10 = (f32[64,384]{1,0:T(8,128)S(1)}, f32[64,384]{1,0:T(8,128)S(1)}, u32[]{:S(2)}, u32[]{:S(2)}) collective-permute-start(f32[64,384]{1,0:T(8,128)S(1)} %slice.57), channel_id=1, source_target_pairs={{0,4},{4,0},{8,12},{12,8},{16,20},{20,16},{24,28},{28,24},{1,5},{5... | collective-permute-start | bytes 294920 | tf_op jit(solution)/shard_map/ppermute | solution.py:77
  16.9 0.0 collective-permute-done
  17.0 2.9 %collective-permute-done.10 = f32[64,384]{1,0:T(8,128)S(1)} collective-permute-done((f32[64,384]{1,0:T(8,128)S(1)}, f32[64,384]{1,0:T(8,128)S(1)}, u32[]{:S(2)}, u32[]{:S(2)}) %collective-permute-start.10) | collective-permute-done | bytes 98336 | tf_op jit(solution)/shard_map/ppermute | solution.py:77
  19.8 1.9 %collective-permute-start.12 = (f32[64,128]{1,0:T(8,128)S(1)}, f32[64,128]{1,0:T(8,128)S(1)}, u32[]{:S(2)}, u32[]{:S(2)}) collective-permute-start(f32[64,128]{1,0:T(8,128)S(1)} %slice.59), channel_id=1, source_target_pairs={{0,8},{4,12},{8,0},{12,4},{16,24},{20,28},{24,16},{28,20},{1,9},{5... | collective-permute-start | bytes 98312 | tf_op jit(solution)/shard_map/ppermute | solution.py:77
  21.7 1.6 %collective-permute-start.1 = (f32[64,512]{1,0:T(8,128)S(1)}, f32[64,512]{1,0:T(8,128)S(1)}, u32[]{:S(2)}, u32[]{:S(2)}) collective-permute-start(f32[64,512]{1,0:T(8,128)S(1)} %get-tuple-element.24), channel_id=1, source_target_pairs={{0,2},{1,3},{2,0},{3,1},{4,6},{5,7},{6,4},{7,5},{8,10},{9,11},{10,... | collective-permute-start | bytes 393224 | tf_op jit(solution)/shard_map/ppermute | solution.py:77
  23.3 0.1 collective-permute-start.4
  23.4 0.5 %collective-permute-start.11 = (f32[64,256]{1,0:T(8,128)S(1)}, f32[64,256]{1,0:T(8,128)S(1)}, u32[]{:S(2)}, u32[]{:S(2)}) collective-permute-start(f32[64,256]{1,0:T(8,128)S(1)} %slice.58.own_ref), channel_id=1, source_target_pairs={{0,1},{1,0},{2,3},{3,2},{4,5},{5,4},{6,7},{7,6},{8,9},{9,8},{10,11... | collective-permute-start | bytes 196616 | tf_op jit(solution)/shard_map/ppermute | solution.py:77
  23.9 0.0 collective-permute-done.12
  23.9 0.2 collective-permute-start.13
  24.1 0.9 %dynamic-slice_bitcast_fusion = (f32[128,128]{1,0:T(8,128)S(1)}, f32[128,128]{1,0:T(8,128)S(1)}, f32[128,128]{1,0:T(8,128)S(1)}) fusion(f32[14,128,128]{2,1,0:T(8,128)} %param.11, s32[]{:T(128)S(6)} %select_n.23, s32[]{:T(128)S(6)} %select_n.19, s32[]{:T(128)S(6)} %select_n.21), kind=kLoop, calls=%fused_computation.3 | loop fusion | bytes 393228 | tf_op jit(solution)/shard_map/jit(dynamic_index_in_dim)/squeeze | solution.py:116
  25.0 0.0 collective-permute-done.11.other_ref
  25.0 0.0 copy-start.5
  25.0 0.3 product2.1.refs_6_.refs_2_
  25.3 0.0 collective-permute-done.4.other_ref
  25.3 0.6 %copy-done.5 = f32[1,128,128]{2,1,0:T(8,128)S(1)} copy-done((f32[1,128,128]{2,1,0:T(8,128)S(1)}, f32[1,128,128]{2,1,0:T(8,128)}, u32[]{:S(2)}) %copy-start.5) | copy-done | bytes 65560
  25.8 0.4 product0.1
  26.2 0.0 collective-permute-done.5.refs_5_
  26.2 0.6 %collective-permute-done.1.refs_1_ = f32[64,512]{1,0:T(8,128)S(1)} collective-permute-done((f32[64,512]{1,0:T(8,128)S(1)}, f32[64,512]{1,0:T(8,128)S(1)}, u32[]{:S(2)}, u32[]{:S(2)}) %collective-permute-start.1) | collective-permute-done | bytes 131104 | tf_op jit(solution)/shard_map/ppermute | solution.py:77
  26.8 0.4 head.1
  27.1 1.6 %collective-permute-start.6 = (f32[256,128]{1,0:T(8,128)S(1)}, f32[256,128]{1,0:T(8,128)S(1)}, u32[]{:S(2)}, u32[]{:S(2)}) collective-permute-start(f32[256,128]{1,0:T(8,128)S(1)} %get-tuple-element.14), channel_id=1, source_target_pairs={{0,2},{1,3},{2,0},{3,1},{4,6},{5,7},{6,4},{7,5},{8,10},{9,11},{10,... | collective-permute-start | bytes 393224 | tf_op jit(solution)/shard_map/ppermute | solution.py:77
  28.7 0.5 %collective-permute-start.8 = (f32[64,256]{1,0:T(8,128)S(1)}, f32[64,256]{1,0:T(8,128)S(1)}, u32[]{:S(2)}, u32[]{:S(2)}) collective-permute-start(f32[64,256]{1,0:T(8,128)S(1)} %get-tuple-element.15), channel_id=1, source_target_pairs={{0,2},{1,3},{2,0},{3,1},{4,6},{5,7},{6,4},{7,5},{8,10},{9,11},{10,... | collective-permute-start | bytes 196616 | tf_op jit(solution)/shard_map/ppermute | solution.py:77
  29.2 1.5 %collective-permute-start.14 = (f32[64,256]{1,0:T(8,128)S(1)}, f32[64,256]{1,0:T(8,128)S(1)}, u32[]{:S(2)}, u32[]{:S(2)}) collective-permute-start(f32[64,256]{1,0:T(8,128)S(1)} %get-tuple-element.16.refs_0_), channel_id=1, source_target_pairs={{0,4},{4,0},{8,12},{12,8},{16,20},{20,16},{24,28},{28,24},{1,5},{5... | collective-permute-start | bytes 196616 | tf_op jit(solution)/shard_map/ppermute | solution.py:77
  30.7 0.0 collective-permute-done.13.other_ref
  30.7 0.2 product3.1.refs_7_
  31.0 2.5 %collective-permute-done.14.refs_1_ = f32[64,256]{1,0:T(8,128)S(1)} collective-permute-done((f32[64,256]{1,0:T(8,128)S(1)}, f32[64,256]{1,0:T(8,128)S(1)}, u32[]{:S(2)}, u32[]{:S(2)}) %collective-permute-start.14) | collective-permute-done | bytes 65568 | tf_op jit(solution)/shard_map/ppermute | solution.py:77
  33.5 0.1 step2.1
  33.6 1.6 %collective-permute-start.15 = (f32[64,128]{1,0:T(8,128)S(1)}, f32[64,128]{1,0:T(8,128)S(1)}, u32[]{:S(2)}, u32[]{:S(2)}) collective-permute-start(f32[64,128]{1,0:T(8,128)S(1)} %get-tuple-element.17), channel_id=1, source_target_pairs={{0,2},{1,3},{2,0},{3,1},{4,6},{5,7},{6,4},{7,5},{8,10},{9,11},{10,... | collective-permute-start | bytes 98312 | tf_op jit(solution)/shard_map/ppermute | solution.py:77
  35.2 1.0 %collective-permute-start.17 = (f32[64,128]{1,0:T(8,128)S(1)}, f32[64,128]{1,0:T(8,128)S(1)}, u32[]{:S(2)}, u32[]{:S(2)}) collective-permute-start(f32[64,128]{1,0:T(8,128)S(1)} %get-tuple-element.18), channel_id=1, source_target_pairs={{0,8},{4,12},{8,0},{12,4},{16,24},{20,28},{24,16},{28,20},{1,9},{5... | collective-permute-start | bytes 98312 | tf_op jit(solution)/shard_map/ppermute | solution.py:77
  36.3 0.0 collective-permute-done.8
  36.3 0.1 collective-permute-start.9
  36.4 2.8 %collective-permute-done.17 = f32[64,128]{1,0:T(8,128)S(1)} collective-permute-done((f32[64,128]{1,0:T(8,128)S(1)}, f32[64,128]{1,0:T(8,128)S(1)}, u32[]{:S(2)}, u32[]{:S(2)}) %collective-permute-start.17) | collective-permute-done | bytes 32800 | tf_op jit(solution)/shard_map/ppermute | solution.py:77
  39.1 0.5 %collective-permute-start.18 = (f32[64,128]{1,0:T(8,128)S(1)}, f32[64,128]{1,0:T(8,128)S(1)}, u32[]{:S(2)}, u32[]{:S(2)}) collective-permute-start(f32[64,128]{1,0:T(8,128)S(1)} %add.51), channel_id=1, source_target_pairs={{0,2},{1,3},{2,0},{3,1},{4,6},{5,7},{6,4},{7,5},{8,10},{9,11},{10,... | collective-permute-start | bytes 98312 | tf_op jit(solution)/shard_map/ppermute | solution.py:77
  39.6 0.0 collective-permute-done.15
  39.7 0.0 collective-permute-start.16
  39.7 0.0 collective-permute-done.6
  39.7 0.0 copy-start.7
  39.7 0.6 %collective-permute-start.7 = (f32[256,128]{1,0:T(8,128)S(1)}, f32[256,128]{1,0:T(8,128)S(1)}, u32[]{:S(2)}, u32[]{:S(2)}) collective-permute-start(f32[256,128]{1,0:T(8,128)S(1)} %add.45.own_ref), channel_id=1, source_target_pairs={{0,1},{1,0},{2,3},{3,2},{4,5},{5,4},{6,7},{7,6},{8,9},{9,8},{10,11... | collective-permute-start | bytes 393224 | tf_op jit(solution)/shard_map/ppermute | solution.py:77
  40.3 2.8 %collective-permute-done.18 = f32[64,128]{1,0:T(8,128)S(1)} collective-permute-done((f32[64,128]{1,0:T(8,128)S(1)}, f32[64,128]{1,0:T(8,128)S(1)}, u32[]{:S(2)}, u32[]{:S(2)}) %collective-permute-start.18) | collective-permute-done | bytes 32800 | tf_op jit(solution)/shard_map/ppermute | solution.py:77
  43.1 0.0 collective-permute-start.19
  43.1 0.0 copy-done.7
  43.1 2.2 %coarse.1.coarse_ref = f32[512,256]{1,0:T(8,128)S(1)} custom-call(f32[4,128]{1,0:T(4,128)S(1)} %bitcast.14, f32[512,128]{1,0:T(8,128)S(1)} %copy-done.3, f32[3,512,128]{2,1,0:T(8,128)S(1)} %copy-done.1, f32[128,128]{1,0:T(8,128)S(1)} %bitcast.9, f32[128,128]{1,0:T(8,128)S(1)} %get-tuple-element.20.refs_1_, f32[128,128]{1,0:T(8,128)S(1)} %get-tuple-element.21.refs_0_.refs_2_, ...), custom_call_target="tpu_custom_call" | custom-call | flops 402653184 | bytes 1837056 | tf_op jit(solution)/shard_map/coarse/pallas_call | solution.py:64
  45.2 0.0 collective-permute-done.9.refs_5_
  45.3 0.0 collective-permute-done.7.other_ref
  45.3 2.1 %base.1.base_ref = f32[512,256]{1,0:T(8,128)S(1)} custom-call(f32[4,128]{1,0:T(4,128)S(1)} %bitcast.15, f32[512,256]{1,0:T(8,128)S(1)} %copy-done.4, f32[512,128]{1,0:T(8,128)S(1)} %copy-done.3, f32[3,512,128]{2,1,0:T(8,128)S(1)} %copy-done.1, f32[256,128]{1,0:T(8,128)S(1)} %add.45.own_ref, f32[256,128]{1,0:T(8,128)S(1)} %collective-permute-done.7.other_ref, ...), custom_call_target="tpu_custom_call" | custom-call | flops 301989888 | bytes 2557952 | tf_op jit(solution)/shard_map/base/pallas_call | solution.py:64
  47.4 0.0 collective-permute-done.16.refs_1_
  47.4 0.0 collective-permute-done.19.refs_3_
  47.4 1.2 %last.1 = f32[512,256]{1,0:T(8,128)} custom-call(f32[512,256]{1,0:T(8,128)S(1)} %base.1.base_ref, f32[512,256]{1,0:T(8,128)S(1)} %coarse.1.coarse_ref, f32[128,128]{1,0:T(8,128)S(1)} %constant_dynamic-update-slice_fusion.2.refs_0_, f32[128,128]{1,0:T(8,128)S(1)} %collective-permute-done.16.refs_1_, f32[128,128]{1,0:T(8,128)S(1)} %pad_maximum_fusion.refs_2_, ...), custom_call_target="tpu_custom_call" | custom-call | flops 201326592 | bytes 1310720 | tf_op jit(solution)/shard_map/last/pallas_call | solution.py:64
  (24 shorter events, 0.3 us)
Async XLA Ops:
  0.0 1.1 %copy-start = (f32[3,512,128]{2,1,0:T(8,128)S(1)}, f32[3,512,128]{2,1,0:T(8,128)}, u32[]{:S(2)}) copy-start(f32[3,512,128]{2,1,0:T(8,128)} %level_ref.7) | copy-start | bytes 2359300
  1.1 0.9 %copy-start.2 = (f32[512,128]{1,0:T(8,128)S(1)}, f32[512,128]{1,0:T(8,128)}, u32[]{:S(2)}) copy-start(f32[512,128]{1,0:T(8,128)} %leaf_ref.7) | copy-start | bytes 786436
  2.1 0.7 %copy-start.6 = (f32[512]{0:T(512)S(1)}, f32[512]{0:T(512)}, u32[]{:S(2)}) copy-start(f32[512]{0:T(512)} %param.7) | copy-start | bytes 6148
  2.8 5.7 %copy-start.4 = (f32[512,256]{1,0:T(8,128)S(1)}, f32[512,256]{1,0:T(8,128)}, u32[]{:S(2)}) copy-start(f32[512,256]{1,0:T(8,128)} %queries_ref.5) | copy-start | bytes 1572868
  3.7 4.8 %copy-start.1 = (f32[3,512,128]{2,1,0:T(8,128)S(1)}, f32[3,512,128]{2,1,0:T(8,128)}, u32[]{:S(2)}) copy-start(f32[3,512,128]{2,1,0:T(8,128)} %level_ref.7) | copy-start | bytes 2359300
  3.8 4.7 %copy-start.3 = (f32[512,128]{1,0:T(8,128)S(1)}, f32[512,128]{1,0:T(8,128)}, u32[]{:S(2)}) copy-start(f32[512,128]{1,0:T(8,128)} %leaf_ref.7) | copy-start | bytes 786436
  3.8 1.7 %collective-permute-start.2 = (f32[64,1024]{1,0:T(8,128)S(1)}, f32[64,1024]{1,0:T(8,128)S(1)}, u32[]{:S(2)}, u32[]{:S(2)}) collective-permute-start(f32[64,1024]{1,0:T(8,128)S(1)} %slice.53), channel_id=1, source_target_pairs={{0,1},{1,0},{2,3},{3,2},{4,5},{5,4},{6,7},{7,6},{8,9},{9,8},{10,11... | collective-permute-start | bytes 786440 | tf_op jit(solution)/shard_map/ppermute | solution.py:77
  5.5 9.5 %collective-permute-start.3 = (f32[64,1024]{1,0:T(8,128)S(1)}, f32[64,1024]{1,0:T(8,128)S(1)}, u32[]{:S(2)}, u32[]{:S(2)}) collective-permute-start(f32[64,1024]{1,0:T(8,128)S(1)} %slice_add_fusion), channel_id=1, source_target_pairs={{0,2},{1,3},{2,0},{3,1},{4,6},{5,7},{6,4},{7,5},{8,10},{9,11},{10,... | collective-permute-start | bytes 786440 | tf_op jit(solution)/shard_map/ppermute | solution.py:77
  9.3 7.7 %collective-permute-start = (f32[128,512]{1,0:T(8,128)S(1)}, f32[128,512]{1,0:T(8,128)S(1)}, u32[]{:S(2)}, u32[]{:S(2)}) collective-permute-start(f32[128,512]{1,0:T(8,128)S(1)} %slice.49), channel_id=1, source_target_pairs={{0,1},{1,0},{2,3},{3,2},{4,5},{5,4},{6,7},{7,6},{8,9},{9,8},{10,11... | collective-permute-start | bytes 786440 | tf_op jit(solution)/shard_map/ppermute | solution.py:77
  10.1 16.1 %collective-permute-start.5 = (f32[256,128]{1,0:T(8,128)S(1)}, f32[256,128]{1,0:T(8,128)S(1)}, u32[]{:S(2)}, u32[]{:S(2)}) collective-permute-start(f32[256,128]{1,0:T(8,128)S(1)} %get-tuple-element.22), channel_id=1, source_target_pairs={{0,1},{1,0},{2,3},{3,2},{4,5},{5,4},{6,7},{7,6},{8,9},{9,8},{10,11... | collective-permute-start | bytes 393224 | tf_op jit(solution)/shard_map/ppermute | solution.py:77
  15.1 4.7 %collective-permute-start.10 = (f32[64,384]{1,0:T(8,128)S(1)}, f32[64,384]{1,0:T(8,128)S(1)}, u32[]{:S(2)}, u32[]{:S(2)}) collective-permute-start(f32[64,384]{1,0:T(8,128)S(1)} %slice.57), channel_id=1, source_target_pairs={{0,4},{4,0},{8,12},{12,8},{16,20},{20,16},{24,28},{28,24},{1,5},{5... | collective-permute-start | bytes 294920 | tf_op jit(solution)/shard_map/ppermute | solution.py:77
  19.8 4.1 %collective-permute-start.12 = (f32[64,128]{1,0:T(8,128)S(1)}, f32[64,128]{1,0:T(8,128)S(1)}, u32[]{:S(2)}, u32[]{:S(2)}) collective-permute-start(f32[64,128]{1,0:T(8,128)S(1)} %slice.59), channel_id=1, source_target_pairs={{0,8},{4,12},{8,0},{12,4},{16,24},{20,28},{24,16},{28,20},{1,9},{5... | collective-permute-start | bytes 98312 | tf_op jit(solution)/shard_map/ppermute | solution.py:77
  21.7 5.0 %collective-permute-start.1 = (f32[64,512]{1,0:T(8,128)S(1)}, f32[64,512]{1,0:T(8,128)S(1)}, u32[]{:S(2)}, u32[]{:S(2)}) collective-permute-start(f32[64,512]{1,0:T(8,128)S(1)} %get-tuple-element.24), channel_id=1, source_target_pairs={{0,2},{1,3},{2,0},{3,1},{4,6},{5,7},{6,4},{7,5},{8,10},{9,11},{10,... | collective-permute-start | bytes 393224 | tf_op jit(solution)/shard_map/ppermute | solution.py:77
  23.3 2.0 %collective-permute-start.4 = (f32[64,640]{1,0:T(8,128)S(1)}, f32[64,640]{1,0:T(8,128)S(1)}, u32[]{:S(2)}, u32[]{:S(2)}) collective-permute-start(f32[64,640]{1,0:T(8,128)S(1)} %slice.54.own_ref), channel_id=1, source_target_pairs={{0,1},{1,0},{2,3},{3,2},{4,5},{5,4},{6,7},{7,6},{8,9},{9,8},{10,11... | collective-permute-start | bytes 491528 | tf_op jit(solution)/shard_map/ppermute | solution.py:77
  23.4 1.6 %collective-permute-start.11 = (f32[64,256]{1,0:T(8,128)S(1)}, f32[64,256]{1,0:T(8,128)S(1)}, u32[]{:S(2)}, u32[]{:S(2)}) collective-permute-start(f32[64,256]{1,0:T(8,128)S(1)} %slice.58.own_ref), channel_id=1, source_target_pairs={{0,1},{1,0},{2,3},{3,2},{4,5},{5,4},{6,7},{7,6},{8,9},{9,8},{10,11... | collective-permute-start | bytes 196616 | tf_op jit(solution)/shard_map/ppermute | solution.py:77
  23.9 6.8 %collective-permute-start.13 = (f32[64,128]{1,0:T(8,128)S(1)}, f32[64,128]{1,0:T(8,128)S(1)}, u32[]{:S(2)}, u32[]{:S(2)}) collective-permute-start(f32[64,128]{1,0:T(8,128)S(1)} %slice_add_fusion.2.own_ref), channel_id=1, source_target_pairs={{0,1},{1,0},{2,3},{3,2},{4,5},{5,4},{6,7},{7,6},{8,9},{9,8},{10,11... | collective-permute-start | bytes 98312 | tf_op jit(solution)/shard_map/ppermute | solution.py:77
  25.0 0.8 %copy-start.5 = (f32[1,128,128]{2,1,0:T(8,128)S(1)}, f32[1,128,128]{2,1,0:T(8,128)}, u32[]{:S(2)}) copy-start(f32[1,128,128]{2,1,0:T(8,128)} %param.9) | copy-start | bytes 196612
  27.1 12.5 %collective-permute-start.6 = (f32[256,128]{1,0:T(8,128)S(1)}, f32[256,128]{1,0:T(8,128)S(1)}, u32[]{:S(2)}, u32[]{:S(2)}) collective-permute-start(f32[256,128]{1,0:T(8,128)S(1)} %get-tuple-element.14), channel_id=1, source_target_pairs={{0,2},{1,3},{2,0},{3,1},{4,6},{5,7},{6,4},{7,5},{8,10},{9,11},{10,... | collective-permute-start | bytes 393224 | tf_op jit(solution)/shard_map/ppermute | solution.py:77
  28.7 7.6 %collective-permute-start.8 = (f32[64,256]{1,0:T(8,128)S(1)}, f32[64,256]{1,0:T(8,128)S(1)}, u32[]{:S(2)}, u32[]{:S(2)}) collective-permute-start(f32[64,256]{1,0:T(8,128)S(1)} %get-tuple-element.15), channel_id=1, source_target_pairs={{0,2},{1,3},{2,0},{3,1},{4,6},{5,7},{6,4},{7,5},{8,10},{9,11},{10,... | collective-permute-start | bytes 196616 | tf_op jit(solution)/shard_map/ppermute | solution.py:77
  29.2 4.3 %collective-permute-start.14 = (f32[64,256]{1,0:T(8,128)S(1)}, f32[64,256]{1,0:T(8,128)S(1)}, u32[]{:S(2)}, u32[]{:S(2)}) collective-permute-start(f32[64,256]{1,0:T(8,128)S(1)} %get-tuple-element.16.refs_0_), channel_id=1, source_target_pairs={{0,4},{4,0},{8,12},{12,8},{16,20},{20,16},{24,28},{28,24},{1,5},{5... | collective-permute-start | bytes 196616 | tf_op jit(solution)/shard_map/ppermute | solution.py:77
  33.6 6.0 %collective-permute-start.15 = (f32[64,128]{1,0:T(8,128)S(1)}, f32[64,128]{1,0:T(8,128)S(1)}, u32[]{:S(2)}, u32[]{:S(2)}) collective-permute-start(f32[64,128]{1,0:T(8,128)S(1)} %get-tuple-element.17), channel_id=1, source_target_pairs={{0,2},{1,3},{2,0},{3,1},{4,6},{5,7},{6,4},{7,5},{8,10},{9,11},{10,... | collective-permute-start | bytes 98312 | tf_op jit(solution)/shard_map/ppermute | solution.py:77
  35.2 3.9 %collective-permute-start.17 = (f32[64,128]{1,0:T(8,128)S(1)}, f32[64,128]{1,0:T(8,128)S(1)}, u32[]{:S(2)}, u32[]{:S(2)}) collective-permute-start(f32[64,128]{1,0:T(8,128)S(1)} %get-tuple-element.18), channel_id=1, source_target_pairs={{0,8},{4,12},{8,0},{12,4},{16,24},{20,28},{24,16},{28,20},{1,9},{5... | collective-permute-start | bytes 98312 | tf_op jit(solution)/shard_map/ppermute | solution.py:77
  36.3 9.0 %collective-permute-start.9 = (f32[128,256]{1,0:T(8,128)S(1)}, f32[128,256]{1,0:T(8,128)S(1)}, u32[]{:S(2)}, u32[]{:S(2)}) collective-permute-start(f32[128,256]{1,0:T(8,128)S(1)} %constant_dynamic-update-slice_fusion.refs_4_), channel_id=1, source_target_pairs={{0,1},{1,0},{2,3},{3,2},{4,5},{5,4},{6,7},{7,6},{8,9},{9,8},{10,11... | collective-permute-start | bytes 393224 | tf_op jit(solution)/shard_map/ppermute | solution.py:77
  39.1 3.9 %collective-permute-start.18 = (f32[64,128]{1,0:T(8,128)S(1)}, f32[64,128]{1,0:T(8,128)S(1)}, u32[]{:S(2)}, u32[]{:S(2)}) collective-permute-start(f32[64,128]{1,0:T(8,128)S(1)} %add.51), channel_id=1, source_target_pairs={{0,2},{1,3},{2,0},{3,1},{4,6},{5,7},{6,4},{7,5},{8,10},{9,11},{10,... | collective-permute-start | bytes 98312 | tf_op jit(solution)/shard_map/ppermute | solution.py:77
  39.7 7.7 %collective-permute-start.16 = (f32[128,128]{1,0:T(8,128)S(1)}, f32[128,128]{1,0:T(8,128)S(1)}, u32[]{:S(2)}, u32[]{:S(2)}) collective-permute-start(f32[128,128]{1,0:T(8,128)S(1)} %constant_dynamic-update-slice_fusion.2.refs_0_), channel_id=1, source_target_pairs={{0,1},{1,0},{2,3},{3,2},{4,5},{5,4},{6,7},{7,6},{8,9},{9,8},{10,11... | collective-permute-start | bytes 196616 | tf_op jit(solution)/shard_map/ppermute | solution.py:77
  39.7 3.4 %copy-start.7 = (f32[512]{0:T(512)S(1)}, f32[512]{0:T(512)}, u32[]{:S(2)}) copy-start(f32[512]{0:T(512)} %param.7) | copy-start | bytes 6148
  39.7 5.6 %collective-permute-start.7 = (f32[256,128]{1,0:T(8,128)S(1)}, f32[256,128]{1,0:T(8,128)S(1)}, u32[]{:S(2)}, u32[]{:S(2)}) collective-permute-start(f32[256,128]{1,0:T(8,128)S(1)} %add.45.own_ref), channel_id=1, source_target_pairs={{0,1},{1,0},{2,3},{3,2},{4,5},{5,4},{6,7},{7,6},{8,9},{9,8},{10,11... | collective-permute-start | bytes 393224 | tf_op jit(solution)/shard_map/ppermute | solution.py:77
  43.1 4.3 %collective-permute-start.19 = (f32[128,128]{1,0:T(8,128)S(1)}, f32[128,128]{1,0:T(8,128)S(1)}, u32[]{:S(2)}, u32[]{:S(2)}) collective-permute-start(f32[128,128]{1,0:T(8,128)S(1)} %pad_maximum_fusion.refs_2_), channel_id=1, source_target_pairs={{0,1},{1,0},{2,3},{3,2},{4,5},{5,4},{6,7},{7,6},{8,9},{9,8},{10,11... | collective-permute-start | bytes 196616 | tf_op jit(solution)/shard_map/ppermute | solution.py:77

commit v4 on v3

--- a/solution.py
+++ b/solution.py
@@ -57,7 +57,7 @@
     return pl.ds(pl.multiple_of(index * size, 8), size)
 
 
-def call(body, out_shapes, *operands, name, flops, spaces=None, scratch=()):
+def call(body, out_shapes, *operands, flops, spaces=None, scratch=()):
     spaces = spaces or [pltpu.VMEM] * len(operands)
     size = sum(4 * a.size for a in operands)
     outs = [jax.ShapeDtypeStruct(shape, FLOAT) for shape in out_shapes]
@@ -67,7 +67,6 @@
         in_specs=[pl.BlockSpec(memory_space=space) for space in spaces],
         out_specs=[pl.BlockSpec(memory_space=pltpu.VMEM)] * len(outs),
         scratch_shapes=list(scratch),
-        name=name,
         compiler_params=pltpu.CompilerParams(vmem_limit_bytes=VMEM_LIMIT),
         cost_estimate=pl.CostEstimate(flops=flops, bytes_accessed=size, transcendentals=0),
     )(*operands)
@@ -75,6 +74,13 @@
 
 def swap(array, axis, bit):
     return lax.ppermute(array, axis, [(i, i ^ 1 << bit) for i in range(lax.axis_size(axis))])
+
+
+def swap_both(array, row_bit, sub_bit):
+    sub = lax.axis_size("sub")
+    mask = (1 << row_bit) * sub + (1 << sub_bit)
+    pairs = [(i, i ^ mask) for i in range(lax.axis_size("rows") * sub)]
+    return lax.ppermute(array, ("rows", "sub"), pairs)
 
 
 def partial_sums(array, axis, bits):
@@ -146,7 +152,6 @@
         scale,
         leaf_basis,
         level_basis,
-        name="gram",
         flops=small * sum(map(len, blocks)) * rows_here // rank,
         spaces=[pltpu.HBM] * 3,
         scratch=[
@@ -157,7 +162,8 @@
         ],
     )
     gram_chip = gram[:half] + swap(gram[half:], "sub", 0)
-    gram_leaf = add_all(partial_sums(gram_chip, "sub", leaf_bits))
+    tail_leaf = add_all(partial_sums(gram_chip[:, starts[head] :], "sub", leaf_bits))
+    head_leaf = add_all(partial_sums(gram_chip[:, : starts[head]], "sub", leaf_bits))
 
     def moment_body(scale_ref, queries_ref, leaf_ref, level_ref, out_ref):
         spread = column_scale(scale_ref[...])
@@ -174,7 +180,6 @@
         queries,
         leaf_basis,
         level_basis,
-        name="moment",
         flops=small * count * 2 * rows_here // rank,
     )
     size = columns
@@ -208,7 +213,6 @@
         queries,
         leaf_basis,
         level_basis,
-        name="late",
         flops=small * (2 + head) * rows_here // rank,
     )
     late_keep, late_got = late[:late_rows], swap(late[late_rows:], "sub", 0)
@@ -231,38 +235,37 @@
             own,
             swap(own, "sub", 0),
             *[cores[e] for e in group],
-            name=f"product{group[0]}",
             flops=small * sum(len(blocks[e]) for e in group),
             scratch=[pltpu.VMEM((rank, own.shape[1]), FLOAT)],
         )
 
-    factors = products(list(range(head)), gram_leaf[:, : starts[head]])
-    remaining = gram_leaf[:, starts[head] :]
+    factors = products(list(range(head)), head_leaf)
+    remaining, sums = tail_leaf, []
     for e in range(head, count):
         remaining = add_all(partial_sums(remaining, "rows", bits[e]))
         size = starts[e + 1] - starts[e]
-        factors += products([e], remaining[:, :size])
+        sums.append(remaining[:, :size])
         remaining = remaining[:, size:]
+    factors += products(list(range(head, count)), lanes(sums))
 
     def head_body(*refs):
-        part_refs, factor_refs = refs[: len(moment_parts)], refs[len(moment_parts) : -5]
-        keep_ref, got_ref, own_ref, rest_ref, late_ref = refs[-5:]
+        part_refs, factor_refs = refs[: len(moment_parts)], refs[len(moment_parts) : -4]
+        keep_ref, got_ref, rest_ref, late_ref = refs[-4:]
         rest = add_all([part[...] for part in part_refs])
         for e in range(head):
             own, rest = rest[:, :rank], rest[:, rank:]
-            own_ref[:, e * rank : (e + 1) * rank] = own
+            late_ref[late_rows + e * mine : late_rows + (e + 1) * mine, :] = own
             rest = rest - dot(own, factor_refs[e][...])
         rest_ref[...] = rest
-        late_ref[...] = keep_ref[...] + got_ref[...]
-
-    head_moments, rest, late_chip = call(
+        late_ref[:late_rows] = keep_ref[...] + got_ref[...]
+
+    rest, late = call(
         head_body,
-        [(mine, head * rank), (mine, (count - head) * rank), (late_rows, rank)],
+        [(mine, (count - head) * rank), (late_rows + head * mine, rank)],
         *moment_parts,
         *factors[:head],
         late_keep,
         late_got,
-        name="head",
         flops=small * sum(map(len, blocks[:head])),
     )
 
@@ -272,23 +275,21 @@
         own_ref[...] = total[:, :rank]
         rest_ref[...] = total[:, rank:] - dot(total[:, :rank], factor_ref[:, rank:])
 
-    def gather(own):
-        for bit in reversed(range(1, sub_bits)):
-            own = jnp.concatenate([own, swap(own, "sub", bit)], axis=0)
-        return [own, swap(own, "sub", 0)]
-
-    def scatter(parts, stack_ref, where):
+    def scatter(parts, number, stack_ref):
         own, slot = own_block(), 0
         for part in parts:
-            for i in range(part.shape[0] // mine):
-                stack_ref[at(slot ^ own, mine), where] = part[i * mine : (i + 1) * mine, :]
+            for i in range(part.shape[0] // (number * mine)):
+                for e in range(number):
+                    start = (i * number + e) * mine
+                    stack_ref[at(slot ^ own, mine), e * rank : (e + 1) * rank] = part[start : start + mine, :]
                 slot += 1
 
-    late_leaf = add_all(partial_sums(late_chip, "sub", leaf_bits))
-    late_other = swap(late_leaf, "sub", 0)
-    head_parts = gather(head_moments)
-
-    coarse_parts = []
+    for bit in reversed(leaf_bits):
+        got = swap(late, "sub", bit)
+        late = jnp.concatenate([late[:late_rows] + got[:late_rows], late[late_rows:], got[late_rows:]], axis=0)
+    late_parts = [late, swap(late, "sub", 0)]
+
+    coarse = []
     for e in range(head, top):
         parts = partial_sums(rest, "rows", bits[e])
         own, rest = call(
@@ -296,11 +297,23 @@
             [(mine, rank), (mine, (top - e) * rank)],
             *parts,
             factors[e],
-            name=f"step{e}",
             flops=small * (top - e),
         )
-        coarse_parts.append(gather(own))
-    coarse_parts.append(gather(add_all(partial_sums(rest, "rows", bits[top]))))
+        coarse.append(own)
+    coarse.append(rest)
+    if len(bits[top]) == 1 and len(leaf_bits) == 1:
+        row_bit, sub_bit = bits[top][0], leaf_bits[0]
+        across = swap(rest, "rows", row_bit)
+        beside = swap(jnp.concatenate(coarse, axis=0), "sub", sub_bit)
+        corner = swap_both(rest, row_bit, sub_bit)
+        end = (count - head - 1) * mine
+        coarse = jnp.concatenate([*coarse[:-1], rest + across, beside[:end], beside[end:] + corner], axis=0)
+    else:
+        coarse[-1] = add_all(partial_sums(rest, "rows", bits[top]))
+        coarse = jnp.concatenate(coarse, axis=0)
+        for bit in reversed(leaf_bits):
+            coarse = jnp.concatenate([coarse, swap(coarse, "sub", bit)], axis=0)
+    coarse_parts = [coarse, swap(coarse, "sub", 0)]
 
     def response(e, spread, leaf_ref, level_ref, core_refs, factor_refs, diagonal):
         core = core_refs[e][...]
@@ -317,7 +330,7 @@
             right = [gains[f] for f in range(1, e + 1)] + [gains[0]]
         return dot(lanes(left), jnp.concatenate(right, axis=0))
 
-    def coarse_body(scale_ref, leaf_ref, level_ref, *refs):
+    def answer_body(scale_ref, leaf_ref, level_ref, *refs):
         core_refs, factor_refs, out_ref = refs[:count], refs[count:-1], refs[-1]
         spread = column_scale(scale_ref[...])
         for e in range(head, count):
@@ -325,23 +338,22 @@
                 e, spread, leaf_ref, level_ref, core_refs, factor_refs, factor_refs[e][:, :rank]
             )
 
-    (coarse,) = call(
-        coarse_body,
+    (answer,) = call(
+        answer_body,
         [(rows_here, (count - head) * rank)],
         scale,
         leaf_basis,
         level_basis,
         *cores,
         *factors,
-        name="coarse",
         flops=small * (count - head) * count * rows_here // rank,
     )
 
     def base_body(scale_ref, queries_ref, leaf_ref, level_ref, own_ref, other_ref, *refs):
         core_refs, factor_refs = refs[:head], refs[head : 2 * head]
-        part_refs, out_ref, stack_ref, gram_ref = refs[2 * head : -3], refs[-3], refs[-2], refs[-1]
+        out_ref, stack_ref, gram_ref = refs[2 * head :]
         spread = column_scale(scale_ref[...])
-        scatter(part_refs, stack_ref, pl.ds(0, head * rank))
+        scatter([own_ref.at[late_rows:], other_ref.at[late_rows:]], head, stack_ref)
         side = core_side()
         for late_ref, place in ((own_ref, side), (other_ref, 1 - side)):
             stack_ref[at(place, columns // 2), head * rank :] = late_ref[: columns // 2]
@@ -365,31 +377,23 @@
         queries,
         leaf_basis,
         level_basis,
-        late_leaf,
-        late_other,
+        *late_parts,
         *cores[:head],
         *factors[:head],
-        *head_parts,
-        name="base",
         flops=small * 2 * (head + 1) * rows_here // rank,
         scratch=[pltpu.VMEM((columns, (head + 1) * rank), FLOAT), pltpu.VMEM((rank, head * rank), FLOAT)],
     )
 
-    def last_body(base_ref, coarse_ref, *refs):
-        part_refs, out_ref, stack_ref = refs[:-2], refs[-2], refs[-1]
-        at_part = 0
-        for e, parts in enumerate(coarse_parts):
-            scatter(part_refs[at_part : at_part + len(parts)], stack_ref, pl.ds(e * rank, rank))
-            at_part += len(parts)
-        out_ref[...] = base_ref[...] - dot(coarse_ref[...], stack_ref[...], 1)
+    def last_body(base_ref, answer_ref, own_ref, other_ref, out_ref, stack_ref):
+        scatter([own_ref, other_ref], count - head, stack_ref)
+        out_ref[...] = base_ref[...] - dot(answer_ref[...], stack_ref[...], 1)
 
     (out,) = call(
         last_body,
         [(rows_here, columns)],
         base,
-        coarse,
-        *[part for parts in coarse_parts for part in parts],
-        name="last",
+        answer,
+        *coarse_parts,
         flops=small * 2 * (count - head) * rows_here // rank,
         scratch=[pltpu.VMEM((columns, (count - head) * rank), FLOAT)],
     )
@@ -406,4 +410,5 @@
         P(),
     )
     out_specs = P(("rows", "sub"), None)
+
     return jax.shard_map(shards, mesh=mesh, in_specs=in_specs, out_specs=out_specs, check_vma=False)

time: 49 us -> 46.7 us (0.953)
  waiting for transfers between devices: 17.1 us -> 14.6 us
  local copies, waits for them, and re-layouts: 4.39 us -> 5.74 us
  starting transfers between devices: 17.4 us -> 16.6 us
    ppermute x20 -> x16, waiting for transfers between devices: 17.1 us -> 14.6 us  [swap(): lax.ppermute(array, axis, [(i, i ^ 1 << bit) for i in range(lax.axis_size...]
    ppermute x20 -> x16, starting transfers between devices: 17.4 us -> 15 us  [swap(): lax.ppermute(array, axis, [(i, i ^ 1 << bit) for i in range(lax.axis_size...]
    ppermute x0 -> x1, starting transfers between devices: none -> 1.6 us  [swap_both(): return lax.ppermute(array, ('rows', 'sub'), pairs)]
    slice x2, local copies, waits for them, and re-layouts: 0.04 us -> 0.74 us  [shards(): moment_parts = [value[:size], swap(value[size:], 'sub', bit)]]
    slice x1, local copies, waits for them, and re-layouts: 0.02 us -> 0.71 us  [shards(): gram_chip = gram[:half] + swap(gram[half:], 'sub', 0)]
    pallas_call x11 -> x10, Pallas kernels: 9.29 us -> 9.09 us  [call(): pl.pallas_call(body, out_shape=outs, in_specs=[pl.BlockSpec(memory_space=...]
    unnamed x18 -> x16, local copies, waits for them, and re-layouts: 3.35 us -> 3.3 us
  transfers between devices with their start and end apart: 20 -> 17, of which waited for: 7 -> 6; matrix products, arithmetic and copies ran while one was open for 2% -> 4% of each run, Pallas kernels for 15% -> 15%
where the time goes in v4:
time: 46.7 us; the launch traced here: 46.5 us
  starting transfers between devices  16.6 us (36%)
  waiting for transfers between devices  14.6 us (31%)
  Pallas kernels  9.09 us (19%)
  local copies, waits for them, and re-layouts  5.74 us (12%)
    ppermute x16, starting transfers between devices, swap(): lax.ppermute(array, axis, [(i, i ^ 1 << bit) for i in range(lax.axis_size...  15 us
    ppermute x16, waiting for transfers between devices, swap(): lax.ppermute(array, axis, [(i, i ^ 1 << bit) for i in range(lax.axis_size...  14.6 us
    pallas_call x10, Pallas kernels, call(): pl.pallas_call(body, out_shape=outs, in_specs=[pl.BlockSpec(memory_space=...  9.09 us
    unnamed x16, local copies, waits for them, and re-layouts  3.3 us
    ppermute x1, starting transfers between devices, swap_both(): return lax.ppermute(array, ('rows', 'sub'), pairs)  1.6 us
  transfers between devices with their start and end apart: 17, of which 6 were waited for; matrix products, arithmetic and copies ran while one was open for 4% of the time, Pallas kernels for 15%

profile of v4, /device:TPU:0, one launch (start us, length us, event | category | flops | bytes accessed | tf_op | source)
XLA Modules:
  0.0 46.5 jit_solution(11864776764742929508)
XLA Ops:
  0.0 0.0 copy-start
  0.0 1.1 %copy-done = f32[3,512,128]{2,1,0:T(8,128)S(1)} copy-done((f32[3,512,128]{2,1,0:T(8,128)S(1)}, f32[3,512,128]{2,1,0:T(8,128)}, u32[]{:S(2)}) %copy-start) | copy-done | bytes 786456
  1.1 0.0 copy-start.2
  1.1 0.9 %copy-done.2 = f32[512,128]{1,0:T(8,128)S(1)} copy-done((f32[512,128]{1,0:T(8,128)S(1)}, f32[512,128]{1,0:T(8,128)}, u32[]{:S(2)}) %copy-start.2) | copy-done | bytes 262168
  2.1 0.0 copy-start.6
  2.1 0.7 %copy-done.6 = f32[512]{0:T(512)S(1)} copy-done((f32[512]{0:T(512)S(1)}, f32[512]{0:T(512)}, u32[]{:S(2)}) %copy-start.6) | copy-done | bytes 2072
  2.8 0.0 copy-start.1
  2.8 0.0 copy-start.4
  2.8 0.9 %shard_map.65 = f32[128,1024]{1,0:T(8,128)S(1)} custom-call(f32[4,128]{1,0:T(4,128)S(1)} %bitcast.11, f32[512,128]{1,0:T(8,128)S(1)} %copy-done.2, f32[3,512,128]{2,1,0:T(8,128)S(1)} %copy-done), custom_call_target="tpu_custom_call" | custom-call | flops 402653184 | bytes 1050624 | tf_op jit(solution)/shard_map/pallas_call | solution.py:64
  3.7 0.0 copy-start.3
  3.7 0.7 %slice.77 = f32[64,1024]{1,0:T(8,128)} slice(f32[128,1024]{1,0:T(8,128)S(1)} %shard_map.65), slice={[64:128], [0:1024]} | slice | bytes 524288 | tf_op jit(solution)/shard_map/slice | solution.py:164
  4.4 0.5 %collective-permute-start.2 = (f32[64,1024]{1,0:T(8,128)}, f32[64,1024]{1,0:T(8,128)S(1)}, u32[]{:S(2)}, u32[]{:S(2)}) collective-permute-start(f32[64,1024]{1,0:T(8,128)} %slice.77), channel_id=1, source_target_pairs={{0,1},{1,0},{2,3},{3,2},{4,5},{5,4},{6,7},{7,6},{8,9},{9,8},{10,11... | collective-permute-start | bytes 786440 | tf_op jit(solution)/shard_map/ppermute | solution.py:76
  4.9 0.0 copy-done.1
  4.9 0.0 copy-done.4
  4.9 0.0 copy-done.3
  4.9 0.8 %shard_map.64 = f32[256,512]{1,0:T(8,128)S(1)} custom-call(f32[4,128]{1,0:T(4,128)S(1)} %bitcast.12, f32[512,256]{1,0:T(8,128)S(1)} %copy-done.4, f32[512,128]{1,0:T(8,128)S(1)} %copy-done.3, f32[3,512,128]{2,1,0:T(8,128)S(1)} %copy-done.1), custom_call_target="tpu_custom_call" | custom-call | flops 402653184 | bytes 1574912 | tf_op jit(solution)/shard_map/pallas_call | solution.py:64
  5.7 0.7 %slice.73 = f32[128,512]{1,0:T(8,128)} slice(f32[256,512]{1,0:T(8,128)S(1)} %shard_map.64), slice={[128:256], [0:512]} | slice | bytes 524288 | tf_op jit(solution)/shard_map/slice | solution.py:188
  6.4 0.4 collective-permute-start
  6.8 0.7 %shard_map.67 = f32[512,128]{1,0:T(8,128)S(1)} custom-call(f32[4,128]{1,0:T(4,128)S(1)} %bitcast.13, f32[512,256]{1,0:T(8,128)S(1)} %copy-done.4, f32[512,128]{1,0:T(8,128)S(1)} %copy-done.3, f32[3,512,128]{2,1,0:T(8,128)S(1)} %copy-done.1), custom_call_target="tpu_custom_call" | custom-call | flops 201326592 | bytes 1574912 | tf_op jit(solution)/shard_map/pallas_call | solution.py:64
  7.6 0.2 collective-permute-start.5
  7.8 0.0 collective-permute-done.2
  7.9 3.0 %collective-permute-start.3 = (f32[64,640]{1,0:T(8,128)S(1)}, f32[64,640]{1,0:T(8,128)S(1)}, u32[]{:S(2)}, u32[]{:S(2)}) collective-permute-start(f32[64,640]{1,0:T(8,128)S(1)} %slice.78), channel_id=1, source_target_pairs={{0,2},{1,3},{2,0},{3,1},{4,6},{5,7},{6,4},{7,5},{8,10},{9,11},{10,... | collective-permute-start | bytes 491528 | tf_op jit(solution)/shard_map/ppermute | solution.py:76
  10.8 0.1 collective-permute-start.8
  10.9 0.0 collective-permute-done
  10.9 6.4 %collective-permute-done.8 = f32[64,384]{1,0:T(8,128)S(1)} collective-permute-done((f32[64,384]{1,0:T(8,128)S(1)}, f32[64,384]{1,0:T(8,128)S(1)}, u32[]{:S(2)}, u32[]{:S(2)}) %collective-permute-start.8) | collective-permute-done | bytes 98336 | tf_op jit(solution)/shard_map/ppermute | solution.py:76
  17.4 1.8 %collective-permute-start.9 = (f32[64,384]{1,0:T(8,128)S(1)}, f32[64,384]{1,0:T(8,128)S(1)}, u32[]{:S(2)}, u32[]{:S(2)}) collective-permute-start(f32[64,384]{1,0:T(8,128)S(1)} %slice_add_fusion.5), channel_id=1, source_target_pairs={{0,4},{4,0},{8,12},{12,8},{16,20},{20,16},{24,28},{28,24},{1,5},{5... | collective-permute-start | bytes 294920 | tf_op jit(solution)/shard_map/ppermute | solution.py:76
  19.2 1.6 %collective-permute-start.1 = (f32[64,512]{1,0:T(8,128)S(1)}, f32[64,512]{1,0:T(8,128)S(1)}, u32[]{:S(2)}, u32[]{:S(2)}) collective-permute-start(f32[64,512]{1,0:T(8,128)S(1)} %get-tuple-element.26), channel_id=1, source_target_pairs={{0,2},{1,3},{2,0},{3,1},{4,6},{5,7},{6,4},{7,5},{8,10},{9,11},{10,... | collective-permute-start | bytes 393224 | tf_op jit(solution)/shard_map/ppermute | solution.py:76
  20.8 1.3 %collective-permute-done.9 = f32[64,384]{1,0:T(8,128)S(1)} collective-permute-done((f32[64,384]{1,0:T(8,128)S(1)}, f32[64,384]{1,0:T(8,128)S(1)}, u32[]{:S(2)}, u32[]{:S(2)}) %collective-permute-start.9) | collective-permute-done | bytes 98336 | tf_op jit(solution)/shard_map/ppermute | solution.py:76
  22.1 1.9 %collective-permute-start.10 = (f32[64,128]{1,0:T(8,128)S(1)}, f32[64,128]{1,0:T(8,128)S(1)}, u32[]{:S(2)}, u32[]{:S(2)}) collective-permute-start(f32[64,128]{1,0:T(8,128)S(1)} %slice.85), channel_id=1, source_target_pairs={{0,8},{4,12},{8,0},{12,4},{16,24},{20,28},{24,16},{28,20},{1,9},{5... | collective-permute-start | bytes 98312 | tf_op jit(solution)/shard_map/ppermute | solution.py:76
  24.0 0.0 collective-permute-done.3
  24.0 0.1 collective-permute-start.4
  24.1 2.0 %collective-permute-done.10 = f32[64,128]{1,0:T(8,128)S(1)} collective-permute-done((f32[64,128]{1,0:T(8,128)S(1)}, f32[64,128]{1,0:T(8,128)S(1)}, u32[]{:S(2)}, u32[]{:S(2)}) %collective-permute-start.10) | collective-permute-done | bytes 32800 | tf_op jit(solution)/shard_map/ppermute | solution.py:76
  26.1 0.0 copy-start.5
  26.1 0.1 collective-permute-start.11
  26.2 0.9 %dynamic-slice_bitcast_fusion = (f32[128,128]{1,0:T(8,128)S(1)}, f32[128,128]{1,0:T(8,128)S(1)}, f32[128,128]{1,0:T(8,128)S(1)}) fusion(f32[14,128,128]{2,1,0:T(8,128)} %param.11, s32[]{:T(128)S(6)} %select_n.23, s32[]{:T(128)S(6)} %select_n.19, s32[]{:T(128)S(6)} %select_n.21), kind=kLoop, calls=%fused_computation.7 | loop fusion | bytes 393228 | tf_op jit(solution)/shard_map/jit(dynamic_index_in_dim)/squeeze | solution.py:122
  27.1 0.0 collective-permute-done.4.other_ref
  27.1 0.0 copy-done.5
  27.2 0.4 shard_map.66
  27.5 0.0 collective-permute-done.5.refs_5_
  27.5 0.0 collective-permute-done.1.refs_1_
  27.5 0.4 shard_map.68
  27.9 1.8 %collective-permute-start.6 = (f32[384,128]{1,0:T(8,128)S(1)}, f32[384,128]{1,0:T(8,128)S(1)}, u32[]{:S(2)}, u32[]{:S(2)}) collective-permute-start(f32[384,128]{1,0:T(8,128)S(1)} %get-tuple-element.15), channel_id=1, source_target_pairs={{0,2},{1,3},{2,0},{3,1},{4,6},{5,7},{6,4},{7,5},{8,10},{9,11},{10,... | collective-permute-start | bytes 589832 | tf_op jit(solution)/shard_map/ppermute | solution.py:76
  29.7 1.5 %collective-permute-start.12 = (f32[64,256]{1,0:T(8,128)S(1)}, f32[64,256]{1,0:T(8,128)S(1)}, u32[]{:S(2)}, u32[]{:S(2)}) collective-permute-start(f32[64,256]{1,0:T(8,128)S(1)} %get-tuple-element.18.refs_0_), channel_id=1, source_target_pairs={{0,4},{4,0},{8,12},{12,8},{16,20},{20,16},{24,28},{28,24},{1,5},{5... | collective-permute-start | bytes 196616 | tf_op jit(solution)/shard_map/ppermute | solution.py:76
  31.2 0.0 collective-permute-done.11.other_ref
  31.2 0.3 shard_map.70
  31.5 2.4 %collective-permute-done.12.refs_1_ = f32[64,256]{1,0:T(8,128)S(1)} collective-permute-done((f32[64,256]{1,0:T(8,128)S(1)}, f32[64,256]{1,0:T(8,128)S(1)}, u32[]{:S(2)}, u32[]{:S(2)}) %collective-permute-start.12) | collective-permute-done | bytes 65568 | tf_op jit(solution)/shard_map/ppermute | solution.py:76
  34.0 0.1 shard_map.72
  34.1 1.6 %collective-permute-start.15 = (f32[64,128]{1,0:T(8,128)S(1)}, f32[64,128]{1,0:T(8,128)S(1)}, u32[]{:S(2)}, u32[]{:S(2)}) collective-permute-start(f32[64,128]{1,0:T(8,128)S(1)} %get-tuple-element.20), channel_id=1, source_target_pairs={{0,10},{1,11},{2,8},{3,9},{4,14},{5,15},{6,12},{7,13},{8,2},{9,3},... | collective-permute-start | bytes 98312 | tf_op jit(solution)/shard_map/ppermute | solution.py:83
  35.7 0.2 collective-permute-start.13
  36.0 1.7 %collective-permute-start.14 = (f32[128,128]{1,0:T(8,128)S(1)}, f32[128,128]{1,0:T(8,128)S(1)}, u32[]{:S(2)}, u32[]{:S(2)}) collective-permute-start(f32[128,128]{1,0:T(8,128)S(1)} %pad_maximum_fusion.3), channel_id=1, source_target_pairs={{0,2},{1,3},{2,0},{3,1},{4,6},{5,7},{6,4},{7,5},{8,10},{9,11},{10,... | collective-permute-start | bytes 196616 | tf_op jit(solution)/shard_map/ppermute | solution.py:76
  37.7 2.0 %collective-permute-done.13 = f32[64,128]{1,0:T(8,128)S(1)} collective-permute-done((f32[64,128]{1,0:T(8,128)S(1)}, f32[64,128]{1,0:T(8,128)S(1)}, u32[]{:S(2)}, u32[]{:S(2)}) %collective-permute-start.13) | collective-permute-done | bytes 32800 | tf_op jit(solution)/shard_map/ppermute | solution.py:76
  39.6 0.0 collective-permute-done.6
  39.7 0.1 collective-permute-start.7
  39.8 0.0 collective-permute-done.15
  39.8 0.4 collective-permute-done.14
  40.2 0.0 copy-start.7
  40.3 0.1 collective-permute-start.16
  40.4 0.5 %copy-done.7 = f32[512]{0:T(512)S(1)} copy-done((f32[512]{0:T(512)S(1)}, f32[512]{0:T(512)}, u32[]{:S(2)}) %copy-start.7) | copy-done | bytes 2072
  40.9 2.2 %shard_map.71.answer_ref = f32[512,256]{1,0:T(8,128)S(1)} custom-call(f32[4,128]{1,0:T(4,128)S(1)} %bitcast.14, f32[512,128]{1,0:T(8,128)S(1)} %copy-done.3, f32[3,512,128]{2,1,0:T(8,128)S(1)} %copy-done.1, f32[128,128]{1,0:T(8,128)S(1)} %bitcast.9, f32[128,128]{1,0:T(8,128)S(1)} %get-tuple-element.22.refs_1_, ...), custom_call_target="tpu_custom_call" | custom-call | flops 402653184 | bytes 1837056 | tf_op jit(solution)/shard_map/pallas_call | solution.py:64
  43.1 0.0 collective-permute-done.7.other_ref
  43.1 2.1 %shard_map.69.base_ref = f32[512,256]{1,0:T(8,128)S(1)} custom-call(f32[4,128]{1,0:T(4,128)S(1)} %bitcast.15, f32[512,256]{1,0:T(8,128)S(1)} %copy-done.4, f32[512,128]{1,0:T(8,128)S(1)} %copy-done.3, f32[3,512,128]{2,1,0:T(8,128)S(1)} %copy-done.1, f32[512,128]{1,0:T(8,128)S(1)} %pad_maximum_fusion.own_ref, ...), custom_call_target="tpu_custom_call" | custom-call | flops 301989888 | bytes 2557952 | tf_op jit(solution)/shard_map/pallas_call | solution.py:64
  45.2 0.0 collective-permute-done.16.other_ref
  45.2 1.2 %shard_map.73 = f32[512,256]{1,0:T(8,128)} custom-call(f32[512,256]{1,0:T(8,128)S(1)} %shard_map.69.base_ref, f32[512,256]{1,0:T(8,128)S(1)} %shard_map.71.answer_ref, f32[256,128]{1,0:T(8,128)S(1)} %pad_maximum_fusion.1.own_ref, f32[256,128]{1,0:T(8,128)S(1)} %collective-permute-done.16.other_ref), custom_call_target="tpu_custom_call" | custom-call | flops 201326592 | bytes 1310720 | tf_op jit(solution)/shard_map/pallas_call | solution.py:64
  (21 shorter events, 0.3 us)
Async XLA Ops:
  0.0 1.1 %copy-start = (f32[3,512,128]{2,1,0:T(8,128)S(1)}, f32[3,512,128]{2,1,0:T(8,128)}, u32[]{:S(2)}) copy-start(f32[3,512,128]{2,1,0:T(8,128)} %level_ref.7) | copy-start | bytes 2359300
  1.1 0.9 %copy-start.2 = (f32[512,128]{1,0:T(8,128)S(1)}, f32[512,128]{1,0:T(8,128)}, u32[]{:S(2)}) copy-start(f32[512,128]{1,0:T(8,128)} %leaf_ref.7) | copy-start | bytes 786436
  2.1 0.7 %copy-start.6 = (f32[512]{0:T(512)S(1)}, f32[512]{0:T(512)}, u32[]{:S(2)}) copy-start(f32[512]{0:T(512)} %param.7) | copy-start | bytes 6148
  2.8 2.2 %copy-start.1 = (f32[3,512,128]{2,1,0:T(8,128)S(1)}, f32[3,512,128]{2,1,0:T(8,128)}, u32[]{:S(2)}) copy-start(f32[3,512,128]{2,1,0:T(8,128)} %level_ref.7) | copy-start | bytes 2359300
  2.8 2.2 %copy-start.4 = (f32[512,256]{1,0:T(8,128)S(1)}, f32[512,256]{1,0:T(8,128)}, u32[]{:S(2)}) copy-start(f32[512,256]{1,0:T(8,128)} %queries_ref.5) | copy-start | bytes 1572868
  3.7 1.2 %copy-start.3 = (f32[512,128]{1,0:T(8,128)S(1)}, f32[512,128]{1,0:T(8,128)}, u32[]{:S(2)}) copy-start(f32[512,128]{1,0:T(8,128)} %leaf_ref.7) | copy-start | bytes 786436
  4.4 3.3 %collective-permute-start.2 = (f32[64,1024]{1,0:T(8,128)}, f32[64,1024]{1,0:T(8,128)S(1)}, u32[]{:S(2)}, u32[]{:S(2)}) collective-permute-start(f32[64,1024]{1,0:T(8,128)} %slice.77), channel_id=1, source_target_pairs={{0,1},{1,0},{2,3},{3,2},{4,5},{5,4},{6,7},{7,6},{8,9},{9,8},{10,11... | collective-permute-start | bytes 786440 | tf_op jit(solution)/shard_map/ppermute | solution.py:76
  6.4 4.5 %collective-permute-start = (f32[128,512]{1,0:T(8,128)}, f32[128,512]{1,0:T(8,128)S(1)}, u32[]{:S(2)}, u32[]{:S(2)}) collective-permute-start(f32[128,512]{1,0:T(8,128)} %slice.73), channel_id=1, source_target_pairs={{0,1},{1,0},{2,3},{3,2},{4,5},{5,4},{6,7},{7,6},{8,9},{9,8},{10,11... | collective-permute-start | bytes 786440 | tf_op jit(solution)/shard_map/ppermute | solution.py:76
  7.6 19.9 %collective-permute-start.5 = (f32[256,128]{1,0:T(8,128)S(1)}, f32[256,128]{1,0:T(8,128)S(1)}, u32[]{:S(2)}, u32[]{:S(2)}) collective-permute-start(f32[256,128]{1,0:T(8,128)S(1)} %get-tuple-element.24), channel_id=1, source_target_pairs={{0,1},{1,0},{2,3},{3,2},{4,5},{5,4},{6,7},{7,6},{8,9},{9,8},{10,11... | collective-permute-start | bytes 393224 | tf_op jit(solution)/shard_map/ppermute | solution.py:76
  7.9 16.1 %collective-permute-start.3 = (f32[64,640]{1,0:T(8,128)S(1)}, f32[64,640]{1,0:T(8,128)S(1)}, u32[]{:S(2)}, u32[]{:S(2)}) collective-permute-start(f32[64,640]{1,0:T(8,128)S(1)} %slice.78), channel_id=1, source_target_pairs={{0,2},{1,3},{2,0},{3,1},{4,6},{5,7},{6,4},{7,5},{8,10},{9,11},{10,... | collective-permute-start | bytes 491528 | tf_op jit(solution)/shard_map/ppermute | solution.py:76
  10.8 6.6 %collective-permute-start.8 = (f32[64,384]{1,0:T(8,128)S(1)}, f32[64,384]{1,0:T(8,128)S(1)}, u32[]{:S(2)}, u32[]{:S(2)}) collective-permute-start(f32[64,384]{1,0:T(8,128)S(1)} %slice.83), channel_id=1, source_target_pairs={{0,2},{1,3},{2,0},{3,1},{4,6},{5,7},{6,4},{7,5},{8,10},{9,11},{10,... | collective-permute-start | bytes 294920 | tf_op jit(solution)/shard_map/ppermute | solution.py:76
  17.4 4.7 %collective-permute-start.9 = (f32[64,384]{1,0:T(8,128)S(1)}, f32[64,384]{1,0:T(8,128)S(1)}, u32[]{:S(2)}, u32[]{:S(2)}) collective-permute-start(f32[64,384]{1,0:T(8,128)S(1)} %slice_add_fusion.5), channel_id=1, source_target_pairs={{0,4},{4,0},{8,12},{12,8},{16,20},{20,16},{24,28},{28,24},{1,5},{5... | collective-permute-start | bytes 294920 | tf_op jit(solution)/shard_map/ppermute | solution.py:76
  19.2 8.3 %collective-permute-start.1 = (f32[64,512]{1,0:T(8,128)S(1)}, f32[64,512]{1,0:T(8,128)S(1)}, u32[]{:S(2)}, u32[]{:S(2)}) collective-permute-start(f32[64,512]{1,0:T(8,128)S(1)} %get-tuple-element.26), channel_id=1, source_target_pairs={{0,2},{1,3},{2,0},{3,1},{4,6},{5,7},{6,4},{7,5},{8,10},{9,11},{10,... | collective-permute-start | bytes 393224 | tf_op jit(solution)/shard_map/ppermute | solution.py:76
  22.1 4.0 %collective-permute-start.10 = (f32[64,128]{1,0:T(8,128)S(1)}, f32[64,128]{1,0:T(8,128)S(1)}, u32[]{:S(2)}, u32[]{:S(2)}) collective-permute-start(f32[64,128]{1,0:T(8,128)S(1)} %slice.85), channel_id=1, source_target_pairs={{0,8},{4,12},{8,0},{12,4},{16,24},{20,28},{24,16},{28,20},{1,9},{5... | collective-permute-start | bytes 98312 | tf_op jit(solution)/shard_map/ppermute | solution.py:76
  24.0 3.1 %collective-permute-start.4 = (f32[64,640]{1,0:T(8,128)S(1)}, f32[64,640]{1,0:T(8,128)S(1)}, u32[]{:S(2)}, u32[]{:S(2)}) collective-permute-start(f32[64,640]{1,0:T(8,128)S(1)} %slice_add_fusion.6.own_ref), channel_id=1, source_target_pairs={{0,1},{1,0},{2,3},{3,2},{4,5},{5,4},{6,7},{7,6},{8,9},{9,8},{10,11... | collective-permute-start | bytes 491528 | tf_op jit(solution)/shard_map/ppermute | solution.py:76
  26.1 1.0 %copy-start.5 = (f32[1,128,128]{2,1,0:T(8,128)S(1)}, f32[1,128,128]{2,1,0:T(8,128)}, u32[]{:S(2)}) copy-start(f32[1,128,128]{2,1,0:T(8,128)} %param.9) | copy-start | bytes 196612
  26.1 5.1 %collective-permute-start.11 = (f32[64,384]{1,0:T(8,128)S(1)}, f32[64,384]{1,0:T(8,128)S(1)}, u32[]{:S(2)}, u32[]{:S(2)}) collective-permute-start(f32[64,384]{1,0:T(8,128)S(1)} %pad_maximum_fusion.2.own_ref), channel_id=1, source_target_pairs={{0,1},{1,0},{2,3},{3,2},{4,5},{5,4},{6,7},{7,6},{8,9},{9,8},{10,11... | collective-permute-start | bytes 294920 | tf_op jit(solution)/shard_map/ppermute | solution.py:76
  27.9 11.7 %collective-permute-start.6 = (f32[384,128]{1,0:T(8,128)S(1)}, f32[384,128]{1,0:T(8,128)S(1)}, u32[]{:S(2)}, u32[]{:S(2)}) collective-permute-start(f32[384,128]{1,0:T(8,128)S(1)} %get-tuple-element.15), channel_id=1, source_target_pairs={{0,2},{1,3},{2,0},{3,1},{4,6},{5,7},{6,4},{7,5},{8,10},{9,11},{10,... | collective-permute-start | bytes 589832 | tf_op jit(solution)/shard_map/ppermute | solution.py:76
  29.7 4.3 %collective-permute-start.12 = (f32[64,256]{1,0:T(8,128)S(1)}, f32[64,256]{1,0:T(8,128)S(1)}, u32[]{:S(2)}, u32[]{:S(2)}) collective-permute-start(f32[64,256]{1,0:T(8,128)S(1)} %get-tuple-element.18.refs_0_), channel_id=1, source_target_pairs={{0,4},{4,0},{8,12},{12,8},{16,20},{20,16},{24,28},{28,24},{1,5},{5... | collective-permute-start | bytes 196616 | tf_op jit(solution)/shard_map/ppermute | solution.py:76
  34.1 5.7 %collective-permute-start.15 = (f32[64,128]{1,0:T(8,128)S(1)}, f32[64,128]{1,0:T(8,128)S(1)}, u32[]{:S(2)}, u32[]{:S(2)}) collective-permute-start(f32[64,128]{1,0:T(8,128)S(1)} %get-tuple-element.20), channel_id=1, source_target_pairs={{0,10},{1,11},{2,8},{3,9},{4,14},{5,15},{6,12},{7,13},{8,2},{9,3},... | collective-permute-start | bytes 98312 | tf_op jit(solution)/shard_map/ppermute | solution.py:83
  35.7 3.9 %collective-permute-start.13 = (f32[64,128]{1,0:T(8,128)S(1)}, f32[64,128]{1,0:T(8,128)S(1)}, u32[]{:S(2)}, u32[]{:S(2)}) collective-permute-start(f32[64,128]{1,0:T(8,128)S(1)} %get-tuple-element.20), channel_id=1, source_target_pairs={{0,8},{4,12},{8,0},{12,4},{16,24},{20,28},{24,16},{28,20},{1,9},{5... | collective-permute-start | bytes 98312 | tf_op jit(solution)/shard_map/ppermute | solution.py:76
  36.0 4.3 %collective-permute-start.14 = (f32[128,128]{1,0:T(8,128)S(1)}, f32[128,128]{1,0:T(8,128)S(1)}, u32[]{:S(2)}, u32[]{:S(2)}) collective-permute-start(f32[128,128]{1,0:T(8,128)S(1)} %pad_maximum_fusion.3), channel_id=1, source_target_pairs={{0,2},{1,3},{2,0},{3,1},{4,6},{5,7},{6,4},{7,5},{8,10},{9,11},{10,... | collective-permute-start | bytes 196616 | tf_op jit(solution)/shard_map/ppermute | solution.py:76
  39.7 3.4 %collective-permute-start.7 = (f32[512,128]{1,0:T(8,128)S(1)}, f32[512,128]{1,0:T(8,128)S(1)}, u32[]{:S(2)}, u32[]{:S(2)}) collective-permute-start(f32[512,128]{1,0:T(8,128)S(1)} %pad_maximum_fusion.own_ref), channel_id=1, source_target_pairs={{0,1},{1,0},{2,3},{3,2},{4,5},{5,4},{6,7},{7,6},{8,9},{9,8},{10,11... | collective-permute-start | bytes 786440 | tf_op jit(solution)/shard_map/ppermute | solution.py:76
  40.2 0.7 %copy-start.7 = (f32[512]{0:T(512)S(1)}, f32[512]{0:T(512)}, u32[]{:S(2)}) copy-start(f32[512]{0:T(512)} %param.7) | copy-start | bytes 6148
  40.3 4.9 %collective-permute-start.16 = (f32[256,128]{1,0:T(8,128)S(1)}, f32[256,128]{1,0:T(8,128)S(1)}, u32[]{:S(2)}, u32[]{:S(2)}) collective-permute-start(f32[256,128]{1,0:T(8,128)S(1)} %pad_maximum_fusion.1.own_ref), channel_id=1, source_target_pairs={{0,1},{1,0},{2,3},{3,2},{4,5},{5,4},{6,7},{7,6},{8,9},{9,8},{10,11... | collective-permute-start | bytes 393224 | tf_op jit(solution)/shard_map/ppermute | solution.py:76

commit v5 on v4

v5 whole, which is shorter than its diff:
```python
import functools

import jax
import jax.numpy as jnp
from jax import lax
from jax.experimental import pallas as pl
from jax.experimental.pallas import tpu as pltpu
from jax.sharding import PartitionSpec as P


FLOAT = jnp.float32
VMEM_LIMIT = 16 << 20


def halves(value):
    high = value.astype(jnp.bfloat16)
    return high, (value - high.astype(FLOAT)).astype(jnp.bfloat16)


def dot_parts(left, right, right_dim=0):
    mult = functools.partial(
        lax.dot_general,
        dimension_numbers=(((1,), (right_dim,)), ((), ())),
        preferred_element_type=FLOAT,
    )
    return mult(left[0], right[0]) + (mult(left[0], right[1]) + mult(left[1], right[0]))


def dot(left, right, right_dim=0):
    return dot_parts(halves(left), halves(right), right_dim)


def lanes(values):
    return values[0] if len(values) == 1 else jnp.concatenate(values, axis=1)


def column_scale(scale):
    size = scale.shape[1]
    return jnp.concatenate(
        [jnp.broadcast_to(scale[i : i + 1, :], (size, size)).T for i in range(scale.shape[0])], axis=0
    )


def core_side():
    return lax.rem(lax.axis_index("sub"), 2)


def own_block():
    place, value = lax.axis_index("sub"), 0
    for _ in range(lax.axis_size("sub").bit_length() - 1):
        value = value * 2 + lax.rem(place, 2)
        place = place // 2
    return value


def at(index, size):
    return pl.ds(pl.multiple_of(index * size, 8), size)


def call(body, outs, *operands, flops, spaces=None, out_space=pltpu.VMEM, scratch=()):
    spaces = spaces or [pltpu.VMEM] * len(operands)
    size = sum(a.dtype.itemsize * a.size for a in operands)
    outs = [out if isinstance(out, jax.ShapeDtypeStruct) else jax.ShapeDtypeStruct(out, FLOAT) for out in outs]
    return pl.pallas_call(
        body,
        out_shape=outs,
        in_specs=[pl.BlockSpec(memory_space=space) for space in spaces],
        out_specs=[pl.BlockSpec(memory_space=out_space)] * len(outs),
        scratch_shapes=list(scratch),
        compiler_params=pltpu.CompilerParams(vmem_limit_bytes=VMEM_LIMIT),
        cost_estimate=pl.CostEstimate(flops=flops, bytes_accessed=size, transcendentals=0),
    )(*operands)


def pair(*shape):
    return [jax.ShapeDtypeStruct(shape, jnp.bfloat16)] * 2


def store(refs, value):
    for ref, part in zip(refs, halves(value)):
        ref[...] = part


def swap(array, axis, bit):
    return lax.ppermute(array, axis, [(i, i ^ 1 << bit) for i in range(lax.axis_size(axis))])


def swap_both(array, row_bit, sub_bit):
    sub = lax.axis_size("sub")
    mask = (1 << row_bit) * sub + (1 << sub_bit)
    pairs = [(i, i ^ mask) for i in range(lax.axis_size("rows") * sub)]
    return lax.ppermute(array, ("rows", "sub"), pairs)


def partial_sums(array, axis, bits):
    bits = list(bits)
    if not bits:
        return [array]
    for bit in bits[:-1]:
        array = array + swap(array, axis, bit)
    return [array, swap(array, axis, bits[-1])]


def add_all(parts):
    return functools.reduce(lambda a, b: a + b, parts)


def shards(queries, row_scale, leaf_basis, leaf_cores, level_basis, level_cores):
    levels = level_basis.shape[0]
    count = levels + 1
    top = levels
    rows_here, rank = leaf_basis.shape
    columns = queries.shape[1]
    groups, sub = lax.axis_size("rows"), lax.axis_size("sub")
    heights = [None] + [levels + 1 - e for e in range(1, count)]
    widths = [1] + [groups // 2 ** heights[e] for e in range(1, count)]
    head = sum(w == 1 for w in widths)
    bits = [range(0)] + [
        range(widths[e - 1].bit_length() - 1, widths[e].bit_length() - 1) for e in range(1, count)
    ]
    blocks = [list(range(e + 1 if e < head else e, count)) for e in range(count)]
    sub_bits = sub.bit_length() - 1
    leaf_bits = range(1, sub_bits)
    mine = columns // sub
    half = rank // 2
    small = 2 * 3 * rank**3

    scale = row_scale.reshape(-1, rank)
    starts = [sum(len(b) for b in blocks[:e]) * rank for e in range(count + 1)]

    def gram_body(*refs):
        sources, (out_ref, core_ref), (scale_ref, leaf_ref, level_ref, sems) = refs[:5], refs[5:7], refs[7:]
        scale_hbm, leaf_hbm, level_hbm, leaf_core_hbm, core_hbm = sources
        targets = [(scale_hbm, scale_ref), (leaf_hbm, leaf_ref)]
        targets += [(level_hbm.at[e], level_ref.at[e]) for e in reversed(range(levels))]
        place = lax.axis_index("rows")
        targets.append((leaf_core_hbm.at[0], core_ref.at[0]))
        for e in range(1, count):
            targets.append((core_hbm.at[2 ** heights[e] - 2 + place // widths[e]], core_ref.at[e]))
        copies = [pltpu.make_async_copy(a, b, sems.at[i]) for i, (a, b) in enumerate(targets)]
        for copy in copies:
            copy.start()
        for copy in copies[: 2 + levels]:
            copy.wait()
        vectors = [column_scale(scale_ref[...]) * leaf_ref[...]]
        vectors += [level_ref[levels - e] for e in range(1, count)]
        parts = [halves(v) for v in vectors]
        side = core_side()
        for e in range(count):
            right = [lanes([parts[f][i] for f in blocks[e]]) for i in range(2)]
            value = dot_parts(halves(vectors[e].T), right)
            for h in range(2):
                out_ref[at(h ^ side, half), starts[e] : starts[e + 1]] = value[h * half : (h + 1) * half]
        for copy in copies[2 + levels :]:
            copy.wait()

    gram, cores = call(
        gram_body,
        [(rank, starts[count]), (count, rank, rank)],
        *[
            pltpu.with_memory_space_constraint(array, pltpu.HBM)
            for array in (scale, leaf_basis, level_basis, leaf_cores, level_cores)
        ],
        flops=small * sum(map(len, blocks)) * rows_here // rank,
        spaces=[pltpu.HBM] * 5,
        scratch=[
            pltpu.VMEM(scale.shape, FLOAT),
            pltpu.VMEM(leaf_basis.shape, FLOAT),
            pltpu.VMEM(level_basis.shape, FLOAT),
            pltpu.SemaphoreType.DMA((2 + levels + count,)),
        ],
    )
    gram_chip = gram[:half] + swap(gram[half:], "sub", 0)
    tail_leaf = add_all(partial_sums(gram_chip[:, starts[head] :], "sub", leaf_bits))
    head_leaf = add_all(partial_sums(gram_chip[:, : starts[head]], "sub", leaf_bits))

    def moment_body(scale_ref, queries_ref, leaf_ref, level_ref, out_ref, *basis_refs):
        spread = column_scale(scale_ref[...])
        right = halves(lanes([leaf_ref[...]] + [spread * level_ref[levels - e] for e in range(1, count)]))
        for basis_ref, part in zip(basis_refs, right):
            basis_ref[...] = part
        value = dot_parts(halves(queries_ref[...].T), right)
        own = own_block()
        for i in range(sub):
            out_ref[at(i ^ own, mine), :] = value[i * mine : (i + 1) * mine]

    value, *basis = call(
        moment_body,
        [(columns, count * rank), *pair(rows_here, count * rank)],
        scale,
        queries,
        leaf_basis,
        level_basis,
        flops=small * count * 2 * rows_here // rank,
    )
    size = columns
    for bit in range(sub_bits):
        size //= 2
        moment_parts = [value[:size], swap(value[size:], "sub", bit)]
        value = add_all(moment_parts)

    late_rows = columns // 2 + head * half

    def late_body(scale_ref, queries_ref, leaf_ref, level_ref, out_ref, *scaled_refs):
        spread = column_scale(scale_ref[...])
        vectors = spread * leaf_ref[...]
        side = core_side()
        scaled = halves(spread * vectors)
        for scaled_ref, part in zip(scaled_refs, scaled):
            scaled_ref[...] = part
        value = dot_parts(halves(queries_ref[...].T), scaled)
        for h in range(2):
            base = (h ^ side) * late_rows
            part = value[h * columns // 2 : (h + 1) * columns // 2]
            out_ref[pl.ds(pl.multiple_of(base, 8), columns // 2), :] = part
        for e in range(head):
            basis = vectors if e == 0 else level_ref[levels - e]
            value = dot(basis.T, basis)
            for h in range(2):
                base = (h ^ side) * late_rows + columns // 2 + e * half
                out_ref[pl.ds(pl.multiple_of(base, 8), half), :] = value[h * half : (h + 1) * half]

    late, *scaled = call(
        late_body,
        [(2 * late_rows, rank), *pair(rows_here, rank)],
        scale,
        queries,
        leaf_basis,
        level_basis,
        flops=small * (2 + head) * rows_here // rank,
    )
    late_keep, late_got = late[:late_rows], swap(late[late_rows:], "sub", 0)

    def product_body(group, own_ref, other_ref, core_ref, *refs):
        out_refs, stack_ref = refs[:-1], refs[-1]
        side = core_side()
        stack_ref[at(side, half), :] = own_ref[...]
        stack_ref[at(1 - side, half), :] = other_ref[...]
        base = starts[group[0]]
        for i, e in enumerate(group):
            block = stack_ref[:, starts[e] - base : starts[e + 1] - base]
            store(out_refs[2 * i : 2 * i + 2], dot(core_ref[e].T, block))

    def products(group, own):
        out = call(
            functools.partial(product_body, group),
            [part for e in group for part in pair(rank, starts[e + 1] - starts[e])],
            own,
            swap(own, "sub", 0),
            cores,
            flops=small * sum(len(blocks[e]) for e in group),
            scratch=[pltpu.VMEM((rank, own.shape[1]), FLOAT)],
        )
        return [out[2 * i : 2 * i + 2] for i in range(len(group))]

    factors = products(list(range(head)), head_leaf)
    remaining = tail_leaf
    for e in range(head, count):
        remaining = add_all(partial_sums(remaining, "rows", bits[e]))
        size = starts[e + 1] - starts[e]
        factors += products([e], remaining[:, :size])
        remaining = remaining[:, size:]

    def flat(group):
        return [part for factor in group for part in factor]

    def paired(refs):
        return [refs[i : i + 2] for i in range(0, len(refs), 2)]

    def take(factor, start, size):
        return [ref[:, start : start + size] for ref in factor]

    def head_body(*refs):
        part_refs, factor_refs = refs[: len(moment_parts)], paired(refs[len(moment_parts) : -4])
        keep_ref, got_ref, rest_ref, late_ref = refs[-4:]
        rest = add_all([part[...] for part in part_refs])
        for e in range(head):
            own, rest = rest[:, :rank], rest[:, rank:]
            late_ref[late_rows + e * mine : late_rows + (e + 1) * mine, :] = own
            rest = rest - dot_parts(halves(own), take(factor_refs[e], 0, (count - 1 - e) * rank))
        rest_ref[...] = rest
        late_ref[:late_rows] = keep_ref[...] + got_ref[...]

    rest, late = call(
        head_body,
        [(mine, (count - head) * rank), (late_rows + head * mine, rank)],
        *moment_parts,
        *flat(factors[:head]),
        late_keep,
        late_got,
        flops=small * sum(map(len, blocks[:head])),
    )

    def step_body(number, *refs):
        part_refs, factor, (own_ref, rest_ref) = refs[:number], refs[number:-2], refs[-2:]
        total = add_all([part[...] for part in part_refs])
        own, rest = total[:, :rank], total[:, rank:]
        own_ref[...] = own
        rest_ref[...] = rest - dot_parts(halves(own), take(factor, rank, rest.shape[1]))

    def scatter(parts, number, stack_ref):
        own, slot = own_block(), 0
        for part in parts:
            for i in range(part.shape[0] // (number * mine)):
                for e in range(number):
                    start = (i * number + e) * mine
                    stack_ref[at(slot ^ own, mine), e * rank : (e + 1) * rank] = part[start : start + mine, :]
                slot += 1

    for bit in reversed(leaf_bits):
        got = swap(late, "sub", bit)
        late = jnp.concatenate([late[:late_rows] + got[:late_rows], late[late_rows:], got[late_rows:]], axis=0)
    late_parts = [late, swap(late, "sub", 0)]

    coarse = []
    for e in range(head, top):
        parts = partial_sums(rest, "rows", bits[e])
        own, rest = call(
            functools.partial(step_body, len(parts)),
            [(mine, rank), (mine, (top - e) * rank)],
            *parts,
            *factors[e],
            flops=small * (top - e),
        )
        coarse.append(own)
    coarse.append(rest)
    if len(bits[top]) == 1 and len(leaf_bits) == 1:
        row_bit, sub_bit = bits[top][0], leaf_bits[0]
        across = swap(rest, "rows", row_bit)
        beside = swap(jnp.concatenate(coarse, axis=0), "sub", sub_bit)
        corner = swap_both(rest, row_bit, sub_bit)
        end = (count - head - 1) * mine
        coarse = jnp.concatenate([*coarse[:-1], rest + across, beside[:end], beside[end:] + corner], axis=0)
    else:
        coarse[-1] = add_all(partial_sums(rest, "rows", bits[top]))
        coarse = jnp.concatenate(coarse, axis=0)
        for bit in reversed(leaf_bits):
            coarse = jnp.concatenate([coarse, swap(coarse, "sub", bit)], axis=0)
    coarse_parts = [coarse, swap(coarse, "sub", 0)]

    def answer_body(core_ref, *refs):
        factor_refs, basis_refs, out_refs = paired(refs[:-4]), refs[-4:-2], refs[-2:]
        wide = count - head
        zero = jnp.zeros((rank, rank), FLOAT)
        rows = {}
        for f in reversed(range(count)):
            start = 0 if f < head else rank
            if f + 1 < count:
                stack = jnp.concatenate([rows[g] for g in range(f + 1, count)], axis=0)
                row = -dot_parts(take(factor_refs[f], start, stack.shape[0]), halves(stack))
            else:
                row = jnp.zeros((rank, wide * rank), FLOAT)
            if f >= head:
                core = core_ref[f]
                own = core + core.T - dot_parts(take(factor_refs[f], 0, rank), halves(core))
                pieces = [zero] * (f - head) + [own]
                pieces += [row[:, e * rank : (e + 1) * rank] for e in range(f - head + 1, wide)]
                row = lanes(pieces)
            rows[f] = row
        gains = jnp.concatenate([rows[f] for f in range(count)], axis=0)
        store(out_refs, dot_parts([ref[...] for ref in basis_refs], halves(gains)))

    answer = call(
        answer_body,
        pair(rows_here, (count - head) * rank),
        cores,
        *flat(factors),
        *basis,
        flops=small * (count - head) * count * rows_here // rank,
    )

    def base_body(scale_ref, queries_ref, own_ref, other_ref, core_ref, *refs):
        factor_refs, basis_refs, scaled_refs = paired(refs[: 2 * head]), refs[2 * head : -5], refs[-5:-3]
        out_ref, stack_ref, gram_ref = refs[-3:]
        scatter([own_ref.at[late_rows:], other_ref.at[late_rows:]], head, stack_ref)
        side = core_side()
        for late_ref, place in ((own_ref, side), (other_ref, 1 - side)):
            stack_ref[at(place, columns // 2), head * rank :] = late_ref[: columns // 2]
            for e in range(head):
                start = columns // 2 + e * half
                gram_ref[at(place, half), e * rank : (e + 1) * rank] = late_ref[start : start + half]
        found = [None] * head
        for e in reversed(range(head)):
            core = core_ref[e]
            diagonal = dot(core.T, gram_ref[:, e * rank : (e + 1) * rank])
            moment = stack_ref[:, e * rank : (e + 1) * rank]
            if e:
                value = dot(moment, core + core.T - dot(diagonal, core), 1)
            else:
                first = dot(moment, core, 1)
                value = dot(stack_ref[:, head * rank :], core) - dot(first, diagonal, 1)
            if e + 1 < head:
                value = value - dot_parts(
                    halves(lanes(found[e + 1 :])), take(factor_refs[e], 0, (head - 1 - e) * rank), 1
                )
            found[e] = value
        left = [lanes([a[...], b[:, : head * rank]]) for a, b in zip(scaled_refs, basis_refs)]
        square = column_scale(scale_ref[...] * scale_ref[...])
        square = lanes([square] * (columns // rank))
        out_ref[...] = square * queries_ref[...] - dot_parts(left, halves(lanes([first, *found])), 1)

    (base,) = call(
        base_body,
        [(rows_here, columns)],
        scale,
        queries,
        *late_parts,
        cores,
        *flat(factors[:head]),
        *basis,
        *scaled,
        flops=small * 2 * (head + 1) * rows_here // rank,
        scratch=[pltpu.VMEM((columns, (head + 1) * rank), FLOAT), pltpu.VMEM((rank, head * rank), FLOAT)],
    )

    chunk = rows_here // 4

    def last_body(base_ref, high_ref, low_ref, own_ref, other_ref, out_hbm, stack_ref, out_ref, sems):
        scatter([own_ref, other_ref], count - head, stack_ref)
        right = halves(stack_ref[...])
        copies = []
        for i in range(4):
            rows = pl.ds(i * chunk, chunk)
            out_ref[rows, :] = base_ref[rows, :] - dot_parts([high_ref[rows, :], low_ref[rows, :]], right, 1)
            copies.append(pltpu.make_async_copy(out_ref.at[rows, :], out_hbm.at[rows, :], sems.at[i]))
            copies[-1].start()
        for copy in copies:
            copy.wait()

    (out,) = call(
        last_body,
        [(rows_here, columns)],
        base,
        *answer,
        *coarse_parts,
        flops=small * 2 * (count - head) * rows_here // rank,
        out_space=pltpu.HBM,
        scratch=[
            pltpu.VMEM((columns, (count - head) * rank), FLOAT),
            pltpu.VMEM((rows_here, columns), FLOAT),
            pltpu.SemaphoreType.DMA((4,)),
        ],
    )
    return out


def solution(mesh):
    in_specs = (
        P(("rows", "sub"), None),
        P(("rows", "sub")),
        P(("rows", "sub"), None),
        P("rows", None, None),
        P(None, ("rows", "sub"), None),
        P(),
    )
    out_specs = P(("rows", "sub"), None)

    return jax.shard_map(shards, mesh=mesh, in_specs=in_specs, out_specs=out_specs, check_vma=False)
```

time: 46.7 us -> 45.9 us (0.983)
  local copies, waits for them, and re-layouts: 5.74 us -> 0.57 us
  waiting for transfers between devices: 14.6 us -> 17.5 us
  starting transfers between devices: 16.6 us -> 17.6 us
    unnamed x16 -> x8, local copies, waits for them, and re-layouts: 3.3 us -> 0.45 us
    ppermute x16 -> x17, starting transfers between devices: 15 us -> 17.4 us  [swap(): lax.ppermute(array, axis, [(i, i ^ 1 << bit) for i in range(lax.axis_size...]
    ppermute x16 -> x17, waiting for transfers between devices: 14.6 us -> 16.1 us  [swap(): lax.ppermute(array, axis, [(i, i ^ 1 << bit) for i in range(lax.axis_size...]
    ppermute x1, starting transfers between devices: 1.6 us -> 0.17 us  [swap_both(): return lax.ppermute(array, ('rows', 'sub'), pairs)]
    ppermute x1, waiting for transfers between devices: 0.01 us -> 1.39 us  [swap_both(): return lax.ppermute(array, ('rows', 'sub'), pairs)]
    squeeze x1 -> x0, local copies, waits for them, and re-layouts: 0.93 us -> none  [shards(): lax.dynamic_index_in_dim(level_cores, 2 ** heights[e] - 2 + index // widt...]
    slice x2, local copies, waits for them, and re-layouts: 0.74 us -> 0.04 us  [shards(): moment_parts = [value[:size], swap(value[size:], 'sub', bit)]]
    slice x1, local copies, waits for them, and re-layouts: 0.71 us -> 0.02 us  [shards(): gram_chip = gram[:half] + swap(gram[half:], 'sub', 0)]
  transfers between devices with their start and end apart: 17 -> 18, of which waited for: 6 -> 7; matrix products, arithmetic and copies ran while one was open for 4% -> 1% of each run, Pallas kernels for 15% -> 13%
where the time goes in v5:
time: 45.9 us; the launch traced here: 45.7 us
  starting transfers between devices  17.6 us (38%)
  waiting for transfers between devices  17.5 us (38%)
  Pallas kernels  9.5 us (21%)
  local copies, waits for them, and re-layouts  0.57 us (1%)
    ppermute x17, starting transfers between devices, swap(): lax.ppermute(array, axis, [(i, i ^ 1 << bit) for i in range(lax.axis_size...  17.4 us
    ppermute x17, waiting for transfers between devices, swap(): lax.ppermute(array, axis, [(i, i ^ 1 << bit) for i in range(lax.axis_size...  16.1 us
    pallas_call x11, Pallas kernels, call(): pl.pallas_call(body, out_shape=outs, in_specs=[pl.BlockSpec(memory_space=...  9.5 us
    ppermute x1, waiting for transfers between devices, swap_both(): return lax.ppermute(array, ('rows', 'sub'), pairs)  1.39 us
  transfers between devices with their start and end apart: 18, of which 7 were waited for; matrix products, arithmetic and copies ran while one was open for 1% of the time, Pallas kernels for 13%

profile of v5, /device:TPU:0, one launch (start us, length us, event | category | flops | bytes accessed | tf_op | source)
XLA Modules:
  0.0 45.7 jit_solution(10782155683095657704)
XLA Ops:
  0.0 0.0 copy-start
  0.0 0.0 copy-start.2
  0.0 0.0 copy-start.3
  0.0 2.2 %shard_map.65 = (f32[128,1024]{1,0:T(8,128)S(1)}, f32[4,128,128]{2,1,0:T(8,128)S(1)}) custom-call(f32[4,128]{1,0:T(4,128)} %bitcast.1, f32[512,128]{1,0:T(8,128)} %leaf_ref.3, f32[3,512,128]{2,1,0:T(8,128)} %level_ref.3, f32[1,128,128]{2,1,0:T(8,128)} %refs_3_.1, f32[14,128,128]{2,1,0:T(8,128)} %refs_4_.1), custom_call_target="tpu_custom_call" | custom-call | flops 402653184 | bytes 2033664 | tf_op jit(solution)/shard_map/pallas_call | solution.py:64
  2.2 0.0 copy-start.1
  2.2 0.6 %collective-permute-start.2 = (f32[64,1024]{1,0:T(8,128)S(1)}, f32[64,1024]{1,0:T(8,128)S(1)}, u32[]{:S(2)}, u32[]{:S(2)}) collective-permute-start(f32[64,1024]{1,0:T(8,128)S(1)} %slice.59), channel_id=1, source_target_pairs={{0,1},{1,0},{2,3},{3,2},{4,5},{5,4},{6,7},{7,6},{8,9},{9,8},{10,11... | collective-permute-start | bytes 786440 | tf_op jit(solution)/shard_map/ppermute | solution.py:85
  2.8 0.0 copy-done
  2.8 0.0 copy-done.2
  2.8 0.0 copy-done.3
  2.8 0.4 copy-done.1
  3.2 0.8 %shard_map.64 = (f32[256,512]{1,0:T(8,128)S(1)}, bf16[512,512]{1,0:T(8,128)(2,1)S(1)}, bf16[512,512]{1,0:T(8,128)(2,1)S(1)}) custom-call(f32[4,128]{1,0:T(4,128)S(1)} %bitcast.2, f32[512,256]{1,0:T(8,128)S(1)} %copy-done.1, f32[512,128]{1,0:T(8,128)S(1)} %copy-done.2, f32[3,512,128]{2,1,0:T(8,128)S(1)} %copy-done), custom_call_target="tpu_custom_call" | custom-call | flops 402653184 | bytes 1574912 | tf_op jit(solution)/shard_map/pallas_call | solution.py:64
  4.1 0.6 %collective-permute-start = (f32[128,512]{1,0:T(8,128)S(1)}, f32[128,512]{1,0:T(8,128)S(1)}, u32[]{:S(2)}, u32[]{:S(2)}) collective-permute-start(f32[128,512]{1,0:T(8,128)S(1)} %slice.55), channel_id=1, source_target_pairs={{0,1},{1,0},{2,3},{3,2},{4,5},{5,4},{6,7},{7,6},{8,9},{9,8},{10,11... | collective-permute-start | bytes 786440 | tf_op jit(solution)/shard_map/ppermute | solution.py:85
  4.6 0.7 %shard_map.67 = (f32[512,128]{1,0:T(8,128)S(1)}, bf16[512,128]{1,0:T(8,128)(2,1)S(1)}, bf16[512,128]{1,0:T(8,128)(2,1)S(1)}) custom-call(f32[4,128]{1,0:T(4,128)S(1)} %bitcast.3, f32[512,256]{1,0:T(8,128)S(1)} %copy-done.1, f32[512,128]{1,0:T(8,128)S(1)} %copy-done.2, f32[3,512,128]{2,1,0:T(8,128)S(1)} %copy-done), custom_call_target="tpu_custom_call" | custom-call | flops 201326592 | bytes 1574912 | tf_op jit(solution)/shard_map/pallas_call | solution.py:64
  5.4 0.1 collective-permute-start.5
  5.5 0.0 collective-permute-done.2
  5.6 3.1 %collective-permute-start.3 = (f32[64,640]{1,0:T(8,128)S(1)}, f32[64,640]{1,0:T(8,128)S(1)}, u32[]{:S(2)}, u32[]{:S(2)}) collective-permute-start(f32[64,640]{1,0:T(8,128)S(1)} %slice.74), channel_id=1, source_target_pairs={{0,2},{1,3},{2,0},{3,1},{4,6},{5,7},{6,4},{7,5},{8,10},{9,11},{10,... | collective-permute-start | bytes 491528 | tf_op jit(solution)/shard_map/ppermute | solution.py:85
  8.6 0.0 collective-permute-done
  8.7 0.1 collective-permute-start.1
  8.8 2.0 %collective-permute-start.8 = (f32[64,384]{1,0:T(8,128)S(1)}, f32[64,384]{1,0:T(8,128)S(1)}, u32[]{:S(2)}, u32[]{:S(2)}) collective-permute-start(f32[64,384]{1,0:T(8,128)S(1)} %slice.77), channel_id=1, source_target_pairs={{0,2},{1,3},{2,0},{3,1},{4,6},{5,7},{6,4},{7,5},{8,10},{9,11},{10,... | collective-permute-start | bytes 294920 | tf_op jit(solution)/shard_map/ppermute | solution.py:85
  10.8 2.9 %collective-permute-done.3 = f32[64,640]{1,0:T(8,128)S(1)} collective-permute-done((f32[64,640]{1,0:T(8,128)S(1)}, f32[64,640]{1,0:T(8,128)S(1)}, u32[]{:S(2)}, u32[]{:S(2)}) %collective-permute-start.3) | collective-permute-done | bytes 163872 | tf_op jit(solution)/shard_map/ppermute | solution.py:85
  13.7 0.1 collective-permute-start.4
  13.8 4.1 %collective-permute-done.8 = f32[64,384]{1,0:T(8,128)S(1)} collective-permute-done((f32[64,384]{1,0:T(8,128)S(1)}, f32[64,384]{1,0:T(8,128)S(1)}, u32[]{:S(2)}, u32[]{:S(2)}) %collective-permute-start.8) | collective-permute-done | bytes 98336 | tf_op jit(solution)/shard_map/ppermute | solution.py:85
  17.9 1.8 %collective-permute-start.9 = (f32[64,384]{1,0:T(8,128)S(1)}, f32[64,384]{1,0:T(8,128)S(1)}, u32[]{:S(2)}, u32[]{:S(2)}) collective-permute-start(f32[64,384]{1,0:T(8,128)S(1)} %slice_add_fusion.5), channel_id=1, source_target_pairs={{0,4},{4,0},{8,12},{12,8},{16,20},{20,16},{24,28},{28,24},{1,5},{5... | collective-permute-start | bytes 294920 | tf_op jit(solution)/shard_map/ppermute | solution.py:85
  19.7 2.9 %collective-permute-done.9 = f32[64,384]{1,0:T(8,128)S(1)} collective-permute-done((f32[64,384]{1,0:T(8,128)S(1)}, f32[64,384]{1,0:T(8,128)S(1)}, u32[]{:S(2)}, u32[]{:S(2)}) %collective-permute-start.9) | collective-permute-done | bytes 98336 | tf_op jit(solution)/shard_map/ppermute | solution.py:85
  22.7 0.1 collective-permute-start.10
  22.7 0.0 collective-permute-done.4.other_ref
  22.8 0.4 shard_map.66
  23.1 0.0 collective-permute-done.5.refs_7_
  23.1 0.0 collective-permute-done.1.refs_1_
  23.1 0.4 shard_map.68
  23.5 1.8 %collective-permute-start.13 = (f32[64,256]{1,0:T(8,128)S(1)}, f32[64,256]{1,0:T(8,128)S(1)}, u32[]{:S(2)}, u32[]{:S(2)}) collective-permute-start(f32[64,256]{1,0:T(8,128)S(1)} %get-tuple-element.46.refs_0_), channel_id=1, source_target_pairs={{0,4},{4,0},{8,12},{12,8},{16,20},{20,16},{24,28},{28,24},{1,5},{5... | collective-permute-start | bytes 196616 | tf_op jit(solution)/shard_map/ppermute | solution.py:85
  25.3 0.0 collective-permute-done.10.other_ref
  25.3 0.3 shard_map.70
  25.6 2.5 %collective-permute-done.13.refs_1_ = f32[64,256]{1,0:T(8,128)S(1)} collective-permute-done((f32[64,256]{1,0:T(8,128)S(1)}, f32[64,256]{1,0:T(8,128)S(1)}, u32[]{:S(2)}, u32[]{:S(2)}) %collective-permute-start.13) | collective-permute-done | bytes 65568 | tf_op jit(solution)/shard_map/ppermute | solution.py:85
  28.1 0.1 shard_map.73
  28.2 1.8 %collective-permute-start.15 = (f32[128,128]{1,0:T(8,128)S(1)}, f32[128,128]{1,0:T(8,128)S(1)}, u32[]{:S(2)}, u32[]{:S(2)}) collective-permute-start(f32[128,128]{1,0:T(8,128)S(1)} %pad_maximum_fusion.2), channel_id=1, source_target_pairs={{0,2},{1,3},{2,0},{3,1},{4,6},{5,7},{6,4},{7,5},{8,10},{9,11},{10,... | collective-permute-start | bytes 196616 | tf_op jit(solution)/shard_map/ppermute | solution.py:85
  30.0 1.6 %collective-permute-start.14 = (f32[64,128]{1,0:T(8,128)S(1)}, f32[64,128]{1,0:T(8,128)S(1)}, u32[]{:S(2)}, u32[]{:S(2)}) collective-permute-start(f32[64,128]{1,0:T(8,128)S(1)} %get-tuple-element.48), channel_id=1, source_target_pairs={{0,8},{4,12},{8,0},{12,4},{16,24},{20,28},{24,16},{28,20},{1,9},{5... | collective-permute-start | bytes 98312 | tf_op jit(solution)/shard_map/ppermute | solution.py:85
  31.6 0.2 collective-permute-start.16
  31.8 1.8 %collective-permute-start.11 = (f32[64,128]{1,0:T(8,128)S(1)}, f32[64,128]{1,0:T(8,128)S(1)}, u32[]{:S(2)}, u32[]{:S(2)}) collective-permute-start(f32[64,128]{1,0:T(8,128)S(1)} %slice.79), channel_id=1, source_target_pairs={{0,8},{4,12},{8,0},{12,4},{16,24},{20,28},{24,16},{28,20},{1,9},{5... | collective-permute-start | bytes 98312 | tf_op jit(solution)/shard_map/ppermute | solution.py:85
  33.6 1.5 %collective-permute-start.6 = (f32[384,128]{1,0:T(8,128)S(1)}, f32[384,128]{1,0:T(8,128)S(1)}, u32[]{:S(2)}, u32[]{:S(2)}) collective-permute-start(f32[384,128]{1,0:T(8,128)S(1)} %get-tuple-element.35), channel_id=1, source_target_pairs={{0,2},{1,3},{2,0},{3,1},{4,6},{5,7},{6,4},{7,5},{8,10},{9,11},{10,... | collective-permute-start | bytes 589832 | tf_op jit(solution)/shard_map/ppermute | solution.py:85
  35.1 0.0 collective-permute-done.14
  35.1 1.4 %collective-permute-done.16 = f32[64,128]{1,0:T(8,128)S(1)} collective-permute-done((f32[64,128]{1,0:T(8,128)S(1)}, f32[64,128]{1,0:T(8,128)S(1)}, u32[]{:S(2)}, u32[]{:S(2)}) %collective-permute-start.16) | collective-permute-done | bytes 32800 | tf_op jit(solution)/shard_map/ppermute | solution.py:92
  36.5 0.0 collective-permute-done.15
  36.6 0.1 collective-permute-start.17
  36.6 2.6 %collective-permute-done.6 = f32[384,128]{1,0:T(8,128)S(1)} collective-permute-done((f32[384,128]{1,0:T(8,128)S(1)}, f32[384,128]{1,0:T(8,128)S(1)}, u32[]{:S(2)}, u32[]{:S(2)}) %collective-permute-start.6) | collective-permute-done | bytes 196640 | tf_op jit(solution)/shard_map/ppermute | solution.py:85
  39.3 0.1 collective-permute-start.7
  39.4 0.0 collective-permute-done.11
  39.4 0.5 %collective-permute-start.12 = (f32[64,128]{1,0:T(8,128)S(1)}, f32[64,128]{1,0:T(8,128)S(1)}, u32[]{:S(2)}, u32[]{:S(2)}) collective-permute-start(f32[64,128]{1,0:T(8,128)S(1)} %slice_add_fusion.4.own_ref), channel_id=1, source_target_pairs={{0,1},{1,0},{2,3},{3,2},{4,5},{5,4},{6,7},{7,6},{8,9},{9,8},{10,11... | collective-permute-start | bytes 98312 | tf_op jit(solution)/shard_map/ppermute | solution.py:85
  40.0 1.0 %collective-permute-done.12.other_ref = f32[64,128]{1,0:T(8,128)S(1)} collective-permute-done((f32[64,128]{1,0:T(8,128)S(1)}, f32[64,128]{1,0:T(8,128)S(1)}, u32[]{:S(2)}, u32[]{:S(2)}) %collective-permute-start.12) | collective-permute-done | bytes 32800 | tf_op jit(solution)/shard_map/ppermute | solution.py:85
  41.0 0.2 shard_map.71
  41.2 1.6 %shard_map.72 = (bf16[512,256]{1,0:T(8,128)(2,1)S(1)}, bf16[512,256]{1,0:T(8,128)(2,1)S(1)}) custom-call(f32[4,128,128]{2,1,0:T(8,128)S(1)} %get-tuple-element.29.core_ref, bf16[128,384]{1,0:T(8,128)(2,1)S(1)} %get-tuple-element.30.refs_2_.refs_0_, bf16[128,384]{1,0:T(8,128)(2,1)S(1)} %get-tuple-element.31.refs_3_.refs_1_, ...), custom_call_target="tpu_custom_call" | custom-call | flops 402653184 | bytes 1835008 | tf_op jit(solution)/shard_map/pallas_call | solution.py:64
  42.8 0.0 collective-permute-done.7.other_ref
  42.8 1.4 %shard_map.69.base_ref = f32[512,256]{1,0:T(8,128)S(1)} custom-call(f32[4,128]{1,0:T(4,128)S(1)} %bitcast.4, f32[512,256]{1,0:T(8,128)S(1)} %copy-done.1, f32[512,128]{1,0:T(8,128)S(1)} %pad_maximum_fusion.own_ref, f32[512,128]{1,0:T(8,128)S(1)} %collective-permute-done.7.other_ref, f32[4,128,128]{2,1,0:T(8,128)S(1)} %get-tuple-element.29.core_ref, ...), custom_call_target="tpu_custom_call" | custom-call | flops 301989888 | bytes 2951168 | tf_op jit(solution)/shard_map/pallas_call | solution.py:64
  44.2 0.0 collective-permute-done.17.other_ref
  44.3 1.4 %shard_map.74 = f32[512,256]{1,0:T(8,128)} custom-call(f32[512,256]{1,0:T(8,128)S(1)} %shard_map.69.base_ref, bf16[512,256]{1,0:T(8,128)(2,1)S(1)} %get-tuple-element.44.high_ref, bf16[512,256]{1,0:T(8,128)(2,1)S(1)} %get-tuple-element.45.low_ref, f32[256,128]{1,0:T(8,128)S(1)} %pad_maximum_fusion.1.own_ref, f32[256,128]{1,0:T(8,128)S(1)} %collective-permute-done.17.other_ref), custom_call_target="tpu_custom_call" | custom-call | flops 201326592 | bytes 1310720 | tf_op jit(solution)/shard_map/pallas_call | solution.py:64
  (22 shorter events, 0.3 us)
Async XLA Ops:
  0.0 2.8 %copy-start = (f32[3,512,128]{2,1,0:T(8,128)S(1)}, f32[3,512,128]{2,1,0:T(8,128)}, u32[]{:S(2)}) copy-start(f32[3,512,128]{2,1,0:T(8,128)} %level_ref.3) | copy-start | bytes 2359300
  0.0 2.8 %copy-start.2 = (f32[512,128]{1,0:T(8,128)S(1)}, f32[512,128]{1,0:T(8,128)}, u32[]{:S(2)}) copy-start(f32[512,128]{1,0:T(8,128)} %leaf_ref.3) | copy-start | bytes 786436
  0.0 2.8 %copy-start.3 = (f32[512]{0:T(512)S(1)}, f32[512]{0:T(512)}, u32[]{:S(2)}) copy-start(f32[512]{0:T(512)} %param.7) | copy-start | bytes 6148
  2.2 1.0 %copy-start.1 = (f32[512,256]{1,0:T(8,128)S(1)}, f32[512,256]{1,0:T(8,128)}, u32[]{:S(2)}) copy-start(f32[512,256]{1,0:T(8,128)} %queries_ref.5) | copy-start | bytes 1572868
  2.2 3.2 %collective-permute-start.2 = (f32[64,1024]{1,0:T(8,128)S(1)}, f32[64,1024]{1,0:T(8,128)S(1)}, u32[]{:S(2)}, u32[]{:S(2)}) collective-permute-start(f32[64,1024]{1,0:T(8,128)S(1)} %slice.59), channel_id=1, source_target_pairs={{0,1},{1,0},{2,3},{3,2},{4,5},{5,4},{6,7},{7,6},{8,9},{9,8},{10,11... | collective-permute-start | bytes 786440 | tf_op jit(solution)/shard_map/ppermute | solution.py:85
  4.1 4.6 %collective-permute-start = (f32[128,512]{1,0:T(8,128)S(1)}, f32[128,512]{1,0:T(8,128)S(1)}, u32[]{:S(2)}, u32[]{:S(2)}) collective-permute-start(f32[128,512]{1,0:T(8,128)S(1)} %slice.55), channel_id=1, source_target_pairs={{0,1},{1,0},{2,3},{3,2},{4,5},{5,4},{6,7},{7,6},{8,9},{9,8},{10,11... | collective-permute-start | bytes 786440 | tf_op jit(solution)/shard_map/ppermute | solution.py:85
  5.4 17.7 %collective-permute-start.5 = (f32[256,128]{1,0:T(8,128)S(1)}, f32[256,128]{1,0:T(8,128)S(1)}, u32[]{:S(2)}, u32[]{:S(2)}) collective-permute-start(f32[256,128]{1,0:T(8,128)S(1)} %get-tuple-element.49), channel_id=1, source_target_pairs={{0,1},{1,0},{2,3},{3,2},{4,5},{5,4},{6,7},{7,6},{8,9},{9,8},{10,11... | collective-permute-start | bytes 393224 | tf_op jit(solution)/shard_map/ppermute | solution.py:85
  5.6 8.1 %collective-permute-start.3 = (f32[64,640]{1,0:T(8,128)S(1)}, f32[64,640]{1,0:T(8,128)S(1)}, u32[]{:S(2)}, u32[]{:S(2)}) collective-permute-start(f32[64,640]{1,0:T(8,128)S(1)} %slice.74), channel_id=1, source_target_pairs={{0,2},{1,3},{2,0},{3,1},{4,6},{5,7},{6,4},{7,5},{8,10},{9,11},{10,... | collective-permute-start | bytes 491528 | tf_op jit(solution)/shard_map/ppermute | solution.py:85
  8.7 14.4 %collective-permute-start.1 = (f32[64,512]{1,0:T(8,128)S(1)}, f32[64,512]{1,0:T(8,128)S(1)}, u32[]{:S(2)}, u32[]{:S(2)}) collective-permute-start(f32[64,512]{1,0:T(8,128)S(1)} %get-tuple-element.51), channel_id=1, source_target_pairs={{0,2},{1,3},{2,0},{3,1},{4,6},{5,7},{6,4},{7,5},{8,10},{9,11},{10,... | collective-permute-start | bytes 393224 | tf_op jit(solution)/shard_map/ppermute | solution.py:85
  8.8 9.1 %collective-permute-start.8 = (f32[64,384]{1,0:T(8,128)S(1)}, f32[64,384]{1,0:T(8,128)S(1)}, u32[]{:S(2)}, u32[]{:S(2)}) collective-permute-start(f32[64,384]{1,0:T(8,128)S(1)} %slice.77), channel_id=1, source_target_pairs={{0,2},{1,3},{2,0},{3,1},{4,6},{5,7},{6,4},{7,5},{8,10},{9,11},{10,... | collective-permute-start | bytes 294920 | tf_op jit(solution)/shard_map/ppermute | solution.py:85
  13.7 9.0 %collective-permute-start.4 = (f32[64,640]{1,0:T(8,128)S(1)}, f32[64,640]{1,0:T(8,128)S(1)}, u32[]{:S(2)}, u32[]{:S(2)}) collective-permute-start(f32[64,640]{1,0:T(8,128)S(1)} %slice_add_fusion.6.own_ref), channel_id=1, source_target_pairs={{0,1},{1,0},{2,3},{3,2},{4,5},{5,4},{6,7},{7,6},{8,9},{9,8},{10,11... | collective-permute-start | bytes 491528 | tf_op jit(solution)/shard_map/ppermute | solution.py:85
  17.9 4.7 %collective-permute-start.9 = (f32[64,384]{1,0:T(8,128)S(1)}, f32[64,384]{1,0:T(8,128)S(1)}, u32[]{:S(2)}, u32[]{:S(2)}) collective-permute-start(f32[64,384]{1,0:T(8,128)S(1)} %slice_add_fusion.5), channel_id=1, source_target_pairs={{0,4},{4,0},{8,12},{12,8},{16,20},{20,16},{24,28},{28,24},{1,5},{5... | collective-permute-start | bytes 294920 | tf_op jit(solution)/shard_map/ppermute | solution.py:85
  22.7 2.6 %collective-permute-start.10 = (f32[64,256]{1,0:T(8,128)S(1)}, f32[64,256]{1,0:T(8,128)S(1)}, u32[]{:S(2)}, u32[]{:S(2)}) collective-permute-start(f32[64,256]{1,0:T(8,128)S(1)} %slice.78.own_ref), channel_id=1, source_target_pairs={{0,1},{1,0},{2,3},{3,2},{4,5},{5,4},{6,7},{7,6},{8,9},{9,8},{10,11... | collective-permute-start | bytes 196616 | tf_op jit(solution)/shard_map/ppermute | solution.py:85
  23.5 4.6 %collective-permute-start.13 = (f32[64,256]{1,0:T(8,128)S(1)}, f32[64,256]{1,0:T(8,128)S(1)}, u32[]{:S(2)}, u32[]{:S(2)}) collective-permute-start(f32[64,256]{1,0:T(8,128)S(1)} %get-tuple-element.46.refs_0_), channel_id=1, source_target_pairs={{0,4},{4,0},{8,12},{12,8},{16,20},{20,16},{24,28},{28,24},{1,5},{5... | collective-permute-start | bytes 196616 | tf_op jit(solution)/shard_map/ppermute | solution.py:85
  28.2 8.3 %collective-permute-start.15 = (f32[128,128]{1,0:T(8,128)S(1)}, f32[128,128]{1,0:T(8,128)S(1)}, u32[]{:S(2)}, u32[]{:S(2)}) collective-permute-start(f32[128,128]{1,0:T(8,128)S(1)} %pad_maximum_fusion.2), channel_id=1, source_target_pairs={{0,2},{1,3},{2,0},{3,1},{4,6},{5,7},{6,4},{7,5},{8,10},{9,11},{10,... | collective-permute-start | bytes 196616 | tf_op jit(solution)/shard_map/ppermute | solution.py:85
  30.0 5.1 %collective-permute-start.14 = (f32[64,128]{1,0:T(8,128)S(1)}, f32[64,128]{1,0:T(8,128)S(1)}, u32[]{:S(2)}, u32[]{:S(2)}) collective-permute-start(f32[64,128]{1,0:T(8,128)S(1)} %get-tuple-element.48), channel_id=1, source_target_pairs={{0,8},{4,12},{8,0},{12,4},{16,24},{20,28},{24,16},{28,20},{1,9},{5... | collective-permute-start | bytes 98312 | tf_op jit(solution)/shard_map/ppermute | solution.py:85
  31.6 4.9 %collective-permute-start.16 = (f32[64,128]{1,0:T(8,128)S(1)}, f32[64,128]{1,0:T(8,128)S(1)}, u32[]{:S(2)}, u32[]{:S(2)}) collective-permute-start(f32[64,128]{1,0:T(8,128)S(1)} %get-tuple-element.48), channel_id=1, source_target_pairs={{0,10},{1,11},{2,8},{3,9},{4,14},{5,15},{6,12},{7,13},{8,2},{9,3},... | collective-permute-start | bytes 98312 | tf_op jit(solution)/shard_map/ppermute | solution.py:92
  31.8 7.6 %collective-permute-start.11 = (f32[64,128]{1,0:T(8,128)S(1)}, f32[64,128]{1,0:T(8,128)S(1)}, u32[]{:S(2)}, u32[]{:S(2)}) collective-permute-start(f32[64,128]{1,0:T(8,128)S(1)} %slice.79), channel_id=1, source_target_pairs={{0,8},{4,12},{8,0},{12,4},{16,24},{20,28},{24,16},{28,20},{1,9},{5... | collective-permute-start | bytes 98312 | tf_op jit(solution)/shard_map/ppermute | solution.py:85
  33.6 5.7 %collective-permute-start.6 = (f32[384,128]{1,0:T(8,128)S(1)}, f32[384,128]{1,0:T(8,128)S(1)}, u32[]{:S(2)}, u32[]{:S(2)}) collective-permute-start(f32[384,128]{1,0:T(8,128)S(1)} %get-tuple-element.35), channel_id=1, source_target_pairs={{0,2},{1,3},{2,0},{3,1},{4,6},{5,7},{6,4},{7,5},{8,10},{9,11},{10,... | collective-permute-start | bytes 589832 | tf_op jit(solution)/shard_map/ppermute | solution.py:85
  36.6 7.7 %collective-permute-start.17 = (f32[256,128]{1,0:T(8,128)S(1)}, f32[256,128]{1,0:T(8,128)S(1)}, u32[]{:S(2)}, u32[]{:S(2)}) collective-permute-start(f32[256,128]{1,0:T(8,128)S(1)} %pad_maximum_fusion.1.own_ref), channel_id=1, source_target_pairs={{0,1},{1,0},{2,3},{3,2},{4,5},{5,4},{6,7},{7,6},{8,9},{9,8},{10,11... | collective-permute-start | bytes 393224 | tf_op jit(solution)/shard_map/ppermute | solution.py:85
  39.3 3.5 %collective-permute-start.7 = (f32[512,128]{1,0:T(8,128)S(1)}, f32[512,128]{1,0:T(8,128)S(1)}, u32[]{:S(2)}, u32[]{:S(2)}) collective-permute-start(f32[512,128]{1,0:T(8,128)S(1)} %pad_maximum_fusion.own_ref), channel_id=1, source_target_pairs={{0,1},{1,0},{2,3},{3,2},{4,5},{5,4},{6,7},{7,6},{8,9},{9,8},{10,11... | collective-permute-start | bytes 786440 | tf_op jit(solution)/shard_map/ppermute | solution.py:85
  39.4 1.5 %collective-permute-start.12 = (f32[64,128]{1,0:T(8,128)S(1)}, f32[64,128]{1,0:T(8,128)S(1)}, u32[]{:S(2)}, u32[]{:S(2)}) collective-permute-start(f32[64,128]{1,0:T(8,128)S(1)} %slice_add_fusion.4.own_ref), channel_id=1, source_target_pairs={{0,1},{1,0},{2,3},{3,2},{4,5},{5,4},{6,7},{7,6},{8,9},{9,8},{10,11... | collective-permute-start | bytes 98312 | tf_op jit(solution)/shard_map/ppermute | solution.py:85

commit v6 on v5

--- a/solution.py
+++ b/solution.py
@@ -118,7 +118,8 @@
     bits = [range(0)] + [
         range(widths[e - 1].bit_length() - 1, widths[e].bit_length() - 1) for e in range(1, count)
     ]
-    blocks = [list(range(e + 1 if e < head else e, count)) for e in range(count)]
+    blocks = [list(range(e + 1, count)) for e in range(count)]
+    coarse = count - head
     sub_bits = sub.bit_length() - 1
     leaf_bits = range(1, sub_bits)
     mine = columns // sub
@@ -147,21 +148,28 @@
         parts = [halves(v) for v in vectors]
         side = core_side()
         for e in range(count):
-            right = [lanes([parts[f][i] for f in blocks[e]]) for i in range(2)]
+            group = ([e] if e >= head else []) + blocks[e]
+            right = [lanes([parts[f][i] for f in group]) for i in range(2)]
             value = dot_parts(halves(vectors[e].T), right)
             for h in range(2):
-                out_ref[at(h ^ side, half), starts[e] : starts[e + 1]] = value[h * half : (h + 1) * half]
+                rows = value[h * half : (h + 1) * half]
+                if e >= head:
+                    place = starts[count] + (e - head) * rank
+                    out_ref[at(h ^ side, half), place : place + rank] = rows[:, :rank]
+                    rows = rows[:, rank:]
+                if blocks[e]:
+                    out_ref[at(h ^ side, half), starts[e] : starts[e + 1]] = rows
         for copy in copies[2 + levels :]:
             copy.wait()
 
     gram, cores = call(
         gram_body,
-        [(rank, starts[count]), (count, rank, rank)],
+        [(rank, starts[count] + coarse * rank), (count, rank, rank)],
         *[
             pltpu.with_memory_space_constraint(array, pltpu.HBM)
             for array in (scale, leaf_basis, level_basis, leaf_cores, level_cores)
         ],
-        flops=small * sum(map(len, blocks)) * rows_here // rank,
+        flops=small * (starts[count] // rank + coarse) * rows_here // rank,
         spaces=[pltpu.HBM] * 5,
         scratch=[
             pltpu.VMEM(scale.shape, FLOAT),
@@ -171,8 +179,13 @@
         ],
     )
     gram_chip = gram[:half] + swap(gram[half:], "sub", 0)
-    tail_leaf = add_all(partial_sums(gram_chip[:, starts[head] :], "sub", leaf_bits))
-    head_leaf = add_all(partial_sums(gram_chip[:, : starts[head]], "sub", leaf_bits))
+    early = add_all(partial_sums(gram_chip[:, : starts[count]], "sub", leaf_bits))
+    diagonal = []
+    for e in reversed(range(head, count)):
+        place = starts[count] + (e - head) * rank
+        diagonal = lanes([gram_chip[:, place : place + rank], *diagonal])
+        diagonal = [add_all(partial_sums(diagonal, "rows", bits[e]))]
+    diagonal = diagonal[0]
 
     def moment_body(scale_ref, queries_ref, leaf_ref, level_ref, out_ref, *basis_refs):
         spread = column_scale(scale_ref[...])
@@ -196,8 +209,10 @@
     size = columns
     for bit in range(sub_bits):
         size //= 2
-        moment_parts = [value[:size], swap(value[size:], "sub", bit)]
+        sent, moment_parts = value[size:], [value[:size], swap(value[size:], "sub", bit)]
         value = add_all(moment_parts)
+        if bit == 0:
+            moment_chip = value
 
     late_rows = columns // 2 + head * half
 
@@ -229,7 +244,34 @@
         level_basis,
         flops=small * (2 + head) * rows_here // rank,
     )
-    late_keep, late_got = late[:late_rows], swap(late[late_rows:], "sub", 0)
+    late_chip = late[:late_rows] + swap(late[late_rows:], "sub", 0)
+
+    def stacked(array, size):
+        return [
+            array[i : i + size, j : j + rank]
+            for i in range(0, array.shape[0], size)
+            for j in range(0, array.shape[1], rank)
+        ]
+
+    late_chip = [late_chip, *stacked(diagonal, half)]
+    if len(leaf_bits) == 1:
+        late = jnp.concatenate([*late_chip, *stacked(moment_parts[0][:, : head * rank], mine)], axis=0)
+        got = swap(late, "sub", leaf_bits[0])
+        late_size = late_rows + coarse * half
+        others = jnp.concatenate(stacked(sent[:, : head * rank], mine), axis=0)
+        late = jnp.concatenate(
+            [
+                late[:late_size] + got[:late_size],
+                *stacked(value[:, : head * rank], mine),
+                others + got[late_size:],
+            ],
+            axis=0,
+        )
+    else:
+        late = jnp.concatenate([*late_chip, *stacked(moment_chip[:, : head * rank], mine)], axis=0)
+        late_size = late_rows + coarse * half
+        late = add_all(partial_sums(late, "sub", leaf_bits))
+    late_parts = [late, swap(late, "sub", 0)]
 
     def product_body(group, own_ref, other_ref, core_ref, *refs):
         out_refs, stack_ref = refs[:-1], refs[-1]
@@ -253,9 +295,9 @@
         )
         return [out[2 * i : 2 * i + 2] for i in range(len(group))]
 
-    factors = products(list(range(head)), head_leaf)
-    remaining = tail_leaf
-    for e in range(head, count):
+    factors = products(list(range(head)), early[:, : starts[head]])
+    remaining = early[:, starts[head] :]
+    for e in range(head, top):
         remaining = add_all(partial_sums(remaining, "rows", bits[e]))
         size = starts[e + 1] - starts[e]
         factors += products([e], remaining[:, :size])
@@ -271,23 +313,18 @@
         return [ref[:, start : start + size] for ref in factor]
 
     def head_body(*refs):
-        part_refs, factor_refs = refs[: len(moment_parts)], paired(refs[len(moment_parts) : -4])
-        keep_ref, got_ref, rest_ref, late_ref = refs[-4:]
+        part_refs, factor_refs, rest_ref = refs[: len(moment_parts)], paired(refs[len(moment_parts) : -1]), refs[-1]
         rest = add_all([part[...] for part in part_refs])
         for e in range(head):
             own, rest = rest[:, :rank], rest[:, rank:]
-            late_ref[late_rows + e * mine : late_rows + (e + 1) * mine, :] = own
-            rest = rest - dot_parts(halves(own), take(factor_refs[e], 0, (count - 1 - e) * rank))
+            rest = rest - dot_parts(halves(own), take(factor_refs[e], 0, rest.shape[1]))
         rest_ref[...] = rest
-        late_ref[:late_rows] = keep_ref[...] + got_ref[...]
-
-    rest, late = call(
+
+    (rest,) = call(
         head_body,
-        [(mine, (count - head) * rank), (late_rows + head * mine, rank)],
+        [(mine, coarse * rank)],
         *moment_parts,
         *flat(factors[:head]),
-        late_keep,
-        late_got,
         flops=small * sum(map(len, blocks[:head])),
     )
 
@@ -296,7 +333,7 @@
         total = add_all([part[...] for part in part_refs])
         own, rest = total[:, :rank], total[:, rank:]
         own_ref[...] = own
-        rest_ref[...] = rest - dot_parts(halves(own), take(factor, rank, rest.shape[1]))
+        rest_ref[...] = rest - dot_parts(halves(own), take(factor, 0, rest.shape[1]))
 
     def scatter(parts, number, stack_ref):
         own, slot = own_block(), 0
@@ -307,12 +344,7 @@
                     stack_ref[at(slot ^ own, mine), e * rank : (e + 1) * rank] = part[start : start + mine, :]
                 slot += 1
 
-    for bit in reversed(leaf_bits):
-        got = swap(late, "sub", bit)
-        late = jnp.concatenate([late[:late_rows] + got[:late_rows], late[late_rows:], got[late_rows:]], axis=0)
-    late_parts = [late, swap(late, "sub", 0)]
-
-    coarse = []
+    found = []
     for e in range(head, top):
         parts = partial_sums(rest, "rows", bits[e])
         own, rest = call(
@@ -322,86 +354,80 @@
             *factors[e],
             flops=small * (top - e),
         )
-        coarse.append(own)
-    coarse.append(rest)
+        found.append(own)
+    found.append(rest)
     if len(bits[top]) == 1 and len(leaf_bits) == 1:
         row_bit, sub_bit = bits[top][0], leaf_bits[0]
         across = swap(rest, "rows", row_bit)
-        beside = swap(jnp.concatenate(coarse, axis=0), "sub", sub_bit)
+        beside = swap(jnp.concatenate(found, axis=0), "sub", sub_bit)
         corner = swap_both(rest, row_bit, sub_bit)
-        end = (count - head - 1) * mine
-        coarse = jnp.concatenate([*coarse[:-1], rest + across, beside[:end], beside[end:] + corner], axis=0)
+        end = (coarse - 1) * mine
+        found = jnp.concatenate([*found[:-1], rest + across, beside[:end], beside[end:] + corner], axis=0)
     else:
-        coarse[-1] = add_all(partial_sums(rest, "rows", bits[top]))
-        coarse = jnp.concatenate(coarse, axis=0)
+        found[-1] = add_all(partial_sums(rest, "rows", bits[top]))
+        found = jnp.concatenate(found, axis=0)
         for bit in reversed(leaf_bits):
-            coarse = jnp.concatenate([coarse, swap(coarse, "sub", bit)], axis=0)
-    coarse_parts = [coarse, swap(coarse, "sub", 0)]
-
-    def answer_body(core_ref, *refs):
+            found = jnp.concatenate([found, swap(found, "sub", bit)], axis=0)
+    found_parts = [found, swap(found, "sub", 0)]
+
+    def answer_body(*refs):
         factor_refs, basis_refs, out_refs = paired(refs[:-4]), refs[-4:-2], refs[-2:]
-        wide = count - head
-        zero = jnp.zeros((rank, rank), FLOAT)
         rows = {}
         for f in reversed(range(count)):
-            start = 0 if f < head else rank
             if f + 1 < count:
                 stack = jnp.concatenate([rows[g] for g in range(f + 1, count)], axis=0)
-                row = -dot_parts(take(factor_refs[f], start, stack.shape[0]), halves(stack))
+                row = -dot_parts(take(factor_refs[f], 0, stack.shape[0]), halves(stack))
             else:
-                row = jnp.zeros((rank, wide * rank), FLOAT)
+                row = jnp.zeros((rank, coarse * rank), FLOAT)
             if f >= head:
-                core = core_ref[f]
-                own = core + core.T - dot_parts(take(factor_refs[f], 0, rank), halves(core))
-                pieces = [zero] * (f - head) + [own]
-                pieces += [row[:, e * rank : (e + 1) * rank] for e in range(f - head + 1, wide)]
-                row = lanes(pieces)
+                line = lax.broadcasted_iota(jnp.int32, row.shape, 0) + (f - head) * rank
+                row = row + jnp.where(line == lax.broadcasted_iota(jnp.int32, row.shape, 1), 1.0, 0.0)
             rows[f] = row
         gains = jnp.concatenate([rows[f] for f in range(count)], axis=0)
         store(out_refs, dot_parts([ref[...] for ref in basis_refs], halves(gains)))
 
     answer = call(
         answer_body,
-        pair(rows_here, (count - head) * rank),
-        cores,
+        pair(rows_here, coarse * rank),
         *flat(factors),
         *basis,
-        flops=small * (count - head) * count * rows_here // rank,
+        flops=small * coarse * count * rows_here // rank,
     )
 
     def base_body(scale_ref, queries_ref, own_ref, other_ref, core_ref, *refs):
-        factor_refs, basis_refs, scaled_refs = paired(refs[: 2 * head]), refs[2 * head : -5], refs[-5:-3]
-        out_ref, stack_ref, gram_ref = refs[-3:]
-        scatter([own_ref.at[late_rows:], other_ref.at[late_rows:]], head, stack_ref)
+        factor_refs, basis_refs, scaled_refs = paired(refs[: 2 * head]), refs[2 * head : -7], refs[-7:-5]
+        out_ref, *gain_refs, stack_ref, gram_ref = refs[-5:]
+        scatter([own_ref.at[late_size:], other_ref.at[late_size:]], head, stack_ref)
         side = core_side()
         for late_ref, place in ((own_ref, side), (other_ref, 1 - side)):
             stack_ref[at(place, columns // 2), head * rank :] = late_ref[: columns // 2]
-            for e in range(head):
+            for e in range(count):
                 start = columns // 2 + e * half
                 gram_ref[at(place, half), e * rank : (e + 1) * rank] = late_ref[start : start + half]
-        found = [None] * head
-        for e in reversed(range(head)):
-            core = core_ref[e]
-            diagonal = dot(core.T, gram_ref[:, e * rank : (e + 1) * rank])
-            moment = stack_ref[:, e * rank : (e + 1) * rank]
-            if e:
-                value = dot(moment, core + core.T - dot(diagonal, core), 1)
-            else:
-                first = dot(moment, core, 1)
-                value = dot(stack_ref[:, head * rank :], core) - dot(first, diagonal, 1)
+        products = [dot(core_ref[e].T, gram_ref[:, e * rank : (e + 1) * rank]) for e in range(count)]
+        gains = [core_ref[e] + core_ref[e].T - dot(products[e], core_ref[e]) for e in range(1, count)]
+        store(gain_refs, lanes(gains[head - 1 :]))
+        rest = stack_ref[:, : head * rank]
+        moments = []
+        for e in range(head):
+            own, rest = rest[:, :rank], rest[:, rank:]
+            moments.append(own)
             if e + 1 < head:
-                value = value - dot_parts(
-                    halves(lanes(found[e + 1 :])), take(factor_refs[e], 0, (head - 1 - e) * rank), 1
-                )
-            found[e] = value
+                rest = rest - dot_parts(halves(own), take(factor_refs[e], 0, rest.shape[1]))
+        first = dot(moments[0], core_ref[0], 1)
+        found = [dot(stack_ref[:, head * rank :], core_ref[0]) - dot(first, products[0], 1)]
+        found += [dot(moments[e], gains[e - 1], 1) for e in range(1, head)]
+        for e in reversed(range(head - 1)):
+            size = (head - 1 - e) * rank
+            found[e] = found[e] - dot_parts(halves(lanes(found[e + 1 :])), take(factor_refs[e], 0, size), 1)
         left = [lanes([a[...], b[:, : head * rank]]) for a, b in zip(scaled_refs, basis_refs)]
         square = column_scale(scale_ref[...] * scale_ref[...])
         square = lanes([square] * (columns // rank))
         out_ref[...] = square * queries_ref[...] - dot_parts(left, halves(lanes([first, *found])), 1)
 
-    (base,) = call(
+    base, *gains = call(
         base_body,
-        [(rows_here, columns)],
+        [(rows_here, columns), *pair(rank, coarse * rank)],
         scale,
         queries,
         *late_parts,
@@ -410,14 +436,19 @@
         *basis,
         *scaled,
         flops=small * 2 * (head + 1) * rows_here // rank,
-        scratch=[pltpu.VMEM((columns, (head + 1) * rank), FLOAT), pltpu.VMEM((rank, head * rank), FLOAT)],
+        scratch=[pltpu.VMEM((columns, (head + 1) * rank), FLOAT), pltpu.VMEM((rank, count * rank), FLOAT)],
     )
 
     chunk = rows_here // 4
 
-    def last_body(base_ref, high_ref, low_ref, own_ref, other_ref, out_hbm, stack_ref, out_ref, sems):
-        scatter([own_ref, other_ref], count - head, stack_ref)
-        right = halves(stack_ref[...])
+    def last_body(base_ref, high_ref, low_ref, *refs):
+        gain_refs, (own_ref, other_ref, out_hbm, stack_ref, out_ref, sems) = refs[:2], refs[2:]
+        scatter([own_ref, other_ref], coarse, stack_ref)
+        right = []
+        for e in range(coarse):
+            where = slice(e * rank, (e + 1) * rank)
+            right.append(dot_parts(halves(stack_ref[:, where]), [ref[:, where] for ref in gain_refs], 1))
+        right = halves(lanes(right))
         copies = []
         for i in range(4):
             rows = pl.ds(i * chunk, chunk)
@@ -432,11 +463,12 @@
         [(rows_here, columns)],
         base,
         *answer,
-        *coarse_parts,
-        flops=small * 2 * (count - head) * rows_here // rank,
+        *gains,
+        *found_parts,
+        flops=small * 2 * coarse * rows_here // rank,
         out_space=pltpu.HBM,
         scratch=[
-            pltpu.VMEM((columns, (count - head) * rank), FLOAT),
+            pltpu.VMEM((columns, coarse * rank), FLOAT),
             pltpu.VMEM((rows_here, columns), FLOAT),
             pltpu.SemaphoreType.DMA((4,)),
         ],

time: 45.9 us -> 39.5 us (0.86)
  waiting for transfers between devices: 17.5 us -> 10.3 us
  starting transfers between devices: 17.6 us -> 18.4 us
    ppermute x17 -> x16, waiting for transfers between devices: 16.1 us -> 10.3 us  [swap(): lax.ppermute(array, axis, [(i, i ^ 1 << bit) for i in range(lax.axis_size...]
    ppermute x1, starting transfers between devices: 0.17 us -> 1.59 us  [swap_both(): return lax.ppermute(array, ('rows', 'sub'), pairs)]
    ppermute x1, waiting for transfers between devices: 1.39 us -> 0.01 us  [swap_both(): return lax.ppermute(array, ('rows', 'sub'), pairs)]
    ppermute x17 -> x16, starting transfers between devices: 17.4 us -> 16.8 us  [swap(): lax.ppermute(array, axis, [(i, i ^ 1 << bit) for i in range(lax.axis_size...]
    pallas_call x11 -> x10, Pallas kernels: 9.5 us -> 9.44 us  [call(): pl.pallas_call(body, out_shape=outs, in_specs=[pl.BlockSpec(memory_space=...]
  transfers between devices with their start and end apart: 18 -> 17, of which waited for: 7 -> 8; matrix products, arithmetic and copies ran while one was open for 1% -> 1% of each run, Pallas kernels for 13% -> 14%
where the time goes in v6:
time: 39.5 us; the launch traced here: 39.3 us
  starting transfers between devices  18.4 us (47%)
  waiting for transfers between devices  10.3 us (26%)
  Pallas kernels  9.44 us (24%)
  local copies, waits for them, and re-layouts  0.59 us (1%)
    ppermute x16, starting transfers between devices, swap(): lax.ppermute(array, axis, [(i, i ^ 1 << bit) for i in range(lax.axis_size...  16.8 us
    ppermute x16, waiting for transfers between devices, swap(): lax.ppermute(array, axis, [(i, i ^ 1 << bit) for i in range(lax.axis_size...  10.3 us
    pallas_call x10, Pallas kernels, call(): pl.pallas_call(body, out_shape=outs, in_specs=[pl.BlockSpec(memory_space=...  9.44 us
    ppermute x1, starting transfers between devices, swap_both(): return lax.ppermute(array, ('rows', 'sub'), pairs)  1.59 us
  transfers between devices with their start and end apart: 17, of which 8 were waited for; matrix products, arithmetic and copies ran while one was open for 1% of the time, Pallas kernels for 14%

profile of v6, /device:TPU:0, one launch (start us, length us, event | category | flops | bytes accessed | tf_op | source)
XLA Modules:
  0.0 39.3 jit_solution(17621069091156103869)
XLA Ops:
  0.0 0.0 copy-start
  0.0 0.0 copy-start.2
  0.0 0.0 copy-start.3
  0.0 2.2 %shard_map.65 = (f32[128,1024]{1,0:T(8,128)S(1)}, f32[4,128,128]{2,1,0:T(8,128)S(1)}) custom-call(f32[4,128]{1,0:T(4,128)} %bitcast.1, f32[512,128]{1,0:T(8,128)} %leaf_ref.3, f32[3,512,128]{2,1,0:T(8,128)} %level_ref.3, f32[1,128,128]{2,1,0:T(8,128)} %refs_3_.1, f32[14,128,128]{2,1,0:T(8,128)} %refs_4_.1), custom_call_target="tpu_custom_call" | custom-call | flops 402653184 | bytes 2033664 | tf_op jit(solution)/shard_map/pallas_call | solution.py:64
  2.2 0.0 copy-start.1
  2.2 0.6 %collective-permute-start.1 = (f32[64,1024]{1,0:T(8,128)S(1)}, f32[64,1024]{1,0:T(8,128)S(1)}, u32[]{:S(2)}, u32[]{:S(2)}) collective-permute-start(f32[64,1024]{1,0:T(8,128)S(1)} %slice.92), channel_id=1, source_target_pairs={{0,1},{1,0},{2,3},{3,2},{4,5},{5,4},{6,7},{7,6},{8,9},{9,8},{10,11... | collective-permute-start | bytes 786440 | tf_op jit(solution)/shard_map/ppermute | solution.py:85
  2.8 0.0 copy-done
  2.8 0.0 copy-done.2
  2.8 0.0 copy-done.3
  2.8 0.4 %copy-done.1 = f32[512,256]{1,0:T(8,128)S(1)} copy-done((f32[512,256]{1,0:T(8,128)S(1)}, f32[512,256]{1,0:T(8,128)}, u32[]{:S(2)}) %copy-start.1) | copy-done | bytes 524312
  3.2 0.7 %shard_map.64 = (f32[512,128]{1,0:T(8,128)S(1)}, bf16[512,128]{1,0:T(8,128)(2,1)S(1)}, bf16[512,128]{1,0:T(8,128)(2,1)S(1)}) custom-call(f32[4,128]{1,0:T(4,128)S(1)} %bitcast.2, f32[512,256]{1,0:T(8,128)S(1)} %copy-done.1, f32[512,128]{1,0:T(8,128)S(1)} %copy-done.2, f32[3,512,128]{2,1,0:T(8,128)S(1)} %copy-done), custom_call_target="tpu_custom_call" | custom-call | flops 201326592 | bytes 1574912 | tf_op jit(solution)/shard_map/pallas_call | solution.py:64
  4.0 0.6 %collective-permute-start = (f32[256,128]{1,0:T(8,128)S(1)}, f32[256,128]{1,0:T(8,128)S(1)}, u32[]{:S(2)}, u32[]{:S(2)}) collective-permute-start(f32[256,128]{1,0:T(8,128)S(1)} %slice.90), channel_id=1, source_target_pairs={{0,1},{1,0},{2,3},{3,2},{4,5},{5,4},{6,7},{7,6},{8,9},{9,8},{10,11... | collective-permute-start | bytes 393224 | tf_op jit(solution)/shard_map/ppermute | solution.py:85
  4.6 0.8 %shard_map.66 = (f32[256,512]{1,0:T(8,128)S(1)}, bf16[512,512]{1,0:T(8,128)(2,1)S(1)}, bf16[512,512]{1,0:T(8,128)(2,1)S(1)}) custom-call(f32[4,128]{1,0:T(4,128)S(1)} %bitcast.3, f32[512,256]{1,0:T(8,128)S(1)} %copy-done.1, f32[512,128]{1,0:T(8,128)S(1)} %copy-done.2, f32[3,512,128]{2,1,0:T(8,128)S(1)} %copy-done), custom_call_target="tpu_custom_call" | custom-call | flops 402653184 | bytes 1574912 | tf_op jit(solution)/shard_map/pallas_call | solution.py:64
  5.4 0.1 collective-permute-start.4
  5.5 0.0 collective-permute-done.1
  5.5 3.1 %collective-permute-start.2 = (f32[64,128]{1,0:T(8,128)S(1)}, f32[64,128]{1,0:T(8,128)S(1)}, u32[]{:S(2)}, u32[]{:S(2)}) collective-permute-start(f32[64,128]{1,0:T(8,128)S(1)} %slice.115), channel_id=1, source_target_pairs={{0,8},{4,12},{8,0},{12,4},{16,24},{20,28},{24,16},{28,20},{1,9},{5... | collective-permute-start | bytes 98312 | tf_op jit(solution)/shard_map/ppermute | solution.py:85
  8.6 0.0 collective-permute-done
  8.7 1.6 %collective-permute-start.8 = (f32[64,768]{1,0:T(8,128)S(1)}, f32[64,768]{1,0:T(8,128)S(1)}, u32[]{:S(2)}, u32[]{:S(2)}) collective-permute-start(f32[64,768]{1,0:T(8,128)S(1)} %slice.128), channel_id=1, source_target_pairs={{0,2},{1,3},{2,0},{3,1},{4,6},{5,7},{6,4},{7,5},{8,10},{9,11},{10,... | collective-permute-start | bytes 589832 | tf_op jit(solution)/shard_map/ppermute | solution.py:85
  10.3 0.3 collective-permute-done.2
  10.6 2.0 %collective-permute-start.3 = (f32[64,256]{1,0:T(8,128)S(1)}, f32[64,256]{1,0:T(8,128)S(1)}, u32[]{:S(2)}, u32[]{:S(2)}) collective-permute-start(f32[64,256]{1,0:T(8,128)S(1)} %pad_maximum_fusion.2), channel_id=1, source_target_pairs={{0,4},{4,0},{8,12},{12,8},{16,20},{20,16},{24,28},{28,24},{1,5},{5... | collective-permute-start | bytes 196616 | tf_op jit(solution)/shard_map/ppermute | solution.py:85
  12.6 0.0 collective-permute-done.4
  12.6 1.6 %collective-permute-start.6 = (f32[64,512]{1,0:T(8,128)S(1)}, f32[64,512]{1,0:T(8,128)S(1)}, u32[]{:S(2)}, u32[]{:S(2)}) collective-permute-start(f32[64,512]{1,0:T(8,128)S(1)} %slice.122), channel_id=1, source_target_pairs={{0,2},{1,3},{2,0},{3,1},{4,6},{5,7},{6,4},{7,5},{8,10},{9,11},{10,... | collective-permute-start | bytes 393224 | tf_op jit(solution)/shard_map/ppermute | solution.py:85
  14.2 0.7 %collective-permute-done.3 = f32[64,256]{1,0:T(8,128)S(1)} collective-permute-done((f32[64,256]{1,0:T(8,128)S(1)}, f32[64,256]{1,0:T(8,128)S(1)}, u32[]{:S(2)}, u32[]{:S(2)}) %collective-permute-start.3) | collective-permute-done | bytes 65568 | tf_op jit(solution)/shard_map/ppermute | solution.py:85
  15.0 2.0 %collective-permute-start.5 = (f32[512,128]{1,0:T(8,128)S(1)}, f32[512,128]{1,0:T(8,128)S(1)}, u32[]{:S(2)}, u32[]{:S(2)}) collective-permute-start(f32[512,128]{1,0:T(8,128)S(1)} %get-tuple-element.53), channel_id=1, source_target_pairs={{0,2},{1,3},{2,0},{3,1},{4,6},{5,7},{6,4},{7,5},{8,10},{9,11},{10,... | collective-permute-start | bytes 786440 | tf_op jit(solution)/shard_map/ppermute | solution.py:85
  17.0 0.0 collective-permute-done.8
  17.0 1.6 %collective-permute-start.10 = (f32[64,128]{1,0:T(8,128)S(1)}, f32[64,128]{1,0:T(8,128)S(1)}, u32[]{:S(2)}, u32[]{:S(2)}) collective-permute-start(f32[64,128]{1,0:T(8,128)S(1)} %slice.130), channel_id=1, source_target_pairs={{0,4},{4,0},{8,12},{12,8},{16,20},{20,16},{24,28},{28,24},{1,5},{5... | collective-permute-start | bytes 98312 | tf_op jit(solution)/shard_map/ppermute | solution.py:85
  18.6 0.7 %collective-permute-done.6.refs_1_ = f32[64,512]{1,0:T(8,128)S(1)} collective-permute-done((f32[64,512]{1,0:T(8,128)S(1)}, f32[64,512]{1,0:T(8,128)S(1)}, u32[]{:S(2)}, u32[]{:S(2)}) %collective-permute-start.6) | collective-permute-done | bytes 131104 | tf_op jit(solution)/shard_map/ppermute | solution.py:85
  19.4 0.1 collective-permute-start.9
  19.5 1.6 %collective-permute-done.10 = f32[64,128]{1,0:T(8,128)S(1)} collective-permute-done((f32[64,128]{1,0:T(8,128)S(1)}, f32[64,128]{1,0:T(8,128)S(1)}, u32[]{:S(2)}, u32[]{:S(2)}) %collective-permute-start.10) | collective-permute-done | bytes 32800 | tf_op jit(solution)/shard_map/ppermute | solution.py:85
  21.0 0.0 collective-permute-start.11
  21.1 1.2 %collective-permute-done.11.other_ref = f32[64,128]{1,0:T(8,128)S(1)} collective-permute-done((f32[64,128]{1,0:T(8,128)S(1)}, f32[64,128]{1,0:T(8,128)S(1)}, u32[]{:S(2)}, u32[]{:S(2)}) %collective-permute-start.11) | collective-permute-done | bytes 32800 | tf_op jit(solution)/shard_map/ppermute | solution.py:85
  22.2 0.2 shard_map.69
  22.5 0.0 collective-permute-done.9.other_ref
  22.5 0.4 shard_map.67
  22.9 0.4 shard_map.71.refs_0_
  23.2 1.6 %collective-permute-start.12 = (f32[64,256]{1,0:T(8,128)S(1)}, f32[64,256]{1,0:T(8,128)S(1)}, u32[]{:S(2)}, u32[]{:S(2)}) collective-permute-start(f32[64,256]{1,0:T(8,128)S(1)} %shard_map.71.refs_0_), channel_id=1, source_target_pairs={{0,4},{4,0},{8,12},{12,8},{16,20},{20,16},{24,28},{28,24},{1,5},{5... | collective-permute-start | bytes 196616 | tf_op jit(solution)/shard_map/ppermute | solution.py:85
  24.8 0.0 collective-permute-done.5
  24.8 2.7 %collective-permute-done.12.refs_1_ = f32[64,256]{1,0:T(8,128)S(1)} collective-permute-done((f32[64,256]{1,0:T(8,128)S(1)}, f32[64,256]{1,0:T(8,128)S(1)}, u32[]{:S(2)}, u32[]{:S(2)}) %collective-permute-start.12) | collective-permute-done | bytes 65568 | tf_op jit(solution)/shard_map/ppermute | solution.py:85
  27.6 0.1 shard_map.72
  27.7 1.6 %collective-permute-start.15 = (f32[64,128]{1,0:T(8,128)S(1)}, f32[64,128]{1,0:T(8,128)S(1)}, u32[]{:S(2)}, u32[]{:S(2)}) collective-permute-start(f32[64,128]{1,0:T(8,128)S(1)} %get-tuple-element.46), channel_id=1, source_target_pairs={{0,10},{1,11},{2,8},{3,9},{4,14},{5,15},{6,12},{7,13},{8,2},{9,3},... | collective-permute-start | bytes 98312 | tf_op jit(solution)/shard_map/ppermute | solution.py:92
  29.3 1.0 %collective-permute-start.13 = (f32[64,128]{1,0:T(8,128)S(1)}, f32[64,128]{1,0:T(8,128)S(1)}, u32[]{:S(2)}, u32[]{:S(2)}) collective-permute-start(f32[64,128]{1,0:T(8,128)S(1)} %get-tuple-element.46), channel_id=1, source_target_pairs={{0,8},{4,12},{8,0},{12,4},{16,24},{20,28},{24,16},{28,20},{1,9},{5... | collective-permute-start | bytes 98312 | tf_op jit(solution)/shard_map/ppermute | solution.py:85
  30.3 1.0 %collective-permute-start.14 = (f32[128,128]{1,0:T(8,128)S(1)}, f32[128,128]{1,0:T(8,128)S(1)}, u32[]{:S(2)}, u32[]{:S(2)}) collective-permute-start(f32[128,128]{1,0:T(8,128)S(1)} %pad_maximum_fusion.3), channel_id=1, source_target_pairs={{0,2},{1,3},{2,0},{3,1},{4,6},{5,7},{6,4},{7,5},{8,10},{9,11},{10,... | collective-permute-start | bytes 196616 | tf_op jit(solution)/shard_map/ppermute | solution.py:85
  31.3 0.1 collective-permute-start.7
  31.4 1.8 %collective-permute-done.13 = f32[64,128]{1,0:T(8,128)S(1)} collective-permute-done((f32[64,128]{1,0:T(8,128)S(1)}, f32[64,128]{1,0:T(8,128)S(1)}, u32[]{:S(2)}, u32[]{:S(2)}) %collective-permute-start.13) | collective-permute-done | bytes 32800 | tf_op jit(solution)/shard_map/ppermute | solution.py:85
  33.2 0.0 collective-permute-done.15
  33.2 1.3 %collective-permute-done.14 = f32[128,128]{1,0:T(8,128)S(1)} collective-permute-done((f32[128,128]{1,0:T(8,128)S(1)}, f32[128,128]{1,0:T(8,128)S(1)}, u32[]{:S(2)}, u32[]{:S(2)}) %collective-permute-start.14) | collective-permute-done | bytes 65568 | tf_op jit(solution)/shard_map/ppermute | solution.py:85
  34.6 0.1 collective-permute-start.16
  34.7 1.5 %shard_map.70 = (bf16[512,256]{1,0:T(8,128)(2,1)S(1)}, bf16[512,256]{1,0:T(8,128)(2,1)S(1)}) custom-call(bf16[128,384]{1,0:T(8,128)(2,1)S(1)} %get-tuple-element.30.refs_0_.refs_2_, bf16[128,384]{1,0:T(8,128)(2,1)S(1)} %get-tuple-element.31.refs_1_.refs_3_, bf16[128,256]{1,0:T(8,128)(2,1)S(1)} %get-tuple-element.32.refs_2_.refs_4_, ...), custom_call_target="tpu_custom_call" | custom-call | flops 402653184 | bytes 1441792 | tf_op jit(solution)/shard_map/pallas_call | solution.py:64
  36.1 0.0 collective-permute-done.7.other_ref
  36.2 1.5 %shard_map.68 = (f32[512,256]{1,0:T(8,128)S(1)}, bf16[128,256]{1,0:T(8,128)(2,1)S(1)}, bf16[128,256]{1,0:T(8,128)(2,1)S(1)}) custom-call(f32[4,128]{1,0:T(4,128)S(1)} %bitcast.4, f32[512,256]{1,0:T(8,128)S(1)} %copy-done.1, f32[640,128]{1,0:T(8,128)S(1)} %pad_maximum_fusion.own_ref, f32[640,128]{1,0:T(8,128)S(1)} %collective-permute-done.7.other_ref, ...), custom_call_target="tpu_custom_call" | custom-call | flops 301989888 | bytes 3082240 | tf_op jit(solution)/shard_map/pallas_call | solution.py:64
  37.7 0.0 collective-permute-done.16.refs_3_
  37.7 1.6 %shard_map.73 = f32[512,256]{1,0:T(8,128)} custom-call(f32[512,256]{1,0:T(8,128)S(1)} %get-tuple-element.38.base_ref, bf16[512,256]{1,0:T(8,128)(2,1)S(1)} %get-tuple-element.41.high_ref, bf16[512,256]{1,0:T(8,128)(2,1)S(1)} %get-tuple-element.42.low_ref, bf16[128,256]{1,0:T(8,128)(2,1)S(1)} %get-tuple-element.43.refs_0_, ...), custom_call_target="tpu_custom_call" | custom-call | flops 201326592 | bytes 1441792 | tf_op jit(solution)/shard_map/pallas_call | solution.py:64
  (29 shorter events, 0.4 us)
Async XLA Ops:
  0.0 2.8 %copy-start = (f32[3,512,128]{2,1,0:T(8,128)S(1)}, f32[3,512,128]{2,1,0:T(8,128)}, u32[]{:S(2)}) copy-start(f32[3,512,128]{2,1,0:T(8,128)} %level_ref.3) | copy-start | bytes 2359300
  0.0 2.8 %copy-start.2 = (f32[512,128]{1,0:T(8,128)S(1)}, f32[512,128]{1,0:T(8,128)}, u32[]{:S(2)}) copy-start(f32[512,128]{1,0:T(8,128)} %leaf_ref.3) | copy-start | bytes 786436
  0.0 2.8 %copy-start.3 = (f32[512]{0:T(512)S(1)}, f32[512]{0:T(512)}, u32[]{:S(2)}) copy-start(f32[512]{0:T(512)} %param.7) | copy-start | bytes 6148
  2.2 1.0 %copy-start.1 = (f32[512,256]{1,0:T(8,128)S(1)}, f32[512,256]{1,0:T(8,128)}, u32[]{:S(2)}) copy-start(f32[512,256]{1,0:T(8,128)} %queries_ref.5) | copy-start | bytes 1572868
  2.2 3.2 %collective-permute-start.1 = (f32[64,1024]{1,0:T(8,128)S(1)}, f32[64,1024]{1,0:T(8,128)S(1)}, u32[]{:S(2)}, u32[]{:S(2)}) collective-permute-start(f32[64,1024]{1,0:T(8,128)S(1)} %slice.92), channel_id=1, source_target_pairs={{0,1},{1,0},{2,3},{3,2},{4,5},{5,4},{6,7},{7,6},{8,9},{9,8},{10,11... | collective-permute-start | bytes 786440 | tf_op jit(solution)/shard_map/ppermute | solution.py:85
  4.0 4.6 %collective-permute-start = (f32[256,128]{1,0:T(8,128)S(1)}, f32[256,128]{1,0:T(8,128)S(1)}, u32[]{:S(2)}, u32[]{:S(2)}) collective-permute-start(f32[256,128]{1,0:T(8,128)S(1)} %slice.90), channel_id=1, source_target_pairs={{0,1},{1,0},{2,3},{3,2},{4,5},{5,4},{6,7},{7,6},{8,9},{9,8},{10,11... | collective-permute-start | bytes 393224 | tf_op jit(solution)/shard_map/ppermute | solution.py:85
  5.4 7.2 %collective-permute-start.4 = (f32[128,512]{1,0:T(8,128)S(1)}, f32[128,512]{1,0:T(8,128)S(1)}, u32[]{:S(2)}, u32[]{:S(2)}) collective-permute-start(f32[128,512]{1,0:T(8,128)S(1)} %slice.98), channel_id=1, source_target_pairs={{0,1},{1,0},{2,3},{3,2},{4,5},{5,4},{6,7},{7,6},{8,9},{9,8},{10,11... | collective-permute-start | bytes 786440 | tf_op jit(solution)/shard_map/ppermute | solution.py:85
  5.5 5.0 %collective-permute-start.2 = (f32[64,128]{1,0:T(8,128)S(1)}, f32[64,128]{1,0:T(8,128)S(1)}, u32[]{:S(2)}, u32[]{:S(2)}) collective-permute-start(f32[64,128]{1,0:T(8,128)S(1)} %slice.115), channel_id=1, source_target_pairs={{0,8},{4,12},{8,0},{12,4},{16,24},{20,28},{24,16},{28,20},{1,9},{5... | collective-permute-start | bytes 98312 | tf_op jit(solution)/shard_map/ppermute | solution.py:85
  8.7 8.3 %collective-permute-start.8 = (f32[64,768]{1,0:T(8,128)S(1)}, f32[64,768]{1,0:T(8,128)S(1)}, u32[]{:S(2)}, u32[]{:S(2)}) collective-permute-start(f32[64,768]{1,0:T(8,128)S(1)} %slice.128), channel_id=1, source_target_pairs={{0,2},{1,3},{2,0},{3,1},{4,6},{5,7},{6,4},{7,5},{8,10},{9,11},{10,... | collective-permute-start | bytes 589832 | tf_op jit(solution)/shard_map/ppermute | solution.py:85
  10.6 4.3 %collective-permute-start.3 = (f32[64,256]{1,0:T(8,128)S(1)}, f32[64,256]{1,0:T(8,128)S(1)}, u32[]{:S(2)}, u32[]{:S(2)}) collective-permute-start(f32[64,256]{1,0:T(8,128)S(1)} %pad_maximum_fusion.2), channel_id=1, source_target_pairs={{0,4},{4,0},{8,12},{12,8},{16,20},{20,16},{24,28},{28,24},{1,5},{5... | collective-permute-start | bytes 196616 | tf_op jit(solution)/shard_map/ppermute | solution.py:85
  12.6 6.7 %collective-permute-start.6 = (f32[64,512]{1,0:T(8,128)S(1)}, f32[64,512]{1,0:T(8,128)S(1)}, u32[]{:S(2)}, u32[]{:S(2)}) collective-permute-start(f32[64,512]{1,0:T(8,128)S(1)} %slice.122), channel_id=1, source_target_pairs={{0,2},{1,3},{2,0},{3,1},{4,6},{5,7},{6,4},{7,5},{8,10},{9,11},{10,... | collective-permute-start | bytes 393224 | tf_op jit(solution)/shard_map/ppermute | solution.py:85
  15.0 9.8 %collective-permute-start.5 = (f32[512,128]{1,0:T(8,128)S(1)}, f32[512,128]{1,0:T(8,128)S(1)}, u32[]{:S(2)}, u32[]{:S(2)}) collective-permute-start(f32[512,128]{1,0:T(8,128)S(1)} %get-tuple-element.53), channel_id=1, source_target_pairs={{0,2},{1,3},{2,0},{3,1},{4,6},{5,7},{6,4},{7,5},{8,10},{9,11},{10,... | collective-permute-start | bytes 786440 | tf_op jit(solution)/shard_map/ppermute | solution.py:85
  17.0 4.0 %collective-permute-start.10 = (f32[64,128]{1,0:T(8,128)S(1)}, f32[64,128]{1,0:T(8,128)S(1)}, u32[]{:S(2)}, u32[]{:S(2)}) collective-permute-start(f32[64,128]{1,0:T(8,128)S(1)} %slice.130), channel_id=1, source_target_pairs={{0,4},{4,0},{8,12},{12,8},{16,20},{20,16},{24,28},{28,24},{1,5},{5... | collective-permute-start | bytes 98312 | tf_op jit(solution)/shard_map/ppermute | solution.py:85
  19.4 3.1 %collective-permute-start.9 = (f32[64,640]{1,0:T(8,128)S(1)}, f32[64,640]{1,0:T(8,128)S(1)}, u32[]{:S(2)}, u32[]{:S(2)}) collective-permute-start(f32[64,640]{1,0:T(8,128)S(1)} %slice.129.own_ref), channel_id=1, source_target_pairs={{0,1},{1,0},{2,3},{3,2},{4,5},{5,4},{6,7},{7,6},{8,9},{9,8},{10,11... | collective-permute-start | bytes 491528 | tf_op jit(solution)/shard_map/ppermute | solution.py:85
  21.0 1.2 %collective-permute-start.11 = (f32[64,128]{1,0:T(8,128)S(1)}, f32[64,128]{1,0:T(8,128)S(1)}, u32[]{:S(2)}, u32[]{:S(2)}) collective-permute-start(f32[64,128]{1,0:T(8,128)S(1)} %slice_add_fusion.6.own_ref), channel_id=1, source_target_pairs={{0,1},{1,0},{2,3},{3,2},{4,5},{5,4},{6,7},{7,6},{8,9},{9,8},{10,11... | collective-permute-start | bytes 98312 | tf_op jit(solution)/shard_map/ppermute | solution.py:85
  23.2 4.3 %collective-permute-start.12 = (f32[64,256]{1,0:T(8,128)S(1)}, f32[64,256]{1,0:T(8,128)S(1)}, u32[]{:S(2)}, u32[]{:S(2)}) collective-permute-start(f32[64,256]{1,0:T(8,128)S(1)} %shard_map.71.refs_0_), channel_id=1, source_target_pairs={{0,4},{4,0},{8,12},{12,8},{16,20},{20,16},{24,28},{28,24},{1,5},{5... | collective-permute-start | bytes 196616 | tf_op jit(solution)/shard_map/ppermute | solution.py:85
  27.7 5.5 %collective-permute-start.15 = (f32[64,128]{1,0:T(8,128)S(1)}, f32[64,128]{1,0:T(8,128)S(1)}, u32[]{:S(2)}, u32[]{:S(2)}) collective-permute-start(f32[64,128]{1,0:T(8,128)S(1)} %get-tuple-element.46), channel_id=1, source_target_pairs={{0,10},{1,11},{2,8},{3,9},{4,14},{5,15},{6,12},{7,13},{8,2},{9,3},... | collective-permute-start | bytes 98312 | tf_op jit(solution)/shard_map/ppermute | solution.py:92
  29.3 3.9 %collective-permute-start.13 = (f32[64,128]{1,0:T(8,128)S(1)}, f32[64,128]{1,0:T(8,128)S(1)}, u32[]{:S(2)}, u32[]{:S(2)}) collective-permute-start(f32[64,128]{1,0:T(8,128)S(1)} %get-tuple-element.46), channel_id=1, source_target_pairs={{0,8},{4,12},{8,0},{12,4},{16,24},{20,28},{24,16},{28,20},{1,9},{5... | collective-permute-start | bytes 98312 | tf_op jit(solution)/shard_map/ppermute | solution.py:85
  30.3 4.3 %collective-permute-start.14 = (f32[128,128]{1,0:T(8,128)S(1)}, f32[128,128]{1,0:T(8,128)S(1)}, u32[]{:S(2)}, u32[]{:S(2)}) collective-permute-start(f32[128,128]{1,0:T(8,128)S(1)} %pad_maximum_fusion.3), channel_id=1, source_target_pairs={{0,2},{1,3},{2,0},{3,1},{4,6},{5,7},{6,4},{7,5},{8,10},{9,11},{10,... | collective-permute-start | bytes 196616 | tf_op jit(solution)/shard_map/ppermute | solution.py:85
  31.3 4.9 %collective-permute-start.7 = (f32[640,128]{1,0:T(8,128)S(1)}, f32[640,128]{1,0:T(8,128)S(1)}, u32[]{:S(2)}, u32[]{:S(2)}) collective-permute-start(f32[640,128]{1,0:T(8,128)S(1)} %pad_maximum_fusion.own_ref), channel_id=1, source_target_pairs={{0,1},{1,0},{2,3},{3,2},{4,5},{5,4},{6,7},{7,6},{8,9},{9,8},{10,11... | collective-permute-start | bytes 983048 | tf_op jit(solution)/shard_map/ppermute | solution.py:85
  34.6 3.1 %collective-permute-start.16 = (f32[256,128]{1,0:T(8,128)S(1)}, f32[256,128]{1,0:T(8,128)S(1)}, u32[]{:S(2)}, u32[]{:S(2)}) collective-permute-start(f32[256,128]{1,0:T(8,128)S(1)} %pad_maximum_fusion.1.refs_2_), channel_id=1, source_target_pairs={{0,1},{1,0},{2,3},{3,2},{4,5},{5,4},{6,7},{7,6},{8,9},{9,8},{10,11... | collective-permute-start | bytes 393224 | tf_op jit(solution)/shard_map/ppermute | solution.py:85

commit v7 on v6

--- a/solution.py
+++ b/solution.py
@@ -83,13 +83,6 @@
 
 def swap(array, axis, bit):
     return lax.ppermute(array, axis, [(i, i ^ 1 << bit) for i in range(lax.axis_size(axis))])
-
-
-def swap_both(array, row_bit, sub_bit):
-    sub = lax.axis_size("sub")
-    mask = (1 << row_bit) * sub + (1 << sub_bit)
-    pairs = [(i, i ^ mask) for i in range(lax.axis_size("rows") * sub)]
-    return lax.ppermute(array, ("rows", "sub"), pairs)
 
 
 def partial_sums(array, axis, bits):
@@ -356,18 +349,10 @@
         )
         found.append(own)
     found.append(rest)
-    if len(bits[top]) == 1 and len(leaf_bits) == 1:
-        row_bit, sub_bit = bits[top][0], leaf_bits[0]
-        across = swap(rest, "rows", row_bit)
-        beside = swap(jnp.concatenate(found, axis=0), "sub", sub_bit)
-        corner = swap_both(rest, row_bit, sub_bit)
-        end = (coarse - 1) * mine
-        found = jnp.concatenate([*found[:-1], rest + across, beside[:end], beside[end:] + corner], axis=0)
-    else:
-        found[-1] = add_all(partial_sums(rest, "rows", bits[top]))
-        found = jnp.concatenate(found, axis=0)
-        for bit in reversed(leaf_bits):
-            found = jnp.concatenate([found, swap(found, "sub", bit)], axis=0)
+    found[-1] = add_all(partial_sums(rest, "rows", bits[top]))
+    found = jnp.concatenate(found, axis=0)
+    for bit in reversed(leaf_bits):
+        found = jnp.concatenate([found, swap(found, "sub", bit)], axis=0)
     found_parts = [found, swap(found, "sub", 0)]
 
     def answer_body(*refs):

time: 39.5 us -> 41 us (1.038)
  waiting for transfers between devices: 10.3 us -> 12.6 us
  starting transfers between devices: 18.4 us -> 17.6 us
    ppermute x16, waiting for transfers between devices: 10.3 us -> 12.6 us  [swap(): lax.ppermute(array, axis, [(i, i ^ 1 << bit) for i in range(lax.axis_size...]
    ppermute x1 -> x0, starting transfers between devices: 1.59 us -> none  [swap_both(): return lax.ppermute(array, ('rows', 'sub'), pairs)]
    ppermute x16, starting transfers between devices: 16.8 us -> 17.6 us  [swap(): lax.ppermute(array, axis, [(i, i ^ 1 << bit) for i in range(lax.axis_size...]
  transfers between devices with their start and end apart: 17 -> 16, of which waited for: 8 -> 8; matrix products, arithmetic and copies ran while one was open for 1% -> 1% of each run, Pallas kernels for 14% -> 13%
where the time goes in v7:
time: 41 us; the launch traced here: 40.8 us
  starting transfers between devices  17.6 us (43%)
  waiting for transfers between devices  12.6 us (31%)
  Pallas kernels  9.45 us (23%)
  local copies, waits for them, and re-layouts  0.59 us (1%)
    ppermute x16, starting transfers between devices, swap(): lax.ppermute(array, axis, [(i, i ^ 1 << bit) for i in range(lax.axis_size...  17.6 us
    ppermute x16, waiting for transfers between devices, swap(): lax.ppermute(array, axis, [(i, i ^ 1 << bit) for i in range(lax.axis_size...  12.6 us
    pallas_call x10, Pallas kernels, call(): pl.pallas_call(body, out_shape=outs, in_specs=[pl.BlockSpec(memory_space=...  9.45 us
  transfers between devices with their start and end apart: 16, of which 8 were waited for; matrix products, arithmetic and copies ran while one was open for 1% of the time, Pallas kernels for 13%

profile of v7, /device:TPU:0, one launch (start us, length us, event | category | flops | bytes accessed | tf_op | source)
XLA Modules:
  0.0 40.8 jit_solution(12522193109129139206)
XLA Ops:
  0.0 0.0 copy-start
  0.0 0.0 copy-start.2
  0.0 0.0 copy-start.3
  0.0 2.2 %shard_map.65 = (f32[128,1024]{1,0:T(8,128)S(1)}, f32[4,128,128]{2,1,0:T(8,128)S(1)}) custom-call(f32[4,128]{1,0:T(4,128)} %bitcast.1, f32[512,128]{1,0:T(8,128)} %leaf_ref.3, f32[3,512,128]{2,1,0:T(8,128)} %level_ref.3, f32[1,128,128]{2,1,0:T(8,128)} %refs_3_.1, f32[14,128,128]{2,1,0:T(8,128)} %refs_4_.1), custom_call_target="tpu_custom_call" | custom-call | flops 402653184 | bytes 2033664 | tf_op jit(solution)/shard_map/pallas_call | solution.py:64
  2.2 0.0 copy-start.1
  2.2 0.6 %collective-permute-start.1 = (f32[64,1024]{1,0:T(8,128)S(1)}, f32[64,1024]{1,0:T(8,128)S(1)}, u32[]{:S(2)}, u32[]{:S(2)}) collective-permute-start(f32[64,1024]{1,0:T(8,128)S(1)} %slice.86), channel_id=1, source_target_pairs={{0,1},{1,0},{2,3},{3,2},{4,5},{5,4},{6,7},{7,6},{8,9},{9,8},{10,11... | collective-permute-start | bytes 786440 | tf_op jit(solution)/shard_map/ppermute | solution.py:85
  2.8 0.0 copy-done
  2.8 0.0 copy-done.2
  2.8 0.0 copy-done.3
  2.8 0.4 %copy-done.1 = f32[512,256]{1,0:T(8,128)S(1)} copy-done((f32[512,256]{1,0:T(8,128)S(1)}, f32[512,256]{1,0:T(8,128)}, u32[]{:S(2)}) %copy-start.1) | copy-done | bytes 524312
  3.2 0.7 %shard_map.64 = (f32[512,128]{1,0:T(8,128)S(1)}, bf16[512,128]{1,0:T(8,128)(2,1)S(1)}, bf16[512,128]{1,0:T(8,128)(2,1)S(1)}) custom-call(f32[4,128]{1,0:T(4,128)S(1)} %bitcast.2, f32[512,256]{1,0:T(8,128)S(1)} %copy-done.1, f32[512,128]{1,0:T(8,128)S(1)} %copy-done.2, f32[3,512,128]{2,1,0:T(8,128)S(1)} %copy-done), custom_call_target="tpu_custom_call" | custom-call | flops 201326592 | bytes 1574912 | tf_op jit(solution)/shard_map/pallas_call | solution.py:64
  4.0 0.6 %collective-permute-start = (f32[256,128]{1,0:T(8,128)S(1)}, f32[256,128]{1,0:T(8,128)S(1)}, u32[]{:S(2)}, u32[]{:S(2)}) collective-permute-start(f32[256,128]{1,0:T(8,128)S(1)} %slice.84), channel_id=1, source_target_pairs={{0,1},{1,0},{2,3},{3,2},{4,5},{5,4},{6,7},{7,6},{8,9},{9,8},{10,11... | collective-permute-start | bytes 393224 | tf_op jit(solution)/shard_map/ppermute | solution.py:85
  4.6 0.8 %shard_map.66 = (f32[256,512]{1,0:T(8,128)S(1)}, bf16[512,512]{1,0:T(8,128)(2,1)S(1)}, bf16[512,512]{1,0:T(8,128)(2,1)S(1)}) custom-call(f32[4,128]{1,0:T(4,128)S(1)} %bitcast.3, f32[512,256]{1,0:T(8,128)S(1)} %copy-done.1, f32[512,128]{1,0:T(8,128)S(1)} %copy-done.2, f32[3,512,128]{2,1,0:T(8,128)S(1)} %copy-done), custom_call_target="tpu_custom_call" | custom-call | flops 402653184 | bytes 1574912 | tf_op jit(solution)/shard_map/pallas_call | solution.py:64
  5.4 0.1 collective-permute-start.4
  5.5 0.0 collective-permute-done.1
  5.5 3.1 %collective-permute-start.2 = (f32[64,128]{1,0:T(8,128)S(1)}, f32[64,128]{1,0:T(8,128)S(1)}, u32[]{:S(2)}, u32[]{:S(2)}) collective-permute-start(f32[64,128]{1,0:T(8,128)S(1)} %slice.107), channel_id=1, source_target_pairs={{0,8},{4,12},{8,0},{12,4},{16,24},{20,28},{24,16},{28,20},{1,9},{5... | collective-permute-start | bytes 98312 | tf_op jit(solution)/shard_map/ppermute | solution.py:85
  8.6 0.0 collective-permute-done
  8.7 1.6 %collective-permute-start.8 = (f32[64,768]{1,0:T(8,128)S(1)}, f32[64,768]{1,0:T(8,128)S(1)}, u32[]{:S(2)}, u32[]{:S(2)}) collective-permute-start(f32[64,768]{1,0:T(8,128)S(1)} %slice.120), channel_id=1, source_target_pairs={{0,2},{1,3},{2,0},{3,1},{4,6},{5,7},{6,4},{7,5},{8,10},{9,11},{10,... | collective-permute-start | bytes 589832 | tf_op jit(solution)/shard_map/ppermute | solution.py:85
  10.3 0.3 collective-permute-done.2
  10.6 2.0 %collective-permute-start.3 = (f32[64,256]{1,0:T(8,128)S(1)}, f32[64,256]{1,0:T(8,128)S(1)}, u32[]{:S(2)}, u32[]{:S(2)}) collective-permute-start(f32[64,256]{1,0:T(8,128)S(1)} %pad_maximum_fusion.2), channel_id=1, source_target_pairs={{0,4},{4,0},{8,12},{12,8},{16,20},{20,16},{24,28},{28,24},{1,5},{5... | collective-permute-start | bytes 196616 | tf_op jit(solution)/shard_map/ppermute | solution.py:85
  12.6 0.0 collective-permute-done.4
  12.6 1.6 %collective-permute-start.6 = (f32[64,512]{1,0:T(8,128)S(1)}, f32[64,512]{1,0:T(8,128)S(1)}, u32[]{:S(2)}, u32[]{:S(2)}) collective-permute-start(f32[64,512]{1,0:T(8,128)S(1)} %slice.114), channel_id=1, source_target_pairs={{0,2},{1,3},{2,0},{3,1},{4,6},{5,7},{6,4},{7,5},{8,10},{9,11},{10,... | collective-permute-start | bytes 393224 | tf_op jit(solution)/shard_map/ppermute | solution.py:85
  14.2 0.7 %collective-permute-done.3 = f32[64,256]{1,0:T(8,128)S(1)} collective-permute-done((f32[64,256]{1,0:T(8,128)S(1)}, f32[64,256]{1,0:T(8,128)S(1)}, u32[]{:S(2)}, u32[]{:S(2)}) %collective-permute-start.3) | collective-permute-done | bytes 65568 | tf_op jit(solution)/shard_map/ppermute | solution.py:85
  15.0 2.0 %collective-permute-start.5 = (f32[512,128]{1,0:T(8,128)S(1)}, f32[512,128]{1,0:T(8,128)S(1)}, u32[]{:S(2)}, u32[]{:S(2)}) collective-permute-start(f32[512,128]{1,0:T(8,128)S(1)} %get-tuple-element.53), channel_id=1, source_target_pairs={{0,2},{1,3},{2,0},{3,1},{4,6},{5,7},{6,4},{7,5},{8,10},{9,11},{10,... | collective-permute-start | bytes 786440 | tf_op jit(solution)/shard_map/ppermute | solution.py:85
  17.0 0.0 collective-permute-done.8
  17.0 1.6 %collective-permute-start.10 = (f32[64,128]{1,0:T(8,128)S(1)}, f32[64,128]{1,0:T(8,128)S(1)}, u32[]{:S(2)}, u32[]{:S(2)}) collective-permute-start(f32[64,128]{1,0:T(8,128)S(1)} %slice.122), channel_id=1, source_target_pairs={{0,4},{4,0},{8,12},{12,8},{16,20},{20,16},{24,28},{28,24},{1,5},{5... | collective-permute-start | bytes 98312 | tf_op jit(solution)/shard_map/ppermute | solution.py:85
  18.6 0.7 %collective-permute-done.6.refs_1_ = f32[64,512]{1,0:T(8,128)S(1)} collective-permute-done((f32[64,512]{1,0:T(8,128)S(1)}, f32[64,512]{1,0:T(8,128)S(1)}, u32[]{:S(2)}, u32[]{:S(2)}) %collective-permute-start.6) | collective-permute-done | bytes 131104 | tf_op jit(solution)/shard_map/ppermute | solution.py:85
  19.4 0.1 collective-permute-start.9
  19.5 1.6 %collective-permute-done.10 = f32[64,128]{1,0:T(8,128)S(1)} collective-permute-done((f32[64,128]{1,0:T(8,128)S(1)}, f32[64,128]{1,0:T(8,128)S(1)}, u32[]{:S(2)}, u32[]{:S(2)}) %collective-permute-start.10) | collective-permute-done | bytes 32800 | tf_op jit(solution)/shard_map/ppermute | solution.py:85
  21.0 0.0 collective-permute-start.11
  21.1 1.2 %collective-permute-done.11.other_ref = f32[64,128]{1,0:T(8,128)S(1)} collective-permute-done((f32[64,128]{1,0:T(8,128)S(1)}, f32[64,128]{1,0:T(8,128)S(1)}, u32[]{:S(2)}, u32[]{:S(2)}) %collective-permute-start.11) | collective-permute-done | bytes 32800 | tf_op jit(solution)/shard_map/ppermute | solution.py:85
  22.2 0.2 shard_map.69
  22.5 0.0 collective-permute-done.9.other_ref
  22.5 0.4 shard_map.67
  22.9 0.4 shard_map.71.refs_0_
  23.2 1.6 %collective-permute-start.12 = (f32[64,256]{1,0:T(8,128)S(1)}, f32[64,256]{1,0:T(8,128)S(1)}, u32[]{:S(2)}, u32[]{:S(2)}) collective-permute-start(f32[64,256]{1,0:T(8,128)S(1)} %shard_map.71.refs_0_), channel_id=1, source_target_pairs={{0,4},{4,0},{8,12},{12,8},{16,20},{20,16},{24,28},{28,24},{1,5},{5... | collective-permute-start | bytes 196616 | tf_op jit(solution)/shard_map/ppermute | solution.py:85
  24.8 0.0 collective-permute-done.5
  24.8 2.7 %collective-permute-done.12.refs_1_ = f32[64,256]{1,0:T(8,128)S(1)} collective-permute-done((f32[64,256]{1,0:T(8,128)S(1)}, f32[64,256]{1,0:T(8,128)S(1)}, u32[]{:S(2)}, u32[]{:S(2)}) %collective-permute-start.12) | collective-permute-done | bytes 65568 | tf_op jit(solution)/shard_map/ppermute | solution.py:85
  27.6 0.1 shard_map.72
  27.7 1.6 %collective-permute-start.13 = (f32[64,128]{1,0:T(8,128)S(1)}, f32[64,128]{1,0:T(8,128)S(1)}, u32[]{:S(2)}, u32[]{:S(2)}) collective-permute-start(f32[64,128]{1,0:T(8,128)S(1)} %get-tuple-element.46), channel_id=1, source_target_pairs={{0,8},{4,12},{8,0},{12,4},{16,24},{20,28},{24,16},{28,20},{1,9},{5... | collective-permute-start | bytes 98312 | tf_op jit(solution)/shard_map/ppermute | solution.py:85
  29.4 0.1 collective-permute-start.7
  29.4 2.2 %collective-permute-done.13 = f32[64,128]{1,0:T(8,128)S(1)} collective-permute-done((f32[64,128]{1,0:T(8,128)S(1)}, f32[64,128]{1,0:T(8,128)S(1)}, u32[]{:S(2)}, u32[]{:S(2)}) %collective-permute-start.13) | collective-permute-done | bytes 32800 | tf_op jit(solution)/shard_map/ppermute | solution.py:85
  31.7 1.1 %collective-permute-start.14 = (f32[128,128]{1,0:T(8,128)S(1)}, f32[128,128]{1,0:T(8,128)S(1)}, u32[]{:S(2)}, u32[]{:S(2)}) collective-permute-start(f32[128,128]{1,0:T(8,128)S(1)} %pad_maximum_fusion.3), channel_id=1, source_target_pairs={{0,2},{1,3},{2,0},{3,1},{4,6},{5,7},{6,4},{7,5},{8,10},{9,11},{10,... | collective-permute-start | bytes 196616 | tf_op jit(solution)/shard_map/ppermute | solution.py:85
  32.8 3.2 %collective-permute-done.14 = f32[128,128]{1,0:T(8,128)S(1)} collective-permute-done((f32[128,128]{1,0:T(8,128)S(1)}, f32[128,128]{1,0:T(8,128)S(1)}, u32[]{:S(2)}, u32[]{:S(2)}) %collective-permute-start.14) | collective-permute-done | bytes 65568 | tf_op jit(solution)/shard_map/ppermute | solution.py:85
  36.0 0.1 collective-permute-start.15
  36.1 1.5 %shard_map.70 = (bf16[512,256]{1,0:T(8,128)(2,1)S(1)}, bf16[512,256]{1,0:T(8,128)(2,1)S(1)}) custom-call(bf16[128,384]{1,0:T(8,128)(2,1)S(1)} %get-tuple-element.30.refs_0_.refs_2_, bf16[128,384]{1,0:T(8,128)(2,1)S(1)} %get-tuple-element.31.refs_1_.refs_3_, bf16[128,256]{1,0:T(8,128)(2,1)S(1)} %get-tuple-element.32.refs_2_.refs_4_, ...), custom_call_target="tpu_custom_call" | custom-call | flops 402653184 | bytes 1441792 | tf_op jit(solution)/shard_map/pallas_call | solution.py:64
  37.6 0.0 collective-permute-done.7.other_ref
  37.6 1.5 %shard_map.68 = (f32[512,256]{1,0:T(8,128)S(1)}, bf16[128,256]{1,0:T(8,128)(2,1)S(1)}, bf16[128,256]{1,0:T(8,128)(2,1)S(1)}) custom-call(f32[4,128]{1,0:T(4,128)S(1)} %bitcast.4, f32[512,256]{1,0:T(8,128)S(1)} %copy-done.1, f32[640,128]{1,0:T(8,128)S(1)} %pad_maximum_fusion.own_ref, f32[640,128]{1,0:T(8,128)S(1)} %collective-permute-done.7.other_ref, ...), custom_call_target="tpu_custom_call" | custom-call | flops 301989888 | bytes 3082240 | tf_op jit(solution)/shard_map/pallas_call | solution.py:64
  39.2 0.0 collective-permute-done.15.refs_3_
  39.2 1.6 %shard_map.73 = f32[512,256]{1,0:T(8,128)} custom-call(f32[512,256]{1,0:T(8,128)S(1)} %get-tuple-element.38.base_ref, bf16[512,256]{1,0:T(8,128)(2,1)S(1)} %get-tuple-element.41.high_ref, bf16[512,256]{1,0:T(8,128)(2,1)S(1)} %get-tuple-element.42.low_ref, bf16[128,256]{1,0:T(8,128)(2,1)S(1)} %get-tuple-element.43.refs_0_, ...), custom_call_target="tpu_custom_call" | custom-call | flops 201326592 | bytes 1441792 | tf_op jit(solution)/shard_map/pallas_call | solution.py:64
  (28 shorter events, 0.4 us)
Async XLA Ops:
  0.0 2.8 %copy-start = (f32[3,512,128]{2,1,0:T(8,128)S(1)}, f32[3,512,128]{2,1,0:T(8,128)}, u32[]{:S(2)}) copy-start(f32[3,512,128]{2,1,0:T(8,128)} %level_ref.3) | copy-start | bytes 2359300
  0.0 2.8 %copy-start.2 = (f32[512,128]{1,0:T(8,128)S(1)}, f32[512,128]{1,0:T(8,128)}, u32[]{:S(2)}) copy-start(f32[512,128]{1,0:T(8,128)} %leaf_ref.3) | copy-start | bytes 786436
  0.0 2.8 %copy-start.3 = (f32[512]{0:T(512)S(1)}, f32[512]{0:T(512)}, u32[]{:S(2)}) copy-start(f32[512]{0:T(512)} %param.7) | copy-start | bytes 6148
  2.2 1.0 %copy-start.1 = (f32[512,256]{1,0:T(8,128)S(1)}, f32[512,256]{1,0:T(8,128)}, u32[]{:S(2)}) copy-start(f32[512,256]{1,0:T(8,128)} %queries_ref.5) | copy-start | bytes 1572868
  2.2 3.2 %collective-permute-start.1 = (f32[64,1024]{1,0:T(8,128)S(1)}, f32[64,1024]{1,0:T(8,128)S(1)}, u32[]{:S(2)}, u32[]{:S(2)}) collective-permute-start(f32[64,1024]{1,0:T(8,128)S(1)} %slice.86), channel_id=1, source_target_pairs={{0,1},{1,0},{2,3},{3,2},{4,5},{5,4},{6,7},{7,6},{8,9},{9,8},{10,11... | collective-permute-start | bytes 786440 | tf_op jit(solution)/shard_map/ppermute | solution.py:85
  4.0 4.6 %collective-permute-start = (f32[256,128]{1,0:T(8,128)S(1)}, f32[256,128]{1,0:T(8,128)S(1)}, u32[]{:S(2)}, u32[]{:S(2)}) collective-permute-start(f32[256,128]{1,0:T(8,128)S(1)} %slice.84), channel_id=1, source_target_pairs={{0,1},{1,0},{2,3},{3,2},{4,5},{5,4},{6,7},{7,6},{8,9},{9,8},{10,11... | collective-permute-start | bytes 393224 | tf_op jit(solution)/shard_map/ppermute | solution.py:85
  5.4 7.2 %collective-permute-start.4 = (f32[128,512]{1,0:T(8,128)S(1)}, f32[128,512]{1,0:T(8,128)S(1)}, u32[]{:S(2)}, u32[]{:S(2)}) collective-permute-start(f32[128,512]{1,0:T(8,128)S(1)} %slice.92), channel_id=1, source_target_pairs={{0,1},{1,0},{2,3},{3,2},{4,5},{5,4},{6,7},{7,6},{8,9},{9,8},{10,11... | collective-permute-start | bytes 786440 | tf_op jit(solution)/shard_map/ppermute | solution.py:85
  5.5 5.0 %collective-permute-start.2 = (f32[64,128]{1,0:T(8,128)S(1)}, f32[64,128]{1,0:T(8,128)S(1)}, u32[]{:S(2)}, u32[]{:S(2)}) collective-permute-start(f32[64,128]{1,0:T(8,128)S(1)} %slice.107), channel_id=1, source_target_pairs={{0,8},{4,12},{8,0},{12,4},{16,24},{20,28},{24,16},{28,20},{1,9},{5... | collective-permute-start | bytes 98312 | tf_op jit(solution)/shard_map/ppermute | solution.py:85
  8.7 8.3 %collective-permute-start.8 = (f32[64,768]{1,0:T(8,128)S(1)}, f32[64,768]{1,0:T(8,128)S(1)}, u32[]{:S(2)}, u32[]{:S(2)}) collective-permute-start(f32[64,768]{1,0:T(8,128)S(1)} %slice.120), channel_id=1, source_target_pairs={{0,2},{1,3},{2,0},{3,1},{4,6},{5,7},{6,4},{7,5},{8,10},{9,11},{10,... | collective-permute-start | bytes 589832 | tf_op jit(solution)/shard_map/ppermute | solution.py:85
  10.6 4.3 %collective-permute-start.3 = (f32[64,256]{1,0:T(8,128)S(1)}, f32[64,256]{1,0:T(8,128)S(1)}, u32[]{:S(2)}, u32[]{:S(2)}) collective-permute-start(f32[64,256]{1,0:T(8,128)S(1)} %pad_maximum_fusion.2), channel_id=1, source_target_pairs={{0,4},{4,0},{8,12},{12,8},{16,20},{20,16},{24,28},{28,24},{1,5},{5... | collective-permute-start | bytes 196616 | tf_op jit(solution)/shard_map/ppermute | solution.py:85
  12.6 6.7 %collective-permute-start.6 = (f32[64,512]{1,0:T(8,128)S(1)}, f32[64,512]{1,0:T(8,128)S(1)}, u32[]{:S(2)}, u32[]{:S(2)}) collective-permute-start(f32[64,512]{1,0:T(8,128)S(1)} %slice.114), channel_id=1, source_target_pairs={{0,2},{1,3},{2,0},{3,1},{4,6},{5,7},{6,4},{7,5},{8,10},{9,11},{10,... | collective-permute-start | bytes 393224 | tf_op jit(solution)/shard_map/ppermute | solution.py:85
  15.0 9.8 %collective-permute-start.5 = (f32[512,128]{1,0:T(8,128)S(1)}, f32[512,128]{1,0:T(8,128)S(1)}, u32[]{:S(2)}, u32[]{:S(2)}) collective-permute-start(f32[512,128]{1,0:T(8,128)S(1)} %get-tuple-element.53), channel_id=1, source_target_pairs={{0,2},{1,3},{2,0},{3,1},{4,6},{5,7},{6,4},{7,5},{8,10},{9,11},{10,... | collective-permute-start | bytes 786440 | tf_op jit(solution)/shard_map/ppermute | solution.py:85
  17.0 4.0 %collective-permute-start.10 = (f32[64,128]{1,0:T(8,128)S(1)}, f32[64,128]{1,0:T(8,128)S(1)}, u32[]{:S(2)}, u32[]{:S(2)}) collective-permute-start(f32[64,128]{1,0:T(8,128)S(1)} %slice.122), channel_id=1, source_target_pairs={{0,4},{4,0},{8,12},{12,8},{16,20},{20,16},{24,28},{28,24},{1,5},{5... | collective-permute-start | bytes 98312 | tf_op jit(solution)/shard_map/ppermute | solution.py:85
  19.4 3.1 %collective-permute-start.9 = (f32[64,640]{1,0:T(8,128)S(1)}, f32[64,640]{1,0:T(8,128)S(1)}, u32[]{:S(2)}, u32[]{:S(2)}) collective-permute-start(f32[64,640]{1,0:T(8,128)S(1)} %slice.121.own_ref), channel_id=1, source_target_pairs={{0,1},{1,0},{2,3},{3,2},{4,5},{5,4},{6,7},{7,6},{8,9},{9,8},{10,11... | collective-permute-start | bytes 491528 | tf_op jit(solution)/shard_map/ppermute | solution.py:85
  21.0 1.2 %collective-permute-start.11 = (f32[64,128]{1,0:T(8,128)S(1)}, f32[64,128]{1,0:T(8,128)S(1)}, u32[]{:S(2)}, u32[]{:S(2)}) collective-permute-start(f32[64,128]{1,0:T(8,128)S(1)} %slice_add_fusion.5.own_ref), channel_id=1, source_target_pairs={{0,1},{1,0},{2,3},{3,2},{4,5},{5,4},{6,7},{7,6},{8,9},{9,8},{10,11... | collective-permute-start | bytes 98312 | tf_op jit(solution)/shard_map/ppermute | solution.py:85
  23.2 4.3 %collective-permute-start.12 = (f32[64,256]{1,0:T(8,128)S(1)}, f32[64,256]{1,0:T(8,128)S(1)}, u32[]{:S(2)}, u32[]{:S(2)}) collective-permute-start(f32[64,256]{1,0:T(8,128)S(1)} %shard_map.71.refs_0_), channel_id=1, source_target_pairs={{0,4},{4,0},{8,12},{12,8},{16,20},{20,16},{24,28},{28,24},{1,5},{5... | collective-permute-start | bytes 196616 | tf_op jit(solution)/shard_map/ppermute | solution.py:85
  27.7 4.0 %collective-permute-start.13 = (f32[64,128]{1,0:T(8,128)S(1)}, f32[64,128]{1,0:T(8,128)S(1)}, u32[]{:S(2)}, u32[]{:S(2)}) collective-permute-start(f32[64,128]{1,0:T(8,128)S(1)} %get-tuple-element.46), channel_id=1, source_target_pairs={{0,8},{4,12},{8,0},{12,4},{16,24},{20,28},{24,16},{28,20},{1,9},{5... | collective-permute-start | bytes 98312 | tf_op jit(solution)/shard_map/ppermute | solution.py:85
  29.4 8.2 %collective-permute-start.7 = (f32[640,128]{1,0:T(8,128)S(1)}, f32[640,128]{1,0:T(8,128)S(1)}, u32[]{:S(2)}, u32[]{:S(2)}) collective-permute-start(f32[640,128]{1,0:T(8,128)S(1)} %pad_maximum_fusion.own_ref), channel_id=1, source_target_pairs={{0,1},{1,0},{2,3},{3,2},{4,5},{5,4},{6,7},{7,6},{8,9},{9,8},{10,11... | collective-permute-start | bytes 983048 | tf_op jit(solution)/shard_map/ppermute | solution.py:85
  31.7 4.3 %collective-permute-start.14 = (f32[128,128]{1,0:T(8,128)S(1)}, f32[128,128]{1,0:T(8,128)S(1)}, u32[]{:S(2)}, u32[]{:S(2)}) collective-permute-start(f32[128,128]{1,0:T(8,128)S(1)} %pad_maximum_fusion.3), channel_id=1, source_target_pairs={{0,2},{1,3},{2,0},{3,1},{4,6},{5,7},{6,4},{7,5},{8,10},{9,11},{10,... | collective-permute-start | bytes 196616 | tf_op jit(solution)/shard_map/ppermute | solution.py:85
  36.0 3.1 %collective-permute-start.15 = (f32[256,128]{1,0:T(8,128)S(1)}, f32[256,128]{1,0:T(8,128)S(1)}, u32[]{:S(2)}, u32[]{:S(2)}) collective-permute-start(f32[256,128]{1,0:T(8,128)S(1)} %pad_maximum_fusion.1.refs_2_), channel_id=1, source_target_pairs={{0,1},{1,0},{2,3},{3,2},{4,5},{5,4},{6,7},{7,6},{8,9},{9,8},{10,11... | collective-permute-start | bytes 393224 | tf_op jit(solution)/shard_map/ppermute | solution.py:85

commit v8 on v7

--- a/solution.py
+++ b/solution.py
@@ -43,14 +43,6 @@
 
 def core_side():
     return lax.rem(lax.axis_index("sub"), 2)
-
-
-def own_block():
-    place, value = lax.axis_index("sub"), 0
-    for _ in range(lax.axis_size("sub").bit_length() - 1):
-        value = value * 2 + lax.rem(place, 2)
-        place = place // 2
-    return value
 
 
 def at(index, size):
@@ -113,9 +105,8 @@
     ]
     blocks = [list(range(e + 1, count)) for e in range(count)]
     coarse = count - head
-    sub_bits = sub.bit_length() - 1
-    leaf_bits = range(1, sub_bits)
-    mine = columns // sub
+    leaf_bits = range(1, sub.bit_length() - 1)
+    mine = columns // 2
     half = rank // 2
     small = 2 * 3 * rank**3
 
@@ -186,9 +177,9 @@
         for basis_ref, part in zip(basis_refs, right):
             basis_ref[...] = part
         value = dot_parts(halves(queries_ref[...].T), right)
-        own = own_block()
-        for i in range(sub):
-            out_ref[at(i ^ own, mine), :] = value[i * mine : (i + 1) * mine]
+        side = core_side()
+        for h in range(2):
+            out_ref[at(h ^ side, mine), :] = value[h * mine : (h + 1) * mine]
 
     value, *basis = call(
         moment_body,
@@ -199,13 +190,8 @@
         level_basis,
         flops=small * count * 2 * rows_here // rank,
     )
-    size = columns
-    for bit in range(sub_bits):
-        size //= 2
-        sent, moment_parts = value[size:], [value[:size], swap(value[size:], "sub", bit)]
-        value = add_all(moment_parts)
-        if bit == 0:
-            moment_chip = value
+    moment_chip = value[:mine] + swap(value[mine:], "sub", 0)
+    moment_parts = partial_sums(moment_chip, "sub", leaf_bits)
 
     late_rows = columns // 2 + head * half
 
@@ -240,31 +226,11 @@
     late_chip = late[:late_rows] + swap(late[late_rows:], "sub", 0)
 
     def stacked(array, size):
-        return [
-            array[i : i + size, j : j + rank]
-            for i in range(0, array.shape[0], size)
-            for j in range(0, array.shape[1], rank)
-        ]
-
-    late_chip = [late_chip, *stacked(diagonal, half)]
-    if len(leaf_bits) == 1:
-        late = jnp.concatenate([*late_chip, *stacked(moment_parts[0][:, : head * rank], mine)], axis=0)
-        got = swap(late, "sub", leaf_bits[0])
-        late_size = late_rows + coarse * half
-        others = jnp.concatenate(stacked(sent[:, : head * rank], mine), axis=0)
-        late = jnp.concatenate(
-            [
-                late[:late_size] + got[:late_size],
-                *stacked(value[:, : head * rank], mine),
-                others + got[late_size:],
-            ],
-            axis=0,
-        )
-    else:
-        late = jnp.concatenate([*late_chip, *stacked(moment_chip[:, : head * rank], mine)], axis=0)
-        late_size = late_rows + coarse * half
-        late = add_all(partial_sums(late, "sub", leaf_bits))
-    late_parts = [late, swap(late, "sub", 0)]
+        return [array[:, j : j + size] for j in range(0, array.shape[1], size)]
+
+    late = jnp.concatenate([late_chip, *stacked(diagonal, rank)], axis=0)
+    late_size = late.shape[0]
+    late = add_all(partial_sums(late, "sub", leaf_bits))
 
     def product_body(group, own_ref, other_ref, core_ref, *refs):
         out_refs, stack_ref = refs[:-1], refs[-1]
@@ -306,20 +272,24 @@
         return [ref[:, start : start + size] for ref in factor]
 
     def head_body(*refs):
-        part_refs, factor_refs, rest_ref = refs[: len(moment_parts)], paired(refs[len(moment_parts) : -1]), refs[-1]
+        part_refs, factor_refs = refs[: len(moment_parts)], paired(refs[len(moment_parts) : -2])
+        own_ref, rest_ref = refs[-2:]
         rest = add_all([part[...] for part in part_refs])
         for e in range(head):
             own, rest = rest[:, :rank], rest[:, rank:]
+            own_ref[e * mine : (e + 1) * mine, :] = own
             rest = rest - dot_parts(halves(own), take(factor_refs[e], 0, rest.shape[1]))
         rest_ref[...] = rest
 
-    (rest,) = call(
+    head_moments, rest = call(
         head_body,
-        [(mine, coarse * rank)],
+        [(head * mine, rank), (mine, coarse * rank)],
         *moment_parts,
         *flat(factors[:head]),
         flops=small * sum(map(len, blocks[:head])),
     )
+    late = jnp.concatenate([late, head_moments], axis=0)
+    late_parts = [late, swap(late, "sub", 0)]
 
     def step_body(number, *refs):
         part_refs, factor, (own_ref, rest_ref) = refs[:number], refs[number:-2], refs[-2:]
@@ -329,13 +299,10 @@
         rest_ref[...] = rest - dot_parts(halves(own), take(factor, 0, rest.shape[1]))
 
     def scatter(parts, number, stack_ref):
-        own, slot = own_block(), 0
-        for part in parts:
-            for i in range(part.shape[0] // (number * mine)):
-                for e in range(number):
-                    start = (i * number + e) * mine
-                    stack_ref[at(slot ^ own, mine), e * rank : (e + 1) * rank] = part[start : start + mine, :]
-                slot += 1
+        side = core_side()
+        for part, place in zip(parts, (side, 1 - side)):
+            for e in range(number):
+                stack_ref[at(place, mine), e * rank : (e + 1) * rank] = part[e * mine : (e + 1) * mine, :]
 
     found = []
     for e in range(head, top):
@@ -351,8 +318,6 @@
     found.append(rest)
     found[-1] = add_all(partial_sums(rest, "rows", bits[top]))
     found = jnp.concatenate(found, axis=0)
-    for bit in reversed(leaf_bits):
-        found = jnp.concatenate([found, swap(found, "sub", bit)], axis=0)
     found_parts = [found, swap(found, "sub", 0)]
 
     def answer_body(*refs):
@@ -392,13 +357,7 @@
         products = [dot(core_ref[e].T, gram_ref[:, e * rank : (e + 1) * rank]) for e in range(count)]
         gains = [core_ref[e] + core_ref[e].T - dot(products[e], core_ref[e]) for e in range(1, count)]
         store(gain_refs, lanes(gains[head - 1 :]))
-        rest = stack_ref[:, : head * rank]
-        moments = []
-        for e in range(head):
-            own, rest = rest[:, :rank], rest[:, rank:]
-            moments.append(own)
-            if e + 1 < head:
-                rest = rest - dot_parts(halves(own), take(factor_refs[e], 0, rest.shape[1]))
+        moments = [stack_ref[:, e * rank : (e + 1) * rank] for e in range(head)]
         first = dot(moments[0], core_ref[0], 1)
         found = [dot(stack_ref[:, head * rank :], core_ref[0]) - dot(first, products[0], 1)]
         found += [dot(moments[e], gains[e - 1], 1) for e in range(1, head)]

time: 41 us -> 40.4 us (0.985)
  starting transfers between devices: 17.6 us -> 15.7 us
  waiting for transfers between devices: 12.6 us -> 14 us
    ppermute x16 -> x15, starting transfers between devices: 17.6 us -> 15.7 us  [swap(): lax.ppermute(array, axis, [(i, i ^ 1 << bit) for i in range(lax.axis_size...]
    ppermute x16 -> x15, waiting for transfers between devices: 12.6 us -> 14 us  [swap(): lax.ppermute(array, axis, [(i, i ^ 1 << bit) for i in range(lax.axis_size...]
  transfers between devices with their start and end apart: 16 -> 15, of which waited for: 8 -> 6; matrix products, arithmetic and copies ran while one was open for 1% -> 1% of each run, Pallas kernels for 13% -> 14%
where the time goes in v8:
time: 40.4 us; the launch traced here: 40.3 us
  starting transfers between devices  15.7 us (39%)
  waiting for transfers between devices  14 us (35%)
  Pallas kernels  9.49 us (23%)
  local copies, waits for them, and re-layouts  0.54 us (1%)
    ppermute x15, starting transfers between devices, swap(): lax.ppermute(array, axis, [(i, i ^ 1 << bit) for i in range(lax.axis_size...  15.7 us
    ppermute x15, waiting for transfers between devices, swap(): lax.ppermute(array, axis, [(i, i ^ 1 << bit) for i in range(lax.axis_size...  14 us
    pallas_call x10, Pallas kernels, call(): pl.pallas_call(body, out_shape=outs, in_specs=[pl.BlockSpec(memory_space=...  9.49 us
  transfers between devices with their start and end apart: 15, of which 6 were waited for; matrix products, arithmetic and copies ran while one was open for 1% of the time, Pallas kernels for 14%

profile of v8, /device:TPU:0, one launch (start us, length us, event | category | flops | bytes accessed | tf_op | source)
XLA Modules:
  0.0 40.3 jit_solution(8907645666540257820)
XLA Ops:
  0.0 0.0 copy-start
  0.0 0.0 copy-start.2
  0.0 0.0 copy-start.3
  0.0 2.2 %shard_map.65 = (f32[128,1024]{1,0:T(8,128)S(1)}, f32[4,128,128]{2,1,0:T(8,128)S(1)}) custom-call(f32[4,128]{1,0:T(4,128)} %bitcast.1, f32[512,128]{1,0:T(8,128)} %leaf_ref.3, f32[3,512,128]{2,1,0:T(8,128)} %level_ref.3, f32[1,128,128]{2,1,0:T(8,128)} %refs_3_.1, f32[14,128,128]{2,1,0:T(8,128)} %refs_4_.1), custom_call_target="tpu_custom_call" | custom-call | flops 402653184 | bytes 2033664 | tf_op jit(solution)/shard_map/pallas_call | solution.py:56
  2.2 0.0 copy-start.1
  2.2 0.6 %collective-permute-start.1 = (f32[64,1024]{1,0:T(8,128)S(1)}, f32[64,1024]{1,0:T(8,128)S(1)}, u32[]{:S(2)}, u32[]{:S(2)}) collective-permute-start(f32[64,1024]{1,0:T(8,128)S(1)} %slice.42), channel_id=1, source_target_pairs={{0,1},{1,0},{2,3},{3,2},{4,5},{5,4},{6,7},{7,6},{8,9},{9,8},{10,11... | collective-permute-start | bytes 786440 | tf_op jit(solution)/shard_map/ppermute | solution.py:77
  2.8 0.0 copy-done
  2.8 0.0 copy-done.2
  2.8 0.0 copy-done.3
  2.8 0.4 %copy-done.1 = f32[512,256]{1,0:T(8,128)S(1)} copy-done((f32[512,256]{1,0:T(8,128)S(1)}, f32[512,256]{1,0:T(8,128)}, u32[]{:S(2)}) %copy-start.1) | copy-done | bytes 524312
  3.2 0.7 %shard_map.64 = (f32[512,128]{1,0:T(8,128)S(1)}, bf16[512,128]{1,0:T(8,128)(2,1)S(1)}, bf16[512,128]{1,0:T(8,128)(2,1)S(1)}) custom-call(f32[4,128]{1,0:T(4,128)S(1)} %bitcast.2, f32[512,256]{1,0:T(8,128)S(1)} %copy-done.1, f32[512,128]{1,0:T(8,128)S(1)} %copy-done.2, f32[3,512,128]{2,1,0:T(8,128)S(1)} %copy-done), custom_call_target="tpu_custom_call" | custom-call | flops 201326592 | bytes 1574912 | tf_op jit(solution)/shard_map/pallas_call | solution.py:56
  4.0 0.6 %collective-permute-start = (f32[256,128]{1,0:T(8,128)S(1)}, f32[256,128]{1,0:T(8,128)S(1)}, u32[]{:S(2)}, u32[]{:S(2)}) collective-permute-start(f32[256,128]{1,0:T(8,128)S(1)} %slice.40), channel_id=1, source_target_pairs={{0,1},{1,0},{2,3},{3,2},{4,5},{5,4},{6,7},{7,6},{8,9},{9,8},{10,11... | collective-permute-start | bytes 393224 | tf_op jit(solution)/shard_map/ppermute | solution.py:77
  4.6 0.8 %shard_map.66 = (f32[256,512]{1,0:T(8,128)S(1)}, bf16[512,512]{1,0:T(8,128)(2,1)S(1)}, bf16[512,512]{1,0:T(8,128)(2,1)S(1)}) custom-call(f32[4,128]{1,0:T(4,128)S(1)} %bitcast.3, f32[512,256]{1,0:T(8,128)S(1)} %copy-done.1, f32[512,128]{1,0:T(8,128)S(1)} %copy-done.2, f32[3,512,128]{2,1,0:T(8,128)S(1)} %copy-done), custom_call_target="tpu_custom_call" | custom-call | flops 402653184 | bytes 1574912 | tf_op jit(solution)/shard_map/pallas_call | solution.py:56
  5.4 0.1 collective-permute-start.5
  5.5 0.0 collective-permute-done.1
  5.5 3.1 %collective-permute-start.2 = (f32[64,128]{1,0:T(8,128)S(1)}, f32[64,128]{1,0:T(8,128)S(1)}, u32[]{:S(2)}, u32[]{:S(2)}) collective-permute-start(f32[64,128]{1,0:T(8,128)S(1)} %slice.53), channel_id=1, source_target_pairs={{0,8},{4,12},{8,0},{12,4},{16,24},{20,28},{24,16},{28,20},{1,9},{5... | collective-permute-start | bytes 98312 | tf_op jit(solution)/shard_map/ppermute | solution.py:77
  8.7 0.0 collective-permute-done
  8.7 1.6 %collective-permute-start.7 = (f32[64,768]{1,0:T(8,128)S(1)}, f32[64,768]{1,0:T(8,128)S(1)}, u32[]{:S(2)}, u32[]{:S(2)}) collective-permute-start(f32[64,768]{1,0:T(8,128)S(1)} %slice.56), channel_id=1, source_target_pairs={{0,2},{1,3},{2,0},{3,1},{4,6},{5,7},{6,4},{7,5},{8,10},{9,11},{10,... | collective-permute-start | bytes 589832 | tf_op jit(solution)/shard_map/ppermute | solution.py:77
  10.3 0.3 collective-permute-done.2
  10.6 2.0 %collective-permute-start.3 = (f32[64,256]{1,0:T(8,128)S(1)}, f32[64,256]{1,0:T(8,128)S(1)}, u32[]{:S(2)}, u32[]{:S(2)}) collective-permute-start(f32[64,256]{1,0:T(8,128)S(1)} %pad_maximum_fusion.3), channel_id=1, source_target_pairs={{0,4},{4,0},{8,12},{12,8},{16,20},{20,16},{24,28},{28,24},{1,5},{5... | collective-permute-start | bytes 196616 | tf_op jit(solution)/shard_map/ppermute | solution.py:77
  12.6 0.0 collective-permute-done.5
  12.6 1.6 %collective-permute-start.6 = (f32[128,512]{1,0:T(8,128)S(1)}, f32[128,512]{1,0:T(8,128)S(1)}, u32[]{:S(2)}, u32[]{:S(2)}) collective-permute-start(f32[128,512]{1,0:T(8,128)S(1)} %slice_add_fusion.refs_0_), channel_id=1, source_target_pairs={{0,2},{1,3},{2,0},{3,1},{4,6},{5,7},{6,4},{7,5},{8,10},{9,11},{10,... | collective-permute-start | bytes 786440 | tf_op jit(solution)/shard_map/ppermute | solution.py:77
  14.2 0.7 %collective-permute-done.3 = f32[64,256]{1,0:T(8,128)S(1)} collective-permute-done((f32[64,256]{1,0:T(8,128)S(1)}, f32[64,256]{1,0:T(8,128)S(1)}, u32[]{:S(2)}, u32[]{:S(2)}) %collective-permute-start.3) | collective-permute-done | bytes 65568 | tf_op jit(solution)/shard_map/ppermute | solution.py:77
  15.0 2.0 %collective-permute-start.4 = (f32[384,128]{1,0:T(8,128)S(1)}, f32[384,128]{1,0:T(8,128)S(1)}, u32[]{:S(2)}, u32[]{:S(2)}) collective-permute-start(f32[384,128]{1,0:T(8,128)S(1)} %pad_maximum_fusion.1), channel_id=1, source_target_pairs={{0,2},{1,3},{2,0},{3,1},{4,6},{5,7},{6,4},{7,5},{8,10},{9,11},{10,... | collective-permute-start | bytes 589832 | tf_op jit(solution)/shard_map/ppermute | solution.py:77
  17.0 0.0 collective-permute-done.7
  17.0 1.6 %collective-permute-start.10 = (f32[64,128]{1,0:T(8,128)S(1)}, f32[64,128]{1,0:T(8,128)S(1)}, u32[]{:S(2)}, u32[]{:S(2)}) collective-permute-start(f32[64,128]{1,0:T(8,128)S(1)} %slice.58), channel_id=1, source_target_pairs={{0,4},{4,0},{8,12},{12,8},{16,20},{20,16},{24,28},{28,24},{1,5},{5... | collective-permute-start | bytes 98312 | tf_op jit(solution)/shard_map/ppermute | solution.py:77
  18.6 0.0 collective-permute-start.8
  18.6 6.5 %collective-permute-done.4 = f32[384,128]{1,0:T(8,128)S(1)} collective-permute-done((f32[384,128]{1,0:T(8,128)S(1)}, f32[384,128]{1,0:T(8,128)S(1)}, u32[]{:S(2)}, u32[]{:S(2)}) %collective-permute-start.4) | collective-permute-done | bytes 196640 | tf_op jit(solution)/shard_map/ppermute | solution.py:77
  25.2 0.0 collective-permute-done.8.other_ref
  25.2 0.4 shard_map.67
  25.6 0.0 collective-permute-done.6.refs_1_
  25.6 0.4 %shard_map.68 = (f32[256,128]{1,0:T(8,128)S(1)}, f32[128,256]{1,0:T(8,128)S(1)}) custom-call(f32[128,512]{1,0:T(8,128)S(1)} %slice_add_fusion.refs_0_, f32[128,512]{1,0:T(8,128)S(1)} %collective-permute-done.6.refs_1_, bf16[128,384]{1,0:T(8,128)(2,1)S(1)} %get-tuple-element.32.refs_2_.refs_0_, bf16[128,384]{1,0:T(8,128)(2,1)S(1)} %get-tuple-element.33.refs_3_.refs_1_, ...), custom_call_target="tpu_custom_call" | custom-call | flops 62914560 | bytes 851968 | tf_op jit(solution)/shard_map/pallas_call | solution.py:56
  26.0 1.6 %collective-permute-start.12 = (f32[128,256]{1,0:T(8,128)S(1)}, f32[128,256]{1,0:T(8,128)S(1)}, u32[]{:S(2)}, u32[]{:S(2)}) collective-permute-start(f32[128,256]{1,0:T(8,128)S(1)} %get-tuple-element.48.refs_0_), channel_id=1, source_target_pairs={{0,4},{4,0},{8,12},{12,8},{16,20},{20,16},{24,28},{28,24},{1,5},{5... | collective-permute-start | bytes 393224 | tf_op jit(solution)/shard_map/ppermute | solution.py:77
  27.6 0.1 collective-permute-start.9
  27.6 0.0 collective-permute-done.10
  27.7 0.5 %collective-permute-start.11 = (f32[64,128]{1,0:T(8,128)S(1)}, f32[64,128]{1,0:T(8,128)S(1)}, u32[]{:S(2)}, u32[]{:S(2)}) collective-permute-start(f32[64,128]{1,0:T(8,128)S(1)} %slice_add_fusion.3.own_ref), channel_id=1, source_target_pairs={{0,1},{1,0},{2,3},{3,2},{4,5},{5,4},{6,7},{7,6},{8,9},{9,8},{10,11... | collective-permute-start | bytes 98312 | tf_op jit(solution)/shard_map/ppermute | solution.py:77
  28.2 1.1 %collective-permute-done.11.other_ref = f32[64,128]{1,0:T(8,128)S(1)} collective-permute-done((f32[64,128]{1,0:T(8,128)S(1)}, f32[64,128]{1,0:T(8,128)S(1)}, u32[]{:S(2)}, u32[]{:S(2)}) %collective-permute-start.11) | collective-permute-done | bytes 32800 | tf_op jit(solution)/shard_map/ppermute | solution.py:77
  29.3 0.2 shard_map.70
  29.6 1.5 %collective-permute-done.12.refs_1_ = f32[128,256]{1,0:T(8,128)S(1)} collective-permute-done((f32[128,256]{1,0:T(8,128)S(1)}, f32[128,256]{1,0:T(8,128)S(1)}, u32[]{:S(2)}, u32[]{:S(2)}) %collective-permute-start.12) | collective-permute-done | bytes 131104 | tf_op jit(solution)/shard_map/ppermute | solution.py:77
  31.0 0.2 shard_map.72
  31.2 0.4 collective-permute-start.13
  31.6 4.0 %collective-permute-done.13 = f32[128,128]{1,0:T(8,128)S(1)} collective-permute-done((f32[128,128]{1,0:T(8,128)S(1)}, f32[128,128]{1,0:T(8,128)S(1)}, u32[]{:S(2)}, u32[]{:S(2)}) %collective-permute-start.13) | collective-permute-done | bytes 65568 | tf_op jit(solution)/shard_map/ppermute | solution.py:77
  35.6 0.1 collective-permute-start.14
  35.6 1.5 %shard_map.71 = (bf16[512,256]{1,0:T(8,128)(2,1)S(1)}, bf16[512,256]{1,0:T(8,128)(2,1)S(1)}) custom-call(bf16[128,384]{1,0:T(8,128)(2,1)S(1)} %get-tuple-element.32.refs_2_.refs_0_, bf16[128,384]{1,0:T(8,128)(2,1)S(1)} %get-tuple-element.33.refs_3_.refs_1_, bf16[128,256]{1,0:T(8,128)(2,1)S(1)} %get-tuple-element.34.refs_4_.refs_2_, ...), custom_call_target="tpu_custom_call" | custom-call | flops 402653184 | bytes 1441792 | tf_op jit(solution)/shard_map/pallas_call | solution.py:56
  37.1 0.0 collective-permute-done.9.other_ref
  37.1 1.5 %shard_map.69 = (f32[512,256]{1,0:T(8,128)S(1)}, bf16[128,256]{1,0:T(8,128)(2,1)S(1)}, bf16[128,256]{1,0:T(8,128)(2,1)S(1)}) custom-call(f32[4,128]{1,0:T(4,128)S(1)} %bitcast.4, f32[512,256]{1,0:T(8,128)S(1)} %copy-done.1, f32[640,128]{1,0:T(8,128)S(1)} %pad_maximum_fusion.own_ref, f32[640,128]{1,0:T(8,128)S(1)} %collective-permute-done.9.other_ref, ...), custom_call_target="tpu_custom_call" | custom-call | flops 301989888 | bytes 3082240 | tf_op jit(solution)/shard_map/pallas_call | solution.py:56
  38.6 0.0 collective-permute-done.14.refs_3_
  38.6 1.6 %shard_map.73 = f32[512,256]{1,0:T(8,128)} custom-call(f32[512,256]{1,0:T(8,128)S(1)} %get-tuple-element.41.base_ref, bf16[512,256]{1,0:T(8,128)(2,1)S(1)} %get-tuple-element.44.high_ref, bf16[512,256]{1,0:T(8,128)(2,1)S(1)} %get-tuple-element.45.low_ref, bf16[128,256]{1,0:T(8,128)(2,1)S(1)} %get-tuple-element.46.refs_0_, ...), custom_call_target="tpu_custom_call" | custom-call | flops 201326592 | bytes 1441792 | tf_op jit(solution)/shard_map/pallas_call | solution.py:56
  (21 shorter events, 0.3 us)
Async XLA Ops:
  0.0 2.8 %copy-start = (f32[3,512,128]{2,1,0:T(8,128)S(1)}, f32[3,512,128]{2,1,0:T(8,128)}, u32[]{:S(2)}) copy-start(f32[3,512,128]{2,1,0:T(8,128)} %level_ref.3) | copy-start | bytes 2359300
  0.0 2.8 %copy-start.2 = (f32[512,128]{1,0:T(8,128)S(1)}, f32[512,128]{1,0:T(8,128)}, u32[]{:S(2)}) copy-start(f32[512,128]{1,0:T(8,128)} %leaf_ref.3) | copy-start | bytes 786436
  0.0 2.8 %copy-start.3 = (f32[512]{0:T(512)S(1)}, f32[512]{0:T(512)}, u32[]{:S(2)}) copy-start(f32[512]{0:T(512)} %param.7) | copy-start | bytes 6148
  2.2 1.0 %copy-start.1 = (f32[512,256]{1,0:T(8,128)S(1)}, f32[512,256]{1,0:T(8,128)}, u32[]{:S(2)}) copy-start(f32[512,256]{1,0:T(8,128)} %queries_ref.5) | copy-start | bytes 1572868
  2.2 3.2 %collective-permute-start.1 = (f32[64,1024]{1,0:T(8,128)S(1)}, f32[64,1024]{1,0:T(8,128)S(1)}, u32[]{:S(2)}, u32[]{:S(2)}) collective-permute-start(f32[64,1024]{1,0:T(8,128)S(1)} %slice.42), channel_id=1, source_target_pairs={{0,1},{1,0},{2,3},{3,2},{4,5},{5,4},{6,7},{7,6},{8,9},{9,8},{10,11... | collective-permute-start | bytes 786440 | tf_op jit(solution)/shard_map/ppermute | solution.py:77
  4.0 4.6 %collective-permute-start = (f32[256,128]{1,0:T(8,128)S(1)}, f32[256,128]{1,0:T(8,128)S(1)}, u32[]{:S(2)}, u32[]{:S(2)}) collective-permute-start(f32[256,128]{1,0:T(8,128)S(1)} %slice.40), channel_id=1, source_target_pairs={{0,1},{1,0},{2,3},{3,2},{4,5},{5,4},{6,7},{7,6},{8,9},{9,8},{10,11... | collective-permute-start | bytes 393224 | tf_op jit(solution)/shard_map/ppermute | solution.py:77
  5.4 7.2 %collective-permute-start.5 = (f32[128,512]{1,0:T(8,128)S(1)}, f32[128,512]{1,0:T(8,128)S(1)}, u32[]{:S(2)}, u32[]{:S(2)}) collective-permute-start(f32[128,512]{1,0:T(8,128)S(1)} %slice.48), channel_id=1, source_target_pairs={{0,1},{1,0},{2,3},{3,2},{4,5},{5,4},{6,7},{7,6},{8,9},{9,8},{10,11... | collective-permute-start | bytes 786440 | tf_op jit(solution)/shard_map/ppermute | solution.py:77
  5.5 5.0 %collective-permute-start.2 = (f32[64,128]{1,0:T(8,128)S(1)}, f32[64,128]{1,0:T(8,128)S(1)}, u32[]{:S(2)}, u32[]{:S(2)}) collective-permute-start(f32[64,128]{1,0:T(8,128)S(1)} %slice.53), channel_id=1, source_target_pairs={{0,8},{4,12},{8,0},{12,4},{16,24},{20,28},{24,16},{28,20},{1,9},{5... | collective-permute-start | bytes 98312 | tf_op jit(solution)/shard_map/ppermute | solution.py:77
  8.7 8.3 %collective-permute-start.7 = (f32[64,768]{1,0:T(8,128)S(1)}, f32[64,768]{1,0:T(8,128)S(1)}, u32[]{:S(2)}, u32[]{:S(2)}) collective-permute-start(f32[64,768]{1,0:T(8,128)S(1)} %slice.56), channel_id=1, source_target_pairs={{0,2},{1,3},{2,0},{3,1},{4,6},{5,7},{6,4},{7,5},{8,10},{9,11},{10,... | collective-permute-start | bytes 589832 | tf_op jit(solution)/shard_map/ppermute | solution.py:77
  10.6 4.3 %collective-permute-start.3 = (f32[64,256]{1,0:T(8,128)S(1)}, f32[64,256]{1,0:T(8,128)S(1)}, u32[]{:S(2)}, u32[]{:S(2)}) collective-permute-start(f32[64,256]{1,0:T(8,128)S(1)} %pad_maximum_fusion.3), channel_id=1, source_target_pairs={{0,4},{4,0},{8,12},{12,8},{16,20},{20,16},{24,28},{28,24},{1,5},{5... | collective-permute-start | bytes 196616 | tf_op jit(solution)/shard_map/ppermute | solution.py:77
  12.6 12.9 %collective-permute-start.6 = (f32[128,512]{1,0:T(8,128)S(1)}, f32[128,512]{1,0:T(8,128)S(1)}, u32[]{:S(2)}, u32[]{:S(2)}) collective-permute-start(f32[128,512]{1,0:T(8,128)S(1)} %slice_add_fusion.refs_0_), channel_id=1, source_target_pairs={{0,2},{1,3},{2,0},{3,1},{4,6},{5,7},{6,4},{7,5},{8,10},{9,11},{10,... | collective-permute-start | bytes 786440 | tf_op jit(solution)/shard_map/ppermute | solution.py:77
  15.0 10.2 %collective-permute-start.4 = (f32[384,128]{1,0:T(8,128)S(1)}, f32[384,128]{1,0:T(8,128)S(1)}, u32[]{:S(2)}, u32[]{:S(2)}) collective-permute-start(f32[384,128]{1,0:T(8,128)S(1)} %pad_maximum_fusion.1), channel_id=1, source_target_pairs={{0,2},{1,3},{2,0},{3,1},{4,6},{5,7},{6,4},{7,5},{8,10},{9,11},{10,... | collective-permute-start | bytes 589832 | tf_op jit(solution)/shard_map/ppermute | solution.py:77
  17.0 10.6 %collective-permute-start.10 = (f32[64,128]{1,0:T(8,128)S(1)}, f32[64,128]{1,0:T(8,128)S(1)}, u32[]{:S(2)}, u32[]{:S(2)}) collective-permute-start(f32[64,128]{1,0:T(8,128)S(1)} %slice.58), channel_id=1, source_target_pairs={{0,4},{4,0},{8,12},{12,8},{16,20},{20,16},{24,28},{28,24},{1,5},{5... | collective-permute-start | bytes 98312 | tf_op jit(solution)/shard_map/ppermute | solution.py:77
  18.6 6.6 %collective-permute-start.8 = (f32[64,640]{1,0:T(8,128)S(1)}, f32[64,640]{1,0:T(8,128)S(1)}, u32[]{:S(2)}, u32[]{:S(2)}) collective-permute-start(f32[64,640]{1,0:T(8,128)S(1)} %slice.57.own_ref), channel_id=1, source_target_pairs={{0,1},{1,0},{2,3},{3,2},{4,5},{5,4},{6,7},{7,6},{8,9},{9,8},{10,11... | collective-permute-start | bytes 491528 | tf_op jit(solution)/shard_map/ppermute | solution.py:77
  26.0 5.0 %collective-permute-start.12 = (f32[128,256]{1,0:T(8,128)S(1)}, f32[128,256]{1,0:T(8,128)S(1)}, u32[]{:S(2)}, u32[]{:S(2)}) collective-permute-start(f32[128,256]{1,0:T(8,128)S(1)} %get-tuple-element.48.refs_0_), channel_id=1, source_target_pairs={{0,4},{4,0},{8,12},{12,8},{16,20},{20,16},{24,28},{28,24},{1,5},{5... | collective-permute-start | bytes 393224 | tf_op jit(solution)/shard_map/ppermute | solution.py:77
  27.6 9.6 %collective-permute-start.9 = (f32[640,128]{1,0:T(8,128)S(1)}, f32[640,128]{1,0:T(8,128)S(1)}, u32[]{:S(2)}, u32[]{:S(2)}) collective-permute-start(f32[640,128]{1,0:T(8,128)S(1)} %pad_maximum_fusion.own_ref), channel_id=1, source_target_pairs={{0,1},{1,0},{2,3},{3,2},{4,5},{5,4},{6,7},{7,6},{8,9},{9,8},{10,11... | collective-permute-start | bytes 983048 | tf_op jit(solution)/shard_map/ppermute | solution.py:77
  27.7 1.6 %collective-permute-start.11 = (f32[64,128]{1,0:T(8,128)S(1)}, f32[64,128]{1,0:T(8,128)S(1)}, u32[]{:S(2)}, u32[]{:S(2)}) collective-permute-start(f32[64,128]{1,0:T(8,128)S(1)} %slice_add_fusion.3.own_ref), channel_id=1, source_target_pairs={{0,1},{1,0},{2,3},{3,2},{4,5},{5,4},{6,7},{7,6},{8,9},{9,8},{10,11... | collective-permute-start | bytes 98312 | tf_op jit(solution)/shard_map/ppermute | solution.py:77
  31.2 4.3 %collective-permute-start.13 = (f32[128,128]{1,0:T(8,128)S(1)}, f32[128,128]{1,0:T(8,128)S(1)}, u32[]{:S(2)}, u32[]{:S(2)}) collective-permute-start(f32[128,128]{1,0:T(8,128)S(1)} %get-tuple-element.50), channel_id=1, source_target_pairs={{0,8},{4,12},{8,0},{12,4},{16,24},{20,28},{24,16},{28,20},{1,9},{5... | collective-permute-start | bytes 196616 | tf_op jit(solution)/shard_map/ppermute | solution.py:77
  35.6 3.1 %collective-permute-start.14 = (f32[256,128]{1,0:T(8,128)S(1)}, f32[256,128]{1,0:T(8,128)S(1)}, u32[]{:S(2)}, u32[]{:S(2)}) collective-permute-start(f32[256,128]{1,0:T(8,128)S(1)} %pad_maximum_fusion.2.refs_2_), channel_id=1, source_target_pairs={{0,1},{1,0},{2,3},{3,2},{4,5},{5,4},{6,7},{7,6},{8,9},{9,8},{10,11... | collective-permute-start | bytes 393224 | tf_op jit(solution)/shard_map/ppermute | solution.py:77
